TPU v7x, 32 devices: a whole 2x2x4 slice. The times are simulated.
32 devices in a mesh: dev: 32 (over z, y, x, core).
Axes of the slice: x: 2, y: 2, z: 4, core: 2. Of those that a mesh axis runs over, the one named last changes fastest.
Arguments:
- tokens: bfloat16 [32768, 768], P('dev'), may hold values from -6 to 6
- seq_ids: int32 [32768], P('dev'), may hold values from 0 to 64, as said below
- cotangent: bfloat16 [32768, 768], P('dev'), may hold values from -6 to 6
- attn_gain: bfloat16 [768], P('dev'), may hold values from 0.25 to 1.75
- attn_shift: bfloat16 [768], P('dev'), may hold values from -3 to 3
- mlp_gain: bfloat16 [768], P('dev'), may hold values from 0.25 to 1.75
- mlp_shift: bfloat16 [768], P('dev'), may hold values from -3 to 3
- qkv_weight: bfloat16 [768, 2304], P('dev'), may hold values from -0.3125 to 0.3125
- qkv_bias: bfloat16 [2304], P('dev'), may hold values from -3 to 3
- out_weight: bfloat16 [768, 768], P('dev'), may hold values from -2.5 to 2.5
- out_bias: bfloat16 [768], P('dev'), may hold values from -3 to 3
- up_weight: bfloat16 [768, 3072], P('dev'), may hold values from -0.21875 to 0.21875
- up_bias: bfloat16 [3072], P('dev'), may hold values from -4 to 4
- down_weight: bfloat16 [3072, 768], P('dev'), may hold values from -0.109375 to 0.109375
- down_bias: bfloat16 [768], P('dev'), may hold values from -3 to 3
Outputs:
- block_out: bfloat16 [32768, 768], P('dev')
- grad_tokens: float32 [32768, 768], P('dev')
- grad_attn_gain: float32 [768], P('dev')
- grad_attn_shift: float32 [768], P('dev')
- grad_mlp_gain: float32 [768], P('dev')
- grad_mlp_shift: float32 [768], P('dev')
- grad_qkv_weight: float32 [768, 2304], P('dev')
- grad_qkv_bias: float32 [2304], P('dev')
- grad_out_weight: float32 [768, 768], P('dev')
- grad_out_bias: float32 [768], P('dev')
- grad_up_weight: float32 [768, 3072], P('dev')
- grad_up_bias: float32 [3072], P('dev')
- grad_down_weight: float32 [3072, 768], P('dev')
- grad_down_bias: float32 [768], P('dev')
Inputs may be any that keep to these rules, and one draw needn't show every extreme that they name: seq_ids starts at 0 and rises by one at the first token of each new sequence; a sequence holds at most 1024 tokens and one holds exactly 1024; apart from token 0, the tokens of each device hold exactly two first tokens of sequences, never the device's first token, so every boundary between two devices' tokens lies inside a sequence; the later of a device's two first tokens lies at index 512 or later within the device, and on some device exactly there, so at most 512 tokens of a device continue on the next device.
All inputs are finite; a program needn't handle non-finite values.
Results may differ from a plain program's by a relative error of at most 0.012.
The roundings to bfloat16 on the way count: a program that leaves them out, or rounds other values in their place, can miss the bound.
Values may be sent and summed in bfloat16 or wider, within the bound.
No kernel may reach another device: no remote copies, remote signals or barrier semaphores. Data moves between devices by JAX's collectives and lax.ppermute only.
A program may use at most 192 MiB of HBM per device.

v0:
```python
import jax
import jax.numpy as jnp
from jax import lax
from jax.sharding import PartitionSpec as P

HDIM = 64
ROT = 16


EPSILON = 1e-05
MASKED = -1e30


def from_behind(value, axis, steps):
    count = lax.axis_size(axis)
    leading, last = (max(0, -steps), min(count, count - steps))
    return lax.ppermute(value, axis, [(source, source + steps) for source in range(leading, last)])


def layer_norm(values, norm_gain, norm_shift):
    center = values - jnp.mean(values, axis=-1, keepdims=True)
    spread = jnp.mean(center * center, axis=-1, keepdims=True)
    return center * lax.rsqrt(spread + EPSILON) * norm_gain + norm_shift


def angles_of(positions):
    frequency = 10000.0 ** (-2.0 * jnp.arange(ROT // 2, dtype=jnp.float32) / ROT)
    return positions.astype(jnp.float32)[:, None] * frequency[None, :]


def rotate(moving, angles):
    half_dims = angles.shape[-1]
    cosine = jnp.cos(angles)[:, None, :]
    sine_part = jnp.sin(angles)[:, None, :]
    first_half = moving[..., :half_dims]
    second_half = moving[..., half_dims : 2 * half_dims]
    return jnp.concatenate(
        [
            first_half * cosine - second_half * sine_part,
            second_half * cosine + first_half * sine_part,
            moving[..., 2 * half_dims :],
        ],
        axis=-1,
    )


def gelu_exact(values):
    return jax.nn.gelu(values, approximate=False)


def by_rows(stacked):
    return jnp.transpose(stacked, (1, 0, 2)).reshape(stacked.shape[1], -1)


def local(
    tokens,
    seq_ids,
    cotangent,
    attn_gain,
    attn_shift,
    mlp_gain,
    mlp_shift,
    qkv_weight,
    qkv_bias,
    out_weight,
    out_bias,
    up_weight,
    up_bias,
    down_weight,
    down_bias,
):
    gathered = (
        lax.all_gather(attn_gain, "dev", axis=0, tiled=True),
        lax.all_gather(attn_shift, "dev", axis=0, tiled=True),
        lax.all_gather(mlp_gain, "dev", axis=0, tiled=True),
        lax.all_gather(mlp_shift, "dev", axis=0, tiled=True),
        lax.all_gather(qkv_weight, "dev", axis=0, tiled=True),
        lax.all_gather(qkv_bias, "dev", axis=0, tiled=True),
        lax.all_gather(out_weight, "dev", axis=0, tiled=True),
        lax.all_gather(out_bias, "dev", axis=0, tiled=True),
        lax.all_gather(up_weight, "dev", axis=0, tiled=True),
        lax.all_gather(up_bias, "dev", axis=0, tiled=True),
        lax.all_gather(down_weight, "dev", axis=0, tiled=True),
        lax.all_gather(down_bias, "dev", axis=0, tiled=True),
    )
    gain_a, shift_a, gain_m, shift_m, w_qkv, b_qkv, w_out, b_out, w_up, b_up, w_down, b_down = (
        gathered
    )
    row_count = tokens.shape[0]
    model_width = tokens.shape[1]
    head_count = model_width // HDIM
    pair_count = head_count // 2
    pair_width = 2 * HDIM
    query_rows = min(512, row_count)
    score_scale = HDIM ** (-0.5)
    key_count = row_count + row_count
    row_index = jnp.arange(row_count, dtype=jnp.int32)
    prior_index = jnp.arange(row_count, dtype=jnp.int32)
    last_id = seq_ids[row_count - 1]
    trailing = jnp.sum((seq_ids == last_id).astype(jnp.int32))
    before = from_behind(jnp.stack([last_id, trailing]), "dev", 1)
    carry = jnp.where(before[0] == seq_ids[0], before[1], 0)
    opening = jnp.concatenate([jnp.ones((1,), jnp.bool_), seq_ids[1:] != seq_ids[:-1]])
    seq_start = lax.cummax(jnp.where(opening, row_index, 0), axis=0)
    leading = seq_ids == seq_ids[0]
    positions = row_index - seq_start + jnp.where(leading, carry, 0)
    angles = angles_of(positions)

    def allowed_rows(offset):
        query_ids = seq_ids[offset : offset + query_rows]
        query_pos = row_index[offset : offset + query_rows]
        local_ok = (row_index[None, :] <= query_pos[:, None]) & (
            seq_ids[None, :] == query_ids[:, None]
        )
        prior_ok = leading[offset : offset + query_rows, None] & (
            prior_index[None, :] >= row_count - carry
        )
        return jnp.concatenate([prior_ok, local_ok], axis=1)

    def pair_slice(matrix, pair_index):
        return lax.dynamic_slice_in_dim(matrix, pair_index * pair_width, pair_width, 1).reshape(
            matrix.shape[0], 2, HDIM
        )

    residual = tokens.astype(jnp.float32)
    attn_in = layer_norm(residual, gain_a.astype(jnp.float32), shift_a.astype(jnp.float32)).astype(
        jnp.bfloat16
    )
    mixed = jnp.dot(attn_in, w_qkv, preferred_element_type=jnp.float32) + b_qkv.astype(jnp.float32)
    mixed = mixed.reshape(row_count, 3, head_count, HDIM)
    query = rotate(mixed[:, 0], angles).astype(jnp.bfloat16).reshape(row_count, model_width)
    own_keys = rotate(mixed[:, 1], angles).astype(jnp.bfloat16).reshape(row_count, model_width)
    own_values = mixed[:, 2].astype(jnp.bfloat16).reshape(row_count, model_width)
    prior_keys, prior_values = from_behind((own_keys, own_values), "dev", 1)
    all_keys = jnp.concatenate([prior_keys, own_keys], axis=0)
    all_values = jnp.concatenate([prior_values, own_values], axis=0)

    def pair_forward(pair_index):
        query_pair = pair_slice(query, pair_index)
        key_pair = pair_slice(all_keys, pair_index)
        value_pair = pair_slice(all_values, pair_index)
        outputs = []
        totals = []
        for offset in range(0, row_count, query_rows):
            scores = (
                jnp.einsum(
                    "qhd,khd->hqk",
                    query_pair[offset : offset + query_rows],
                    key_pair,
                    preferred_element_type=jnp.float32,
                )
                * score_scale
            )
            scores = jnp.where(allowed_rows(offset)[None], scores, MASKED)
            highest = jnp.max(scores, axis=-1, keepdims=True)
            exponent = jnp.exp(scores - highest)
            normal = jnp.sum(exponent, axis=-1, keepdims=True)
            attn_probs = (exponent / normal).astype(jnp.bfloat16)
            outputs.append(
                jnp.einsum(
                    "hqk,khd->qhd", attn_probs, value_pair, preferred_element_type=jnp.float32
                )
            )
            totals.append(highest[..., 0] + jnp.log(normal[..., 0]))
        return (
            jnp.concatenate(outputs, axis=0).reshape(row_count, pair_width),
            jnp.concatenate(totals, axis=1),
        )

    context_pairs, log_totals = lax.map(pair_forward, jnp.arange(pair_count))
    context = by_rows(context_pairs).astype(jnp.bfloat16)
    attn_out = jnp.dot(context, w_out, preferred_element_type=jnp.float32) + b_out.astype(
        jnp.float32
    )
    mlp_in = layer_norm(residual, gain_m.astype(jnp.float32), shift_m.astype(jnp.float32)).astype(
        jnp.bfloat16
    )
    ffn_parts = []
    for offset in range(0, row_count, query_rows):
        hidden = jnp.dot(
            mlp_in[offset : offset + query_rows], w_up, preferred_element_type=jnp.float32
        ) + b_up.astype(jnp.float32)
        active = gelu_exact(hidden).astype(jnp.bfloat16)
        ffn_parts.append(jnp.dot(active, w_down, preferred_element_type=jnp.float32))
    ffn_out = jnp.concatenate(ffn_parts, axis=0) + b_down.astype(jnp.float32)
    block_out = (residual + attn_out + ffn_out).astype(jnp.bfloat16)
    params = (
        lax.all_gather(attn_gain, "dev", axis=0, tiled=True),
        lax.all_gather(attn_shift, "dev", axis=0, tiled=True),
        lax.all_gather(mlp_gain, "dev", axis=0, tiled=True),
        lax.all_gather(mlp_shift, "dev", axis=0, tiled=True),
        lax.all_gather(qkv_weight, "dev", axis=0, tiled=True),
        lax.all_gather(qkv_bias, "dev", axis=0, tiled=True),
        lax.all_gather(out_weight, "dev", axis=0, tiled=True),
        lax.all_gather(out_bias, "dev", axis=0, tiled=True),
        lax.all_gather(up_weight, "dev", axis=0, tiled=True),
        lax.all_gather(up_bias, "dev", axis=0, tiled=True),
        lax.all_gather(down_weight, "dev", axis=0, tiled=True),
        lax.all_gather(down_bias, "dev", axis=0, tiled=True),
    )
    gain_a, shift_a, gain_m, shift_m, w_qkv, b_qkv, w_out, b_out, w_up, b_up, w_down, b_down = (
        params
    )
    upstream = cotangent.astype(jnp.float32)
    grad_bias_out = jnp.sum(upstream, axis=0)
    grad_w_out = jnp.einsum("td,te->de", context, cotangent, preferred_element_type=jnp.float32)
    ff_width = w_up.shape[1]
    grad_w_down = jnp.zeros((ff_width, model_width), jnp.float32)
    grad_w_up = jnp.zeros((model_width, ff_width), jnp.float32)
    grad_bias_up = jnp.zeros((ff_width,), jnp.float32)
    d_mlp_parts = []
    for offset in range(0, row_count, query_rows):
        rows_in = mlp_in[offset : offset + query_rows]
        upstream_part = cotangent[offset : offset + query_rows]
        hidden = jnp.dot(rows_in, w_up, preferred_element_type=jnp.float32) + b_up.astype(
            jnp.float32
        )
        active = gelu_exact(hidden).astype(jnp.bfloat16)
        grad_w_down = grad_w_down + jnp.einsum(
            "tf,td->fd", active, upstream_part, preferred_element_type=jnp.float32
        )
        d_active = jnp.einsum(
            "td,fd->tf", upstream_part, w_down, preferred_element_type=jnp.float32
        )
        _, gelu_pull = jax.vjp(gelu_exact, hidden)
        d_hidden = gelu_pull(d_active)[0].astype(jnp.bfloat16)
        grad_bias_up = grad_bias_up + jnp.sum(d_hidden.astype(jnp.float32), axis=0)
        grad_w_up = grad_w_up + jnp.einsum(
            "td,tf->df", rows_in, d_hidden, preferred_element_type=jnp.float32
        )
        d_mlp_parts.append(
            jnp.einsum("tf,df->td", d_hidden, w_up, preferred_element_type=jnp.float32)
        )
    d_mlp_in = jnp.concatenate(d_mlp_parts, axis=0)
    _, norm_pull_m = jax.vjp(
        layer_norm, residual, gain_m.astype(jnp.float32), shift_m.astype(jnp.float32)
    )
    d_mlp_tokens, grad_gain_m, grad_shift_m = norm_pull_m(d_mlp_in)
    d_context = jnp.einsum(
        "te,de->td", cotangent, w_out, preferred_element_type=jnp.float32
    ).astype(jnp.bfloat16)

    def pair_backward(pair_index):
        query_pair = pair_slice(query, pair_index)
        key_pair = pair_slice(all_keys, pair_index)
        value_pair = pair_slice(all_values, pair_index)
        d_pair = pair_slice(d_context, pair_index)
        total_pair = log_totals[pair_index]
        d_keys = jnp.zeros((key_count, 2, HDIM), jnp.float32)
        d_values = jnp.zeros((key_count, 2, HDIM), jnp.float32)
        d_query_parts = []
        for offset in range(0, row_count, query_rows):
            query_block = query_pair[offset : offset + query_rows]
            d_block = d_pair[offset : offset + query_rows]
            scores = (
                jnp.einsum(
                    "qhd,khd->hqk", query_block, key_pair, preferred_element_type=jnp.float32
                )
                * score_scale
            )
            scores = jnp.where(allowed_rows(offset)[None], scores, MASKED)
            prob_full = jnp.exp(scores - total_pair[:, offset : offset + query_rows, None])
            d_values = d_values + jnp.einsum(
                "hqk,qhd->khd",
                prob_full.astype(jnp.bfloat16),
                d_block,
                preferred_element_type=jnp.float32,
            )
            d_probs = jnp.einsum(
                "qhd,khd->hqk", d_block, value_pair, preferred_element_type=jnp.float32
            )
            inner = jnp.sum(prob_full * d_probs, axis=-1, keepdims=True)
            d_scores = (prob_full * (d_probs - inner)).astype(jnp.bfloat16)
            d_query_parts.append(
                jnp.einsum("hqk,khd->qhd", d_scores, key_pair, preferred_element_type=jnp.float32)
                * score_scale
            )
            d_keys = (
                d_keys
                + jnp.einsum(
                    "hqk,qhd->khd", d_scores, query_block, preferred_element_type=jnp.float32
                )
                * score_scale
            )
        return (
            jnp.concatenate(d_query_parts, axis=0).reshape(row_count, pair_width),
            d_keys.reshape(key_count, pair_width),
            d_values.reshape(key_count, pair_width),
        )

    d_query_pairs, d_key_pairs, d_value_pairs = lax.map(pair_backward, jnp.arange(pair_count))
    d_query_all = by_rows(d_query_pairs)
    d_keys_all = by_rows(d_key_pairs)
    d_values_all = by_rows(d_value_pairs)
    later_keys, later_values = from_behind(
        (d_keys_all[:row_count], d_values_all[:row_count]), "dev", -1
    )
    front_zeros = jnp.zeros((row_count - row_count, model_width), jnp.float32)
    d_own_keys = d_keys_all[row_count:] + jnp.concatenate([front_zeros, later_keys], axis=0)
    d_own_values = d_values_all[row_count:] + jnp.concatenate([front_zeros, later_values], axis=0)
    _, rotate_pull = jax.vjp(lambda moving: rotate(moving, angles), mixed[:, 0])
    d_query_pre = rotate_pull(d_query_all.reshape(row_count, head_count, HDIM))[0]
    d_key_pre = rotate_pull(d_own_keys.reshape(row_count, head_count, HDIM))[0]
    d_mixed = (
        jnp.stack(
            [d_query_pre, d_key_pre, d_own_values.reshape(row_count, head_count, HDIM)], axis=1
        )
        .reshape(row_count, 3 * model_width)
        .astype(jnp.bfloat16)
    )
    grad_bias_qkv = jnp.sum(d_mixed.astype(jnp.float32), axis=0)
    grad_w_qkv = jnp.einsum("td,te->de", attn_in, d_mixed, preferred_element_type=jnp.float32)
    d_attn_in = jnp.einsum("te,de->td", d_mixed, w_qkv, preferred_element_type=jnp.float32)
    _, norm_pull_a = jax.vjp(
        layer_norm, residual, gain_a.astype(jnp.float32), shift_a.astype(jnp.float32)
    )
    d_attn_tokens, grad_gain_a, grad_shift_a = norm_pull_a(d_attn_in)
    grad_tokens = upstream + d_attn_tokens + d_mlp_tokens
    shards = (
        lax.psum_scatter(grad_gain_a, "dev", scatter_dimension=0, tiled=True),
        lax.psum_scatter(grad_shift_a, "dev", scatter_dimension=0, tiled=True),
        lax.psum_scatter(grad_gain_m, "dev", scatter_dimension=0, tiled=True),
        lax.psum_scatter(grad_shift_m, "dev", scatter_dimension=0, tiled=True),
        lax.psum_scatter(grad_w_qkv, "dev", scatter_dimension=0, tiled=True),
        lax.psum_scatter(grad_bias_qkv, "dev", scatter_dimension=0, tiled=True),
        lax.psum_scatter(grad_w_out, "dev", scatter_dimension=0, tiled=True),
        lax.psum_scatter(grad_bias_out, "dev", scatter_dimension=0, tiled=True),
        lax.psum_scatter(grad_w_up, "dev", scatter_dimension=0, tiled=True),
        lax.psum_scatter(grad_bias_up, "dev", scatter_dimension=0, tiled=True),
        lax.psum_scatter(grad_w_down, "dev", scatter_dimension=0, tiled=True),
        lax.psum_scatter(grad_bias_out, "dev", scatter_dimension=0, tiled=True),
    )
    return (block_out, grad_tokens) + tuple(shards)


def solution(mesh):
    placed = (
        P("dev", None),
        P("dev"),
        P("dev", None),
        P("dev"),
        P("dev"),
        P("dev"),
        P("dev"),
        P("dev", None),
        P("dev"),
        P("dev", None),
        P("dev"),
        P("dev", None),
        P("dev"),
        P("dev", None),
        P("dev"),
    )
    return jax.shard_map(
        local,
        mesh=mesh,
        in_specs=placed,
        out_specs=(
            P("dev", None),
            P("dev", None),
            P("dev"),
            P("dev"),
            P("dev"),
            P("dev"),
            P("dev", None),
            P("dev"),
            P("dev", None),
            P("dev"),
            P("dev", None),
            P("dev"),
            P("dev", None),
            P("dev"),
        ),
        check_vma=False,
    )
```

profile of v0, /device:TPU:0, one launch (start us, length us, event | category | flops | bytes accessed | tf_op | source)
XLA Modules:
  0.0 1153.4 jit_solution(13599410053093265000)
XLA Ops:
  23.2 42.8 %all-reduce.22 = (bf16[768]{0:T(1024)(128)(2,1)}, bf16[768]{0:T(1024)(128)(2,1)}, bf16[3072]{0:T(1024)(128)(2,1)}, bf16[2304]{0:T(1024)(128)(2,1)S(1)}, bf16[768...) all-reduce(bf16[768]{0:T(1024)(128)(2,1)S(1)} %dynamic-update-slice, ...), channel_id=1, replica_groups=mesh['dev'=32] {'dev'}, use_global_device_ids=true, to_apply=%add.11 | all-reduce | flops 9984 | bytes 39936
  76.5 10.2 convolution_add_fusion.1
  86.7 9.6 copy.41
  96.4 3.4 slice_bitcast_fusion
  101.5 3.2 collective-permute-start.2
  104.7 3.3 slice.341
  108.0 4.1 collective-permute-start
  113.6 19.6 %all-gather.7.cloned.1.call-done = bf16[768,768]{1,0:T(8,128)(2,1)} async-done(((bf16[24,768]{1,0:T(8,128)(2,1)}), bf16[768,768]{1,0:T(8,128)(2,1)}) %all-gather.7.cloned.1.call-update) | async-done | bytes 1179664 | tf_op jit(solution)/shard_map/all_gather | solution.py:79
  133.2 4.3 convolution_convert_fusion
  139.0 3.9 pad_maximum_fusion.3
  142.9 4.0 pad_maximum_fusion.2
  146.9 126.7 %while.36 = (s32[]{:T(128)}, bf16[6,1024,128]{1,2,0:T(8,128)(2,1)}, f32[6,2,1024]{2,1,0:T(2,128)}, s32[6]{0:T(128)S(1)}, bf16[2048,768]{0,1:T(8,128)(2,1)}, /*in...) while((s32[]{:T(128)}, bf16[6,1024,128]{1,2,0:T(8,128)(2,1)}, ...), condition=%wide.region_10.11_spmd.clone.clone, body=%wide.region_5.10_spmd.clone.sunk.clone | while | flops 1130890240 | bytes 69331144 | solution.py:170
  164.9 2.6 fusion.267
  186.0 2.6 fusion.267
  273.6 333.1 %while.37 = (s32[]{:T(128)}, f32[6,1024,128]{1,2,0:T(8,128)}, f32[6,2048,128]{1,2,0:T(8,128)}, f32[6,2048,128]{1,2,0:T(8,128)}, s32[6]{0:T(128)S(1)}, /*index=5*...) while((s32[]{:T(128)}, f32[6,1024,128]{1,2,0:T(8,128)}, ...), condition=%wide.region_14.15_spmd.clone.clone, body=%wide.region_11.14_spmd.clone.sunk.clone | while | flops 2754608128 | bytes 268561152 | solution.py:291
  288.9 4.6 fusion.298
  302.9 5.6 multiply_reduce_fusion.7
  312.2 4.6 fusion.292
  319.1 5.6 multiply_reduce_fusion.6
  342.4 4.6 fusion.298
  356.3 5.6 multiply_reduce_fusion.7
  365.6 4.6 fusion.292
  372.6 5.6 multiply_reduce_fusion.6
  395.8 4.6 fusion.298
  409.8 5.6 multiply_reduce_fusion.7
  419.1 4.6 fusion.292
  426.0 5.6 multiply_reduce_fusion.6
  449.3 4.6 fusion.298
  463.2 5.6 multiply_reduce_fusion.7
  472.6 4.6 fusion.292
  479.5 5.6 multiply_reduce_fusion.6
  502.8 4.6 fusion.298
  516.8 5.6 multiply_reduce_fusion.7
  526.1 4.6 fusion.292
  533.0 5.6 multiply_reduce_fusion.6
  556.2 4.6 fusion.298
  570.2 5.6 multiply_reduce_fusion.7
  579.5 4.6 fusion.292
  586.4 5.6 multiply_reduce_fusion.6
  606.7 6.7 fusion.101
  614.8 3.3 fusion.102
  620.8 3.9 split.24
  624.7 4.3 fusion.112
  629.1 6.9 fusion.66
  648.7 6.6 fusion.86
  655.4 33.5 %multiply_convert_fusion.3 = (bf16[512,3072]{1,0:T(8,128)(2,1)}, f32[512,3072]{1,0:T(8,128)}, bf16[512,3072]{1,0:T(8,128)(2,1)S(1)}, f32[512,3072]{1,0:T(8,128)}, f32[512,3072]{1,0:T(8,128)}) fusion(f32[3072]{0:T(1024)S(1)} %convert_element_type.161, f32[512,3072]{1,0:T(8,128)} %fusion.66, bf16[768,3072]{1,0:T(8,128)(2,1)} %all-gather.9.cloned.1.call-done, ...), kind=kOutput, calls=%fused_computation.97 | convolution fusion | flops 2623537152 | bytes 36974592 | tf_op jit(solution)/shard_map/dot_general | solution.py:180
  688.9 11.9 %convert_reduce_fusion.2 = (f32[3072]{0:T(1024)S(1)}, bf16[512,3072]{1,0:T(8,128)(2,1)S(1)}) fusion(f32[512,3072]{1,0:T(8,128)} %get-tuple-element.564, bf16[3072,768]{1,0:T(8,128)(2,1)} %all-gather.11.cloned.1.call-done, bf16[1024,768]{1,0:T(8,128)(2,1)} %param.21, f32[512,3072]{1,0:T(8,128)} %get-tuple-element.639, f32[3072]{0:T(1024)S(1)} %convert_element_type.161), kind=kOutput, calls=%fused_computation.81 | convolution fusion | flops 2442654720 | bytes 21258240 | tf_op jit(solution)/shard_map/td,fd->tf/dot_general | solution.py:222
  700.9 2.7 fusion.68
  703.6 9.0 convert_reduce_fusion.1
  714.3 5.2 convolution_add_fusion.3
  719.6 4.9 fusion.77
  724.6 5.5 convolution_add_fusion.2
  730.7 6.1 fusion.105
  736.9 3.8 fusion.106
  740.8 2.6 fusion.110
  743.4 2.6 fusion.111
  746.1 4.3 fusion.64
  750.6 9.3 fusion.91
  759.9 3.2 fusion.59
  763.2 3.8 convert_reduce_fusion.4
  767.0 89.3 %all-reduce.21 = (f32[768]{0:T(1024)S(1)}, f32[768]{0:T(1024)S(1)}, f32[768]{0:T(1024)S(1)}, f32[768]{0:T(1024)S(1)}, f32[2304]{0:T(1024)S(1)}, /*index=5*/f32[768]{0:T(1024)S(1)}, f32[3072]{0:T(1024)S(1)}) all-reduce(f32[768]{0:T(1024)S(1)} %get-tuple-element.492, ...), channel_id=2, replica_groups=mesh['dev'=32] {'dev'}, use_global_device_ids=true, to_apply=%region_20.21.clone | all-reduce | flops 9216 | bytes 73728
  860.0 2.7 reduce-scatter.5.cloned.1.call-done
  862.6 141.2 %reduce-scatter.9.cloned.1.call-done = f32[24,3072]{1,0:T(8,128)} async-done(((f32[768,3072]{1,0:T(8,128)}), f32[24,3072]{1,0:T(8,128)}) %reduce-scatter.9.cloned.1.call-update) | async-done | bytes 294928 | tf_op jit(solution)/shard_map/reduce_scatter | solution.py:328
  1003.8 142.1 %reduce-scatter.11.cloned.1.call-done = f32[96,768]{1,0:T(8,128)} async-done(((f32[3072,768]{1,0:T(8,128)}), f32[96,768]{1,0:T(8,128)}) %reduce-scatter.11.cloned.1.call-update) | async-done | bytes 294928 | tf_op jit(solution)/shard_map/reduce_scatter | solution.py:330
  (664 shorter events, 350.9 us)
Async XLA Ops:
  7.2 69.4 %all-gather.5.cloned.1.call-start = ((), (), s32[]{:S(2)}) async-start(), calls=%async_computation.4 | async-start | bytes 3649536 | tf_op jit(solution)/shard_map/all_gather | solution.py:77
  7.9 125.3 %all-gather.7.cloned.1.call-start = ((), (), s32[]{:S(2)}) async-start(), calls=%async_computation.5 | async-start | bytes 1216512 | tf_op jit(solution)/shard_map/all_gather | solution.py:79
  8.7 620.4 %all-gather.9.cloned.1.call-start = ((), (), s32[]{:S(2)}) async-start(), calls=%async_computation.6 | async-start | bytes 4866048 | tf_op jit(solution)/shard_map/all_gather | solution.py:81
  9.4 679.5 %all-gather.11.cloned.1.call-start = ((), (), s32[]{:S(2)}) async-start(), calls=%async_computation.7 | async-start | bytes 4866048 | tf_op jit(solution)/shard_map/all_gather | solution.py:83
  14.1 57.7 %collective-permute-start.1 = (s32[2]{0:T(128)S(1)}, s32[2]{0:T(128)S(1)}, u32[]{:S(2)}, u32[]{:S(2)}) collective-permute-start(s32[2]{0:T(128)S(1)} %pad_add_fusion.4), channel_id=1, source_target_pairs={{0,1},{1,2},{2,3},{3,4},{4,5},{5,6},{6,7},{7,8},{8,9},{9,10},{10,1... | collective-permute-start | bytes 32 | tf_op jit(solution)/shard_map/ppermute | solution.py:17
  66.0 20.7 %copy-start.37 = (f32[768]{0:T(1024)}, f32[768]{0:T(1024)S(1)}, u32[]{:S(2)}) copy-start(f32[768]{0:T(1024)S(1)} %convert_element_type.145) | copy-start | bytes 9220
  66.0 20.7 %copy-start.43 = (f32[768]{0:T(1024)}, f32[768]{0:T(1024)S(1)}, u32[]{:S(2)}) copy-start(f32[768]{0:T(1024)S(1)} %convert_element_type.146) | copy-start | bytes 9220
  69.1 17.6 %copy-start.28 = (f32[1024]{0:T(1024)}, f32[1024]{0:T(1024)S(1)}, u32[]{:S(2)}) copy-start(f32[1024]{0:T(1024)S(1)} %broadcast_multiply_fusion) | copy-start | bytes 12292
  71.8 15.0 %copy-start.32 = (f32[1024]{0:T(1024)}, f32[1024]{0:T(1024)S(1)}, u32[]{:S(2)}) copy-start(f32[1024]{0:T(1024)S(1)} %fusion.85) | copy-start | bytes 12292
  101.5 37.5 %collective-permute-start.2 = (bf16[1024,768]{0,1:T(8,128)(2,1)}, bf16[1024,768]{0,1:T(8,128)(2,1)}, u32[]{:S(2)}, u32[]{:S(2)}) collective-permute-start(bf16[1024,768]{0,1:T(8,128)(2,1)} %bitcast.12), channel_id=1, source_target_pairs={{0,1},{1,2},{2,3},{3,4},{4,5},{5,6},{6,7},{7,8},{8,9},{9,10},{10,1... | collective-permute-start | bytes 4718600 | tf_op jit(solution)/shard_map/ppermute | solution.py:17
  108.0 35.0 %collective-permute-start = (bf16[1024,768]{0,1:T(8,128)(2,1)}, bf16[1024,768]{0,1:T(8,128)(2,1)}, u32[]{:S(2)}, u32[]{:S(2)}) collective-permute-start(bf16[1024,768]{0,1:T(8,128)(2,1)} %bitcast.1), channel_id=1, source_target_pairs={{0,1},{1,2},{2,3},{3,4},{4,5},{5,6},{6,7},{7,8},{8,9},{9,10},{10,1... | collective-permute-start | bytes 4718600 | tf_op jit(solution)/shard_map/ppermute | solution.py:17
  112.1 747.8 %reduce-scatter.7.cloned.1.call-start = ((), (), s32[]{:S(2)}) async-start(), calls=%async_computation.9 | async-start | bytes 2433024 | tf_op jit(solution)/shard_map/reduce_scatter | solution.py:326
  285.6 7.9 copy-start.26
  285.6 7.9 copy-start.50
  302.9 5.6 slice-start
  302.9 5.9 slice-start.1
  319.1 5.6 slice-start.4
  319.1 5.9 slice-start.5
  339.0 7.9 copy-start.26
  339.0 7.9 copy-start.50
  356.3 5.6 slice-start
  356.3 5.9 slice-start.1
  372.5 5.6 slice-start.4
  372.5 5.9 slice-start.5
  392.5 7.9 copy-start.26
  392.5 7.9 copy-start.50
  409.8 5.9 slice-start.1
  426.0 5.6 slice-start.4
  426.0 5.9 slice-start.5
  446.0 7.9 copy-start.26
  446.0 7.9 copy-start.50
  463.2 5.9 slice-start.1
  479.5 5.6 slice-start.4
  479.5 5.9 slice-start.5
  499.5 7.9 copy-start.26
  499.5 7.9 copy-start.50
  516.8 5.9 slice-start.1
  533.0 5.6 slice-start.4
  533.0 5.9 slice-start.5
  552.9 7.9 copy-start.26
  552.9 7.9 copy-start.50
  570.2 5.6 slice-start
  570.2 5.9 slice-start.1
  586.4 5.6 slice-start.4
  586.4 5.9 slice-start.5
  606.7 8.0 copy-start.11
  613.4 22.6 %collective-permute-start.3 = (f32[1024,768]{0,1:T(8,128)}, f32[1024,768]{0,1:T(8,128)}, u32[]{:S(2)}, u32[]{:S(2)}) collective-permute-start(f32[1024,768]{0,1:T(8,128)} %bitcast.21), channel_id=1, source_target_pairs={{1,0},{2,1},{3,2},{4,3},{5,4},{6,5},{7,6},{8,7},{9,8},{10,9},{11,1... | collective-permute-start | bytes 9437192 | tf_op jit(solution)/shard_map/ppermute | solution.py:17
  618.1 6.6 copy-start.14
  618.1 23.2 %collective-permute-start.4 = (f32[1024,768]{0,1:T(8,128)}, f32[1024,768]{0,1:T(8,128)}, u32[]{:S(2)}, u32[]{:S(2)}) collective-permute-start(f32[1024,768]{0,1:T(8,128)} %bitcast.26), channel_id=1, source_target_pairs={{1,0},{2,1},{3,2},{4,3},{5,4},{6,5},{7,6},{8,7},{9,8},{10,9},{11,1... | collective-permute-start | bytes 9437192 | tf_op jit(solution)/shard_map/ppermute | solution.py:17
  620.8 8.3 copy-start.9
  629.0 233.6 %reduce-scatter.5.cloned.1.call-start = ((), (), s32[]{:S(2)}) async-start(), calls=%async_computation.8 | async-start | bytes 7299072 | tf_op jit(solution)/shard_map/reduce_scatter | solution.py:324
  629.1 7.0 copy-start.5
  655.3 348.5 %reduce-scatter.9.cloned.1.call-start = ((), (), s32[]{:S(2)}) async-start(), calls=%async_computation.10 | async-start | bytes 9732096 | tf_op jit(solution)/shard_map/reduce_scatter | solution.py:328
  688.9 35.7 %copy-start.7 = (bf16[512,3072]{1,0:T(8,128)(2,1)}, bf16[512,3072]{1,0:T(8,128)(2,1)S(1)}, u32[]{:S(2)}) copy-start(bf16[512,3072]{1,0:T(8,128)(2,1)S(1)} %get-tuple-element.629) | copy-start | bytes 9437188
  688.9 12.0 %copy-start.10 = (bf16[1024,768]{1,0:T(8,128)(2,1)S(1)}, bf16[1024,768]{1,0:T(8,128)(2,1)}, u32[]{:S(2)}) copy-start(bf16[1024,768]{1,0:T(8,128)(2,1)} %copy-done.9) | copy-start | bytes 4718596
  719.5 426.4 %reduce-scatter.11.cloned.1.call-start = ((), (), s32[]{:S(2)}) async-start(), calls=%async_computation.11 | async-start | bytes 9732096 | tf_op jit(solution)/shard_map/reduce_scatter | solution.py:330
  730.1 6.8 slice-start.6
  730.7 6.1 copy-start.20
  730.7 6.2 slice-start.7
  730.7 10.0 slice-start.8
  750.5 9.4 copy-start.41
  750.6 9.4 copy-start.12
  750.6 9.4 copy-start.34
  856.4 290.0 %copy-start.52 = (f32[24]{0:T(128)}, f32[24]{0:T(128)S(1)}, u32[]{:S(2)}) copy-start(f32[24]{0:T(128)S(1)} %dynamic-slice.5) | copy-start | bytes 292
  (73 other events, 246.0 us)
Sparse Core Ops, SparseCore 0:
  10.9 63.0 all-gather.4
  76.9 56.2 all-gather.6
  136.1 61.9 all-gather.8
  200.9 62.4 all-gather.10
  629.1 108.2 reduce-scatter.6
  744.5 118.0 reduce-scatter.4
  869.1 134.7 reduce-scatter.8
  1011.3 134.5 reduce-scatter.10
where the time goes:
time: 1160 us; the launch traced here: 1150 us
  matrix products  368 us (32%)
  waiting for transfers between devices  308 us (27%)
  local copies, waits for them, and re-layouts  141 us (12%)
  other arithmetic  141 us (12%)
  blocking collectives  132 us (11%)
  loops' own time  34 us (3%)
  between operations  17.2 us (1%)
  starting transfers between devices  12.7 us (1%)
    reduce_scatter x1, waiting for transfers between devices, local(): lax.psum_scatter(grad_w_down, 'dev', scatter_dimension=0, tiled=True)  142 us
    reduce_scatter x1, waiting for transfers between devices, local(): lax.psum_scatter(grad_w_up, 'dev', scatter_dimension=0, tiled=True)  141 us
    unnamed x2, blocking collectives  132 us
    dot_general x12, matrix products, pair_backward(): jnp.einsum('qhd,khd->hqk', d_block, value_pair, preferred_element_type=jn...  67.3 us
    dot_general x12, matrix products, pair_backward(): jnp.einsum('qhd,khd->hqk', query_block, key_pair, preferred_element_type=...  54.9 us
    dot_general x2, matrix products, local(): jnp.dot(mlp_in[offset:offset + query_rows], w_up, preferred_element_type=...  40.4 us
    dot_general x12, matrix products, pair_forward(): jnp.einsum('hqk,khd->qhd', attn_probs, value_pair, preferred_element_type...  31.3 us
    convert_element_type x12, other arithmetic, pair_backward(): d_scores = (prob_full * (d_probs - inner)).astype(jnp.bfloat16)  30.5 us
  transfers between devices with their start and end apart: 13, of which 4 were waited for; matrix products, arithmetic and copies ran while one was open for 55% of the time, Pallas kernels for 0%

commit v1 on v0

--- a/solution.py
+++ b/solution.py
@@ -100,8 +100,7 @@
     trailing = jnp.sum((seq_ids == last_id).astype(jnp.int32))
     before = from_behind(jnp.stack([last_id, trailing]), "dev", 1)
     carry = jnp.where(before[0] == seq_ids[0], before[1], 0)
-    opening = jnp.concatenate([jnp.ones((1,), jnp.bool_), seq_ids[1:] != seq_ids[:-1]])
-    seq_start = lax.cummax(jnp.where(opening, row_index, 0), axis=0)
+    seq_start = jnp.sum((seq_ids[None, :] < seq_ids[:, None]).astype(jnp.int32), axis=1)
     leading = seq_ids == seq_ids[0]
     positions = row_index - seq_start + jnp.where(leading, carry, 0)
     angles = angles_of(positions)

time: 1160 us -> 1170 us (level)
  no operation moved by 1% of the time
where the time goes in v1:
time: 1170 us; the launch traced here: 1150 us
  matrix products  368 us (31%)
  waiting for transfers between devices  308 us (26%)
  local copies, waits for them, and re-layouts  141 us (12%)
  other arithmetic  141 us (12%)
  blocking collectives  132 us (11%)
  loops' own time  34 us (3%)
  between operations  17.2 us (1%)
  starting transfers between devices  12.7 us (1%)
    reduce_scatter x1, waiting for transfers between devices, local(): lax.psum_scatter(grad_w_down, 'dev', scatter_dimension=0, tiled=True)  142 us
    reduce_scatter x1, waiting for transfers between devices, local(): lax.psum_scatter(grad_w_up, 'dev', scatter_dimension=0, tiled=True)  141 us
    unnamed x2, blocking collectives  132 us
    dot_general x12, matrix products, pair_backward(): jnp.einsum('qhd,khd->hqk', d_block, value_pair, preferred_element_type=jn...  67.3 us
    dot_general x12, matrix products, pair_backward(): jnp.einsum('qhd,khd->hqk', query_block, key_pair, preferred_element_type=...  55 us
    dot_general x2, matrix products, local(): jnp.dot(mlp_in[offset:offset + query_rows], w_up, preferred_element_type=...  40.4 us
    dot_general x12, matrix products, pair_forward(): jnp.einsum('hqk,khd->qhd', attn_probs, value_pair, preferred_element_type...  31.3 us
    convert_element_type x12, other arithmetic, pair_backward(): d_scores = (prob_full * (d_probs - inner)).astype(jnp.bfloat16)  30.5 us
  transfers between devices with their start and end apart: 13, of which 4 were waited for; matrix products, arithmetic and copies ran while one was open for 55% of the time, Pallas kernels for 0%

profile of v1, /device:TPU:0, one launch (start us, length us, event | category | flops | bytes accessed | tf_op | source)
XLA Modules:
  0.0 1154.0 jit_solution(11443385232002993601)
XLA Ops:
  23.2 42.8 %all-reduce.22 = (bf16[768]{0:T(1024)(128)(2,1)}, bf16[768]{0:T(1024)(128)(2,1)}, bf16[3072]{0:T(1024)(128)(2,1)}, bf16[2304]{0:T(1024)(128)(2,1)S(1)}, bf16[768...) all-reduce(bf16[768]{0:T(1024)(128)(2,1)S(1)} %dynamic-update-slice, ...), channel_id=1, replica_groups=mesh['dev'=32] {'dev'}, use_global_device_ids=true, to_apply=%add.11 | all-reduce | flops 9984 | bytes 39936
  76.4 10.2 convolution_add_fusion.1
  86.6 9.6 copy.43
  96.2 3.4 slice_bitcast_fusion
  101.3 3.2 collective-permute-start.2
  104.5 3.3 slice.320
  107.8 4.1 collective-permute-start
  113.4 19.8 %all-gather.7.cloned.1.call-done = bf16[768,768]{1,0:T(8,128)(2,1)} async-done(((bf16[24,768]{1,0:T(8,128)(2,1)}), bf16[768,768]{1,0:T(8,128)(2,1)}) %all-gather.7.cloned.1.call-update) | async-done | bytes 1179664 | tf_op jit(solution)/shard_map/all_gather | solution.py:79
  133.2 4.3 convolution_convert_fusion
  139.0 3.9 pad_maximum_fusion.3
  142.9 4.0 pad_maximum_fusion.2
  146.9 126.7 %while.36 = (s32[]{:T(128)}, bf16[6,1024,128]{1,2,0:T(8,128)(2,1)}, f32[6,2,1024]{2,1,0:T(2,128)}, s32[6]{0:T(128)S(1)}, bf16[2048,768]{0,1:T(8,128)(2,1)}, /*in...) while((s32[]{:T(128)}, bf16[6,1024,128]{1,2,0:T(8,128)(2,1)}, ...), condition=%wide.region_9.10_spmd.clone.clone, body=%wide.region_4.9_spmd.clone.sunk.clone | while | flops 1130890240 | bytes 69331144 | solution.py:169
  164.9 2.6 fusion.265
  207.0 2.6 fusion.265
  273.6 333.3 %while.37 = (s32[]{:T(128)}, f32[6,1024,128]{1,2,0:T(8,128)}, f32[6,2048,128]{1,2,0:T(8,128)}, f32[6,2048,128]{1,2,0:T(8,128)}, s32[6]{0:T(128)S(1)}, /*index=5*...) while((s32[]{:T(128)}, f32[6,1024,128]{1,2,0:T(8,128)}, ...), condition=%wide.region_13.14_spmd.clone.clone, body=%wide.region_10.13_spmd.clone.sunk.clone | while | flops 2754608128 | bytes 268561152 | solution.py:290
  288.9 4.6 fusion.296
  302.9 5.6 multiply_reduce_fusion.7
  312.2 4.6 fusion.290
  319.1 5.6 multiply_reduce_fusion.6
  342.4 4.6 fusion.296
  356.4 5.6 multiply_reduce_fusion.7
  365.7 4.6 fusion.290
  372.6 5.6 multiply_reduce_fusion.6
  395.8 4.6 fusion.296
  409.8 5.6 multiply_reduce_fusion.7
  419.1 4.6 fusion.290
  426.1 5.6 multiply_reduce_fusion.6
  449.3 4.6 fusion.296
  463.3 5.6 multiply_reduce_fusion.7
  472.6 4.6 fusion.290
  479.6 5.6 multiply_reduce_fusion.6
  502.8 4.6 fusion.296
  516.8 5.6 multiply_reduce_fusion.7
  526.1 4.6 fusion.290
  533.1 5.6 multiply_reduce_fusion.6
  556.3 4.6 fusion.296
  570.3 5.6 multiply_reduce_fusion.7
  579.6 4.6 fusion.290
  586.5 5.6 multiply_reduce_fusion.6
  606.9 6.7 fusion.99
  614.9 3.3 fusion.100
  620.9 3.9 split.24
  624.9 4.3 fusion.110
  629.2 7.0 fusion.66
  648.9 6.6 fusion.84
  655.6 33.5 %multiply_convert_fusion.3 = (bf16[512,3072]{1,0:T(8,128)(2,1)}, f32[512,3072]{1,0:T(8,128)}, bf16[512,3072]{1,0:T(8,128)(2,1)S(1)}, f32[512,3072]{1,0:T(8,128)}, f32[512,3072]{1,0:T(8,128)}) fusion(f32[3072]{0:T(1024)S(1)} %convert_element_type.165, f32[512,3072]{1,0:T(8,128)} %fusion.66, bf16[768,3072]{1,0:T(8,128)(2,1)} %all-gather.9.cloned.1.call-done, ...), kind=kOutput, calls=%fused_computation.97 | convolution fusion | flops 2623537152 | bytes 36974592 | tf_op jit(solution)/shard_map/dot_general | solution.py:179
  689.1 12.0 %convert_reduce_fusion.2 = (f32[3072]{0:T(1024)S(1)}, bf16[512,3072]{1,0:T(8,128)(2,1)S(1)}) fusion(f32[512,3072]{1,0:T(8,128)} %get-tuple-element.578, bf16[3072,768]{1,0:T(8,128)(2,1)} %all-gather.11.cloned.1.call-done, bf16[1024,768]{1,0:T(8,128)(2,1)} %param.21, f32[512,3072]{1,0:T(8,128)} %get-tuple-element.653, f32[3072]{0:T(1024)S(1)} %convert_element_type.165), kind=kOutput, calls=%fused_computation.81 | convolution fusion | flops 2442654720 | bytes 21258240 | tf_op jit(solution)/shard_map/td,fd->tf/dot_general | solution.py:221
  701.1 2.7 fusion.68
  703.8 9.0 convert_reduce_fusion.1
  714.5 5.2 convolution_add_fusion.3
  719.8 4.9 fusion.77
  724.8 5.5 convolution_add_fusion.2
  731.0 6.1 fusion.103
  737.2 3.8 fusion.104
  741.0 2.6 fusion.108
  743.7 2.6 fusion.109
  746.4 4.3 fusion.64
  750.8 9.3 fusion.89
  760.2 3.2 fusion.59
  763.5 3.8 convert_reduce_fusion.5
  767.3 89.2 %all-reduce.21 = (f32[768]{0:T(1024)S(1)}, f32[768]{0:T(1024)S(1)}, f32[768]{0:T(1024)S(1)}, f32[768]{0:T(1024)S(1)}, f32[2304]{0:T(1024)S(1)}, /*index=5*/f32[768]{0:T(1024)S(1)}, f32[3072]{0:T(1024)S(1)}) all-reduce(f32[768]{0:T(1024)S(1)} %get-tuple-element.506, ...), channel_id=2, replica_groups=mesh['dev'=32] {'dev'}, use_global_device_ids=true, to_apply=%region_19.20.clone | all-reduce | flops 9216 | bytes 73728
  860.0 3.0 reduce-scatter.5.cloned.1.call-done
  863.0 141.2 %reduce-scatter.9.cloned.1.call-done = f32[24,3072]{1,0:T(8,128)} async-done(((f32[768,3072]{1,0:T(8,128)}), f32[24,3072]{1,0:T(8,128)}) %reduce-scatter.9.cloned.1.call-update) | async-done | bytes 294928 | tf_op jit(solution)/shard_map/reduce_scatter | solution.py:327
  1004.3 142.2 %reduce-scatter.11.cloned.1.call-done = f32[96,768]{1,0:T(8,128)} async-done(((f32[3072,768]{1,0:T(8,128)}), f32[96,768]{1,0:T(8,128)}) %reduce-scatter.11.cloned.1.call-update) | async-done | bytes 294928 | tf_op jit(solution)/shard_map/reduce_scatter | solution.py:329
  (659 shorter events, 350.7 us)
Async XLA Ops:
  7.2 69.2 %all-gather.5.cloned.1.call-start = ((), (), s32[]{:S(2)}) async-start(), calls=%async_computation.4 | async-start | bytes 3649536 | tf_op jit(solution)/shard_map/all_gather | solution.py:77
  7.9 125.3 %all-gather.7.cloned.1.call-start = ((), (), s32[]{:S(2)}) async-start(), calls=%async_computation.5 | async-start | bytes 1216512 | tf_op jit(solution)/shard_map/all_gather | solution.py:79
  8.7 620.6 %all-gather.9.cloned.1.call-start = ((), (), s32[]{:S(2)}) async-start(), calls=%async_computation.6 | async-start | bytes 4866048 | tf_op jit(solution)/shard_map/all_gather | solution.py:81
  9.4 679.7 %all-gather.11.cloned.1.call-start = ((), (), s32[]{:S(2)}) async-start(), calls=%async_computation.7 | async-start | bytes 4866048 | tf_op jit(solution)/shard_map/all_gather | solution.py:83
  14.1 57.6 %collective-permute-start.1 = (s32[2]{0:T(128)S(1)}, s32[2]{0:T(128)S(1)}, u32[]{:S(2)}, u32[]{:S(2)}) collective-permute-start(s32[2]{0:T(128)S(1)} %pad_add_fusion.4), channel_id=1, source_target_pairs={{0,1},{1,2},{2,3},{3,4},{4,5},{5,6},{6,7},{7,8},{8,9},{9,10},{10,1... | collective-permute-start | bytes 32 | tf_op jit(solution)/shard_map/ppermute | solution.py:17
  66.0 20.6 %copy-start.37 = (f32[768]{0:T(1024)}, f32[768]{0:T(1024)S(1)}, u32[]{:S(2)}) copy-start(f32[768]{0:T(1024)S(1)} %convert_element_type.148) | copy-start | bytes 9220
  66.0 20.6 %copy-start.43 = (f32[768]{0:T(1024)}, f32[768]{0:T(1024)S(1)}, u32[]{:S(2)}) copy-start(f32[768]{0:T(1024)S(1)} %convert_element_type.149) | copy-start | bytes 9220
  69.0 17.5 %copy-start.28 = (f32[1024]{0:T(1024)}, f32[1024]{0:T(1024)S(1)}, u32[]{:S(2)}) copy-start(f32[1024]{0:T(1024)S(1)} %broadcast_multiply_fusion) | copy-start | bytes 12292
  71.7 14.9 %copy-start.32 = (f32[1024]{0:T(1024)}, f32[1024]{0:T(1024)S(1)}, u32[]{:S(2)}) copy-start(f32[1024]{0:T(1024)S(1)} %fusion.83) | copy-start | bytes 12292
  101.3 37.7 %collective-permute-start.2 = (bf16[1024,768]{0,1:T(8,128)(2,1)}, bf16[1024,768]{0,1:T(8,128)(2,1)}, u32[]{:S(2)}, u32[]{:S(2)}) collective-permute-start(bf16[1024,768]{0,1:T(8,128)(2,1)} %bitcast.10), channel_id=1, source_target_pairs={{0,1},{1,2},{2,3},{3,4},{4,5},{5,6},{6,7},{7,8},{8,9},{9,10},{10,1... | collective-permute-start | bytes 4718600 | tf_op jit(solution)/shard_map/ppermute | solution.py:17
  107.8 35.1 %collective-permute-start = (bf16[1024,768]{0,1:T(8,128)(2,1)}, bf16[1024,768]{0,1:T(8,128)(2,1)}, u32[]{:S(2)}, u32[]{:S(2)}) collective-permute-start(bf16[1024,768]{0,1:T(8,128)(2,1)} %bitcast.1), channel_id=1, source_target_pairs={{0,1},{1,2},{2,3},{3,4},{4,5},{5,6},{6,7},{7,8},{8,9},{9,10},{10,1... | collective-permute-start | bytes 4718600 | tf_op jit(solution)/shard_map/ppermute | solution.py:17
  112.0 748.1 %reduce-scatter.7.cloned.1.call-start = ((), (), s32[]{:S(2)}) async-start(), calls=%async_computation.9 | async-start | bytes 2433024 | tf_op jit(solution)/shard_map/reduce_scatter | solution.py:325
  285.5 7.9 copy-start.26
  285.6 7.9 copy-start.50
  302.9 5.9 slice-start.1
  319.1 5.6 slice-start.4
  319.1 5.9 slice-start.5
  339.0 7.9 copy-start.26
  339.0 7.9 copy-start.50
  356.4 5.9 slice-start.1
  372.6 5.6 slice-start.4
  372.6 5.9 slice-start.5
  392.5 7.9 copy-start.26
  392.5 7.9 copy-start.50
  409.8 5.6 slice-start
  409.8 5.9 slice-start.1
  426.0 5.6 slice-start.4
  426.1 5.9 slice-start.5
  446.0 7.9 copy-start.26
  446.0 7.9 copy-start.50
  463.3 5.9 slice-start.1
  479.5 5.6 slice-start.4
  479.5 5.9 slice-start.5
  499.5 7.9 copy-start.26
  499.5 7.9 copy-start.50
  516.8 5.6 slice-start
  516.8 5.9 slice-start.1
  533.0 5.6 slice-start.4
  533.1 5.9 slice-start.5
  553.0 7.9 copy-start.26
  553.0 7.9 copy-start.50
  570.3 5.6 slice-start
  570.3 5.9 slice-start.1
  586.5 5.6 slice-start.4
  586.5 5.9 slice-start.5
  606.8 8.0 copy-start.11
  613.6 22.6 %collective-permute-start.3 = (f32[1024,768]{0,1:T(8,128)}, f32[1024,768]{0,1:T(8,128)}, u32[]{:S(2)}, u32[]{:S(2)}) collective-permute-start(f32[1024,768]{0,1:T(8,128)} %bitcast.19), channel_id=1, source_target_pairs={{1,0},{2,1},{3,2},{4,3},{5,4},{6,5},{7,6},{8,7},{9,8},{10,9},{11,1... | collective-permute-start | bytes 9437192 | tf_op jit(solution)/shard_map/ppermute | solution.py:17
  618.2 6.6 copy-start.14
  618.2 23.2 %collective-permute-start.4 = (f32[1024,768]{0,1:T(8,128)}, f32[1024,768]{0,1:T(8,128)}, u32[]{:S(2)}, u32[]{:S(2)}) collective-permute-start(f32[1024,768]{0,1:T(8,128)} %bitcast.24), channel_id=1, source_target_pairs={{1,0},{2,1},{3,2},{4,3},{5,4},{6,5},{7,6},{8,7},{9,8},{10,9},{11,1... | collective-permute-start | bytes 9437192 | tf_op jit(solution)/shard_map/ppermute | solution.py:17
  620.9 8.3 copy-start.9
  629.1 233.9 %reduce-scatter.5.cloned.1.call-start = ((), (), s32[]{:S(2)}) async-start(), calls=%async_computation.8 | async-start | bytes 7299072 | tf_op jit(solution)/shard_map/reduce_scatter | solution.py:323
  629.2 7.0 copy-start.5
  655.5 348.7 %reduce-scatter.9.cloned.1.call-start = ((), (), s32[]{:S(2)}) async-start(), calls=%async_computation.10 | async-start | bytes 9732096 | tf_op jit(solution)/shard_map/reduce_scatter | solution.py:327
  689.1 35.7 %copy-start.7 = (bf16[512,3072]{1,0:T(8,128)(2,1)}, bf16[512,3072]{1,0:T(8,128)(2,1)S(1)}, u32[]{:S(2)}) copy-start(bf16[512,3072]{1,0:T(8,128)(2,1)S(1)} %get-tuple-element.643) | copy-start | bytes 9437188
  689.1 12.0 %copy-start.10 = (bf16[1024,768]{1,0:T(8,128)(2,1)S(1)}, bf16[1024,768]{1,0:T(8,128)(2,1)}, u32[]{:S(2)}) copy-start(bf16[1024,768]{1,0:T(8,128)(2,1)} %copy-done.9) | copy-start | bytes 4718596
  719.8 426.7 %reduce-scatter.11.cloned.1.call-start = ((), (), s32[]{:S(2)}) async-start(), calls=%async_computation.11 | async-start | bytes 9732096 | tf_op jit(solution)/shard_map/reduce_scatter | solution.py:329
  730.3 6.8 slice-start.6
  731.0 6.1 copy-start.20
  731.0 6.2 slice-start.7
  731.0 10.0 slice-start.8
  750.8 9.3 copy-start.41
  750.8 9.4 copy-start.12
  750.8 9.4 copy-start.34
  856.5 290.5 %copy-start.52 = (f32[24]{0:T(128)}, f32[24]{0:T(128)S(1)}, u32[]{:S(2)}) copy-start(f32[24]{0:T(128)S(1)} %dynamic-slice.5) | copy-start | bytes 292
  (73 other events, 246.1 us)
Sparse Core Ops, SparseCore 0:
  10.9 63.1 all-gather.4
  77.0 56.1 all-gather.6
  136.1 61.9 all-gather.8
  200.9 62.4 all-gather.10
  629.3 108.2 reduce-scatter.6
  744.6 118.3 reduce-scatter.4
  869.5 134.7 reduce-scatter.8
  1011.7 134.7 reduce-scatter.10

commit v2 on v1

v2 whole, which is shorter than its diff:
```python
import functools

import jax
import jax.numpy as jnp
from jax import lax
from jax.experimental import pallas as pl
from jax.experimental.pallas import tpu as pltpu
from jax.sharding import PartitionSpec as P

HDIM = 64
ROT = 16
EPSILON = 1e-05
MASKED = -1e30
BLOCK = 256
VMEM_BYTES = 58 << 20
F32 = jnp.float32
BF16 = jnp.bfloat16
AXIS = "dev"


def params_of(*semantics):
    return pltpu.CompilerParams(dimension_semantics=semantics, vmem_limit_bytes=VMEM_BYTES)


def mm(a, b):
    return lax.dot_general(a, b, (((1,), (0,)), ((), ())), preferred_element_type=F32)


def mm_bt(a, b):
    return lax.dot_general(a, b, (((1,), (1,)), ((), ())), preferred_element_type=F32)


def mm_at(a, b):
    return lax.dot_general(a, b, (((0,), (0,)), ((), ())), preferred_element_type=F32)


def split_axis(count):
    bits = (count // 2).bit_length() - 1
    small = 1 << (bits // 3)
    sizes = [count // 2 // small // small, small, small, 2]
    strides = [small * small * 2, small * 2, 2, 1]
    return sizes, strides


def shifted(value, size, stride, steps):
    count = lax.axis_size(AXIS)
    moves = []
    for source in range(count):
        digit = source // stride % size
        moves.append((source, source + ((digit + steps) % size - digit) * stride))
    return lax.ppermute(value, AXIS, moves)


def place(pieces, digit):
    count = len(pieces)
    if count == 2:
        mine, other = pieces
        first = jnp.where(digit == 0, mine, other)
        second = jnp.where(digit == 0, other, mine)
        return jnp.stack([first, second], axis=1)
    slots = [pieces[0]] * count
    for j in range(count):
        slots[j] = lax.select_n((digit - j) % count, *pieces)
    return jnp.stack(slots, axis=1)


def gather(value, order):
    sizes, strides = split_axis(lax.axis_size(AXIS))
    rows, width = value.shape
    held = [1, 1, 1, 1]
    me = lax.axis_index(AXIS)
    for dim in order:
        size = sizes[dim]
        digit = me // strides[dim] % size
        outer = 1
        inner = rows
        for d in range(4):
            if d < dim:
                outer *= held[d]
            if d > dim:
                inner *= held[d]
        piece = value.reshape(outer, inner, width)
        pieces = [piece] + [shifted(piece, size, strides[dim], s) for s in range(1, size)]
        value = place(pieces, digit)
        held[dim] = size
    return value.reshape(lax.axis_size(AXIS) * rows, width)


def scatter(value, order):
    sizes, strides = split_axis(lax.axis_size(AXIS))
    width = value.shape[1]
    rows = value.shape[0] // lax.axis_size(AXIS)
    held = list(sizes)
    me = lax.axis_index(AXIS)
    kind = value.dtype
    for dim in order:
        size = sizes[dim]
        digit = me // strides[dim] % size
        outer = 1
        inner = rows
        for d in range(4):
            if d < dim:
                outer *= held[d]
            if d > dim:
                inner *= held[d]
        parts = value.reshape(outer, size, inner, width)

        def part(at):
            return lax.dynamic_index_in_dim(parts, at, 1, keepdims=False)

        total = part(digit).astype(F32)
        for s in range(1, size):
            total = total + shifted(part((digit + s) % size), size, strides[dim], s).astype(F32)
        held[dim] = 1
        value = total if dim == order[-1] else total.astype(kind)
    return value.reshape(rows, width)


def from_behind(value, steps):
    count = lax.axis_size(AXIS)
    leading, last = (max(0, -steps), min(count, count - steps))
    return lax.ppermute(value, AXIS, [(source, source + steps) for source in range(leading, last)])


def normalize(values):
    center = values - jnp.mean(values, axis=-1, keepdims=True)
    spread = jnp.mean(center * center, axis=-1, keepdims=True)
    scale = lax.rsqrt(spread + EPSILON)
    return center * scale, scale


def norm_back(tokens, error, gain):
    normal, scale = normalize(tokens)
    scaled = error * gain
    first = jnp.mean(scaled, axis=-1, keepdims=True)
    second = jnp.mean(scaled * normal, axis=-1, keepdims=True)
    return scale * (scaled - first - normal * second), error * normal


def turn(values, table, sign):
    cosine = table[0]
    back = pltpu.roll(values, 120, 1) * table[1]
    ahead = pltpu.roll(values, 8, 1) * table[2]
    return values * cosine + sign * (back + ahead)


def qkv_body(x_ref, gain_ref, shift_ref, w_ref, b_ref, table_ref, out_ref, in_ref):
    width = x_ref.shape[1]
    normal, _ = normalize(x_ref[...].astype(F32))
    rows_in = (normal * gain_ref[...] + shift_ref[...]).astype(BF16)
    in_ref[...] = rows_in
    for j in range(0, out_ref.shape[1], 256):
        mixed = mm(rows_in, w_ref[:, j : j + 256]) + b_ref[:, j : j + 256]
        if j < 2 * width:
            for c in (0, 128):
                out_ref[:, j + c : j + c + 128] = turn(
                    mixed[:, c : c + 128], table_ref, 1.0
                ).astype(BF16)
        else:
            out_ref[:, j : j + 256] = mixed.astype(BF16)


def project(tokens, gain, shift, weight, bias, table):
    rows, width = tokens.shape
    total = 3 * width
    whole = lambda i: (0, 0)
    return pl.pallas_call(
        qkv_body,
        grid=(rows // BLOCK,),
        in_specs=[
            pl.BlockSpec((BLOCK, width), lambda i: (i, 0)),
            pl.BlockSpec((1, width), whole),
            pl.BlockSpec((1, width), whole),
            pl.BlockSpec(weight.shape, whole),
            pl.BlockSpec((1, total), whole),
            pl.BlockSpec((3, BLOCK, 128), lambda i: (0, i, 0)),
        ],
        out_specs=[
            pl.BlockSpec((BLOCK, total), lambda i: (i, 0)),
            pl.BlockSpec((BLOCK, width), lambda i: (i, 0)),
        ],
        out_shape=[
            jax.ShapeDtypeStruct((rows, total), BF16),
            jax.ShapeDtypeStruct((rows, width), BF16),
        ],
        compiler_params=params_of("arbitrary"),
        cost_estimate=pl.CostEstimate(
            flops=2 * rows * width * total, transcendentals=0, bytes_accessed=16 << 20
        ),
        name="qkv_project",
    )(tokens, gain, shift, weight, bias, table)


def attend_body(
    prior,
    first_ref,
    q_ref,
    k_ref,
    v_ref,
    pk_ref,
    pv_ref,
    dc_ref,
    low_ref,
    table_ref,
    ctx_ref,
    dq_ref,
    dk_ref,
    dv_ref,
    pdk_ref,
    pdv_ref,
    keys,
    vals,
    dk_sum,
    dv_sum,
):
    block = pl.program_id(1)
    lead = prior // BLOCK

    @pl.when(block == 0)
    def _():
        keys[:prior] = pk_ref[...]
        keys[prior:] = k_ref[...]
        vals[:prior] = pv_ref[...]
        vals[prior:] = v_ref[...]
        dk_sum[...] = jnp.zeros_like(dk_sum)
        dv_sum[...] = jnp.zeros_like(dv_sum)

    lane = lax.broadcasted_iota(jnp.int32, (BLOCK, 2 * HDIM), 1)
    heads = (lane < HDIM, lane >= HDIM)
    used = block + lead + 1 - first_ref[block]

    def blocks(count):
        start = (block + lead + 1 - count) * BLOCK
        query = (q_ref[...].astype(F32) * (HDIM**-0.5)).astype(BF16)
        incoming = dc_ref[...]
        low = low_ref[...]
        column = lax.broadcasted_iota(jnp.int32, (BLOCK, BLOCK), 1)
        row = lax.broadcasted_iota(jnp.int32, (BLOCK, BLOCK), 0)
        spans = [pl.ds(pl.multiple_of(start + b * BLOCK, BLOCK), BLOCK) for b in range(count)]
        ctx, d_query = [], []
        d_keys, d_vals = [[] for _ in spans], [[] for _ in spans]
        for mine in heads:
            own_query = jnp.where(mine, query, jnp.zeros_like(query))
            own_incoming = jnp.where(mine, incoming, jnp.zeros_like(incoming))
            scores = []
            for b, span in enumerate(spans):
                score = mm_bt(own_query, keys[span])
                allowed = column >= low - (start + b * BLOCK)
                if b == count - 1:
                    allowed = allowed & (column <= row)
                scores.append(jnp.where(allowed, score, MASKED))
            highest = functools.reduce(jnp.maximum, scores)
            highest = jnp.max(highest, axis=-1, keepdims=True)
            grown = [jnp.exp(score - highest) for score in scores]
            normal = jnp.sum(functools.reduce(jnp.add, grown), axis=-1, keepdims=True)
            inverse = 1.0 / normal
            probs = [g * inverse for g in grown]
            low_probs = [p.astype(BF16) for p in probs]
            d_probs = [mm_bt(own_incoming, vals[span]) for span in spans]
            inner = functools.reduce(jnp.add, [p * d for p, d in zip(probs, d_probs)])
            inner = jnp.sum(inner, axis=-1, keepdims=True)
            d_scores = [(p * (d - inner)).astype(BF16) for p, d in zip(probs, d_probs)]
            ctx.append(functools.reduce(jnp.add, [mm(p, vals[s]) for p, s in zip(low_probs, spans)]))
            d_query.append(
                functools.reduce(jnp.add, [mm(d, keys[s]) for d, s in zip(d_scores, spans)])
            )
            for b in range(count):
                d_keys[b].append(mm_at(d_scores[b], query))
                d_vals[b].append(mm_at(low_probs[b], incoming))
        ctx_ref[...] = jnp.where(heads[0], ctx[0], ctx[1]).astype(BF16)
        both = jnp.where(heads[0], d_query[0], d_query[1]) * (HDIM**-0.5)
        dq_ref[...] = turn(both, table_ref, -1.0).astype(BF16)
        for b, span in enumerate(spans):
            dk_sum[span] += jnp.where(heads[0], d_keys[b][0], d_keys[b][1])
            dv_sum[span] += jnp.where(heads[0], d_vals[b][0], d_vals[b][1])

    most = k_ref.shape[0] // BLOCK + 1
    for count in range(1, most + 1):
        pl.when(used == count)(functools.partial(blocks, count))

    @pl.when(block == pl.num_programs(1) - 1)
    def _():
        pdk_ref[...] = dk_sum[:prior].astype(BF16)
        pdv_ref[...] = dv_sum[:prior].astype(BF16)
        dk_ref[...] = dk_sum[prior:]
        dv_ref[...] = dv_sum[prior:]


def attend(first, qkv, before, d_context, low, table):
    rows, width = d_context.shape
    prior = before.shape[0]
    pairs = width // 128
    wide = lambda off: (lambda p, i, f: (0, off + p))
    tile = lambda p, i, f: (i, p)
    return pl.pallas_call(
        functools.partial(attend_body, prior),
        grid_spec=pltpu.PrefetchScalarGridSpec(
            num_scalar_prefetch=1,
            grid=(pairs, rows // BLOCK),
            in_specs=[
                pl.BlockSpec((BLOCK, 128), tile),
                pl.BlockSpec((rows, 128), wide(pairs)),
                pl.BlockSpec((rows, 128), wide(2 * pairs)),
                pl.BlockSpec((prior, 128), wide(0)),
                pl.BlockSpec((prior, 128), wide(pairs)),
                pl.BlockSpec((BLOCK, 128), tile),
                pl.BlockSpec((BLOCK, 1), lambda p, i, f: (i, 0)),
                pl.BlockSpec((3, BLOCK, 128), lambda p, i, f: (0, i, 0)),
            ],
            out_specs=[
                pl.BlockSpec((BLOCK, 128), tile),
                pl.BlockSpec((BLOCK, 128), tile),
                pl.BlockSpec((rows, 128), wide(0)),
                pl.BlockSpec((rows, 128), wide(0)),
                pl.BlockSpec((prior, 128), wide(0)),
                pl.BlockSpec((prior, 128), wide(0)),
            ],
            scratch_shapes=[
                pltpu.VMEM((prior + rows, 128), BF16),
                pltpu.VMEM((prior + rows, 128), BF16),
                pltpu.VMEM((prior + rows, 128), F32),
                pltpu.VMEM((prior + rows, 128), F32),
            ],
        ),
        out_shape=[
            jax.ShapeDtypeStruct((rows, width), BF16),
            jax.ShapeDtypeStruct((rows, width), BF16),
            jax.ShapeDtypeStruct((rows, width), F32),
            jax.ShapeDtypeStruct((rows, width), F32),
            jax.ShapeDtypeStruct((prior, width), BF16),
            jax.ShapeDtypeStruct((prior, width), BF16),
        ],
        compiler_params=params_of("arbitrary", "arbitrary"),
        cost_estimate=pl.CostEstimate(
            flops=50 * 10**9, transcendentals=10**7, bytes_accessed=24 << 20
        ),
        name="attend",
    )(first, qkv, qkv, qkv, before, before, d_context, low, table)


def mlp_body(
    x_ref,
    cot_ref,
    gain_ref,
    shift_ref,
    up_ref,
    bias_ref,
    down_ref,
    ffn_ref,
    d_up_ref,
    d_down_ref,
    d_bias_ref,
    back_ref,
    d_gain_ref,
    d_shift_ref,
    d_out_ref,
    in_ref,
    active,
    d_hidden,
):
    step = pl.program_id(0)
    rows = x_ref.shape[0]
    spans = [slice(r, r + BLOCK) for r in range(0, rows, BLOCK)]

    @pl.when(step == 0)
    def _():
        for s in spans:
            normal, _ = normalize(x_ref[s].astype(F32))
            in_ref[s] = (normal * gain_ref[...] + shift_ref[...]).astype(BF16)
        ffn_ref[...] = jnp.zeros_like(ffn_ref)
        back_ref[...] = jnp.zeros_like(back_ref)
        d_out_ref[...] = jnp.sum(cot_ref[...].astype(F32), axis=0, keepdims=True)

    summed = 0.0
    for s in spans:
        hidden = mm(in_ref[s], up_ref[...]) + bias_ref[...]
        d_active = mm_bt(cot_ref[s], down_ref[...])
        phi = 0.5 + 0.5 * lax.erf(hidden * (0.5**0.5))
        density = jnp.exp(hidden * hidden * -0.5) * 0.3989422804014327
        active[s] = (hidden * phi).astype(BF16)
        moved = (d_active * (phi + hidden * density)).astype(BF16)
        d_hidden[s] = moved
        summed = summed + jnp.sum(moved.astype(F32), axis=0, keepdims=True)
    d_bias_ref[...] = summed
    d_down_ref[...] = mm_at(active[...], cot_ref[...]).astype(BF16)
    d_up_ref[...] = mm_at(in_ref[...], d_hidden[...]).astype(BF16)
    for s in spans:
        ffn_ref[s] += mm(active[s], down_ref[...])
        back_ref[s] += mm_bt(d_hidden[s], up_ref[...])

    @pl.when(step == pl.num_programs(0) - 1)
    def _():
        d_gain, d_shift = 0.0, 0.0
        for s in spans:
            error = back_ref[s]
            moved, product = norm_back(x_ref[s].astype(F32), error, gain_ref[...])
            d_gain = d_gain + jnp.sum(product, axis=0, keepdims=True)
            d_shift = d_shift + jnp.sum(error, axis=0, keepdims=True)
            back_ref[s] = cot_ref[s].astype(F32) + moved
        d_gain_ref[...] = d_gain
        d_shift_ref[...] = d_shift


def mlp(tokens, cotangent, gain, shift, up, up_bias, down):
    rows, width = tokens.shape
    ff = down.shape[0]
    tile = 512
    whole = lambda j: (0, 0)
    vector = pl.BlockSpec((1, width), whole)
    full = pl.BlockSpec((rows, width), whole)
    return pl.pallas_call(
        mlp_body,
        grid=(ff // tile,),
        in_specs=[
            full,
            full,
            vector,
            vector,
            pl.BlockSpec((width, tile), lambda j: (0, j)),
            pl.BlockSpec((1, tile), lambda j: (0, j)),
            pl.BlockSpec((tile, width), lambda j: (j, 0)),
        ],
        out_specs=[
            full,
            pl.BlockSpec((width, tile), lambda j: (0, j)),
            pl.BlockSpec((tile, width), lambda j: (j, 0)),
            pl.BlockSpec((1, tile), lambda j: (0, j)),
            full,
            vector,
            vector,
            vector,
        ],
        out_shape=[
            jax.ShapeDtypeStruct((rows, width), F32),
            jax.ShapeDtypeStruct((width, ff), BF16),
            jax.ShapeDtypeStruct((ff, width), BF16),
            jax.ShapeDtypeStruct((1, ff), F32),
            jax.ShapeDtypeStruct((rows, width), F32),
            jax.ShapeDtypeStruct((1, width), F32),
            jax.ShapeDtypeStruct((1, width), F32),
            jax.ShapeDtypeStruct((1, width), F32),
        ],
        scratch_shapes=[
            pltpu.VMEM((rows, width), BF16),
            pltpu.VMEM((rows, tile), BF16),
            pltpu.VMEM((rows, tile), BF16),
        ],
        compiler_params=params_of("arbitrary"),
        cost_estimate=pl.CostEstimate(
            flops=12 * rows * width * ff, transcendentals=2 * rows * ff, bytes_accessed=30 << 20
        ),
        name="mlp",
    )(tokens, cotangent, gain, shift, up, up_bias, down)


def back_body(
    per_part,
    x_ref,
    in_ref,
    gain_ref,
    w_ref,
    dq_ref,
    dk_ref,
    dv_ref,
    hk_ref,
    hv_ref,
    table_ref,
    rest_ref,
    d_w_ref,
    d_bias_ref,
    grad_ref,
    d_gain_ref,
    d_shift_ref,
    moved,
):
    step = pl.program_id(0)
    rows = x_ref.shape[0]
    own = rows - hk_ref.shape[0]
    spans = [slice(r, r + BLOCK) for r in range(0, rows, BLOCK)]

    @pl.when(step == 0)
    def _():
        grad_ref[...] = jnp.zeros_like(grad_ref)

    @pl.when(step < per_part)
    def _():
        moved[...] = dq_ref[...]

    @pl.when((step >= per_part) & (step < 2 * per_part))
    def _():
        for s in spans:
            for c in range(0, moved.shape[1], 128):
                part = dk_ref[s, c : c + 128]
                if s.start >= own:
                    part = part + hk_ref[s.start - own : s.stop - own, c : c + 128].astype(F32)
                moved[s, c : c + 128] = turn(part, table_ref[:, s], -1.0).astype(BF16)

    @pl.when(step >= 2 * per_part)
    def _():
        for s in spans:
            part = dv_ref[s]
            if s.start >= own:
                part = part + hv_ref[s.start - own : s.stop - own].astype(F32)
            moved[s] = part.astype(BF16)

    d_bias_ref[...] = jnp.sum(moved[...].astype(F32), axis=0, keepdims=True)
    d_w_ref[...] = mm_at(in_ref[...], moved[...]).astype(BF16)
    for s in spans:
        grad_ref[s] += mm_bt(moved[s], w_ref[...])

    @pl.when(step == pl.num_programs(0) - 1)
    def _():
        d_gain, d_shift = 0.0, 0.0
        for s in spans:
            error = grad_ref[s]
            back, product = norm_back(x_ref[s].astype(F32), error, gain_ref[...])
            d_gain = d_gain + jnp.sum(product, axis=0, keepdims=True)
            d_shift = d_shift + jnp.sum(error, axis=0, keepdims=True)
            grad_ref[s] = rest_ref[s] + back
        d_gain_ref[...] = d_gain
        d_shift_ref[...] = d_shift


def back(tokens, attn_in, gain, weight, dq, dk, dv, halo_k, halo_v, table, rest):
    rows, width = tokens.shape
    tile = 256
    per = width // tile
    total = 3 * width
    prior = halo_k.shape[0]
    whole = lambda j: (0, 0)
    vector = pl.BlockSpec((1, width), whole)
    full = pl.BlockSpec((rows, width), whole)
    near = lambda off: (lambda j: (0, jnp.clip(j - off, 0, per - 1)))
    return pl.pallas_call(
        functools.partial(back_body, per),
        grid=(total // tile,),
        in_specs=[
            full,
            full,
            vector,
            pl.BlockSpec((width, tile), lambda j: (0, j)),
            pl.BlockSpec((rows, tile), near(0)),
            pl.BlockSpec((rows, tile), near(per)),
            pl.BlockSpec((rows, tile), near(2 * per)),
            pl.BlockSpec((prior, tile), near(per)),
            pl.BlockSpec((prior, tile), near(2 * per)),
            pl.BlockSpec((3, rows, 128), lambda j: (0, 0, 0)),
            full,
        ],
        out_specs=[
            pl.BlockSpec((width, tile), lambda j: (0, j)),
            pl.BlockSpec((1, tile), lambda j: (0, j)),
            full,
            vector,
            vector,
        ],
        out_shape=[
            jax.ShapeDtypeStruct((width, total), BF16),
            jax.ShapeDtypeStruct((1, total), F32),
            jax.ShapeDtypeStruct((rows, width), F32),
            jax.ShapeDtypeStruct((1, width), F32),
            jax.ShapeDtypeStruct((1, width), F32),
        ],
        scratch_shapes=[pltpu.VMEM((rows, tile), BF16)],
        compiler_params=params_of("arbitrary"),
        cost_estimate=pl.CostEstimate(
            flops=4 * rows * width * total, transcendentals=0, bytes_accessed=30 << 20
        ),
        name="qkv_back",
    )(tokens, attn_in, gain, weight, dq, dk, dv, halo_k, halo_v, table, rest)


def local(
    tokens,
    seq_ids,
    cotangent,
    attn_gain,
    attn_shift,
    mlp_gain,
    mlp_shift,
    qkv_weight,
    qkv_bias,
    out_weight,
    out_bias,
    up_weight,
    up_bias,
    down_weight,
    down_bias,
):
    rows, width = tokens.shape
    own = attn_gain.shape[0]
    prior = rows // 2
    vectors = (
        attn_gain,
        attn_shift,
        mlp_gain,
        mlp_shift,
        qkv_bias,
        out_bias,
        up_bias,
        down_bias,
    )
    counts = [v.shape[0] // own for v in vectors]
    packed = jnp.concatenate([v.reshape(own, -1) for v in vectors], axis=1)
    packed = jnp.pad(packed, ((0, 0), (0, 128 - packed.shape[1])))

    first_half = gather(jnp.concatenate([qkv_weight, packed], axis=1), (0, 2, 1, 3))
    w_down = gather(down_weight, (0, 1, 2, 3))
    second = gather(jnp.concatenate([up_weight, out_weight], axis=1), (1, 2, 0, 3))
    w_out = second[:, up_weight.shape[1] :]
    flat, at = [], qkv_weight.shape[1]
    small = first_half[:, at : at + 128].astype(F32)
    at = 0
    for count in counts:
        flat.append(small[:, at : at + count].reshape(1, -1))
        at += count
    gain_a, shift_a, gain_m, shift_m, b_qkv, b_out, b_up, b_down = flat

    row_index = jnp.arange(rows, dtype=jnp.int32)
    last_id = seq_ids[rows - 1]
    trailing = jnp.sum((seq_ids == last_id).astype(jnp.int32))
    before = from_behind(jnp.stack([last_id, trailing]), 1)
    carry = jnp.where(before[0] == seq_ids[0], before[1], 0)
    smaller = jnp.sum((seq_ids[None, :] < seq_ids[:, None]).astype(jnp.int32), axis=1)
    begins = jnp.where(seq_ids == seq_ids[0], -carry, smaller)
    low = begins + prior
    first_block = low[::BLOCK] // BLOCK
    frequency = 10000.0 ** (-2.0 * jnp.arange(ROT // 2, dtype=F32) / ROT)
    angles = (row_index - begins).astype(F32)[:, None] * frequency[None, :]
    cosine, sine = jnp.cos(angles), jnp.sin(angles)
    lane = jnp.arange(128) % HDIM
    spread = lambda v: jnp.tile(v, (1, 128 // v.shape[1]))
    table = jnp.stack(
        [
            jnp.where(lane < ROT, spread(cosine), 1.0),
            jnp.where(lane < ROT // 2, -spread(sine), 0.0),
            jnp.where((lane >= ROT // 2) & (lane < ROT), spread(sine), 0.0),
        ]
    )

    qkv, attn_in = project(tokens, gain_a, shift_a, first_half, b_qkv, table)
    halo = from_behind(qkv[rows - prior :, width:], 1)
    ffn, d_up, d_down, d_up_bias, rest, d_gain_m, d_shift_m, d_out_bias = mlp(
        tokens, cotangent, gain_m, shift_m, second, b_up, w_down
    )
    d_context = mm_bt(cotangent, w_out).astype(BF16)
    context, dq, dk, dv, back_k, back_v = attend(
        first_block, qkv, halo, d_context, low[:, None], table
    )
    halo_k = from_behind(back_k, -1)
    halo_v = from_behind(back_v, -1)
    block_out = (tokens.astype(F32) + (mm(context, w_out) + b_out) + (ffn + b_down)).astype(BF16)
    d_out = mm_at(context, cotangent).astype(BF16)
    d_qkv, d_qkv_bias, grad_tokens, d_gain_a, d_shift_a = back(
        tokens, attn_in, gain_a, first_half, dq, dk, dv, halo_k, halo_v, table, rest
    )

    d_down = scatter(d_down, (3, 2, 1, 0))
    d_up = scatter(d_up, (3, 0, 2, 1))
    d_out = scatter(d_out, (3, 1, 0, 2))
    d_qkv = scatter(d_qkv, (3, 1, 0, 2))
    sums = (
        d_gain_a,
        d_shift_a,
        d_gain_m,
        d_shift_m,
        d_qkv_bias,
        d_out_bias,
        d_up_bias,
    )
    wide = jnp.concatenate([s.reshape(width, -1) for s in sums], axis=1)
    wide = jnp.pad(wide, ((0, 0), (0, 128 - wide.shape[1])))
    wide = scatter(wide, (3, 2, 1, 0))
    out, at = [], 0
    for s in sums:
        count = s.shape[1] // width
        out.append(wide[:, at : at + count].reshape(-1))
        at += count
    g_gain_a, g_shift_a, g_gain_m, g_shift_m, g_qkv_b, g_out_b, g_up_b = out
    return (
        block_out,
        grad_tokens,
        g_gain_a,
        g_shift_a,
        g_gain_m,
        g_shift_m,
        d_qkv,
        g_qkv_b,
        d_out,
        g_out_b,
        d_up,
        g_up_b,
        d_down,
        g_out_b,
    )


def solution(mesh):
    wide, thin = P("dev", None), P("dev")
    return jax.shard_map(
        local,
        mesh=mesh,
        in_specs=(
            wide,
            thin,
            wide,
            thin,
            thin,
            thin,
            thin,
            wide,
            thin,
            wide,
            thin,
            wide,
            thin,
            wide,
            thin,
        ),
        out_specs=(
            wide,
            wide,
            thin,
            thin,
            thin,
            thin,
            wide,
            thin,
            wide,
            thin,
            wide,
            thin,
            wide,
            thin,
        ),
        check_vma=False,
    )
```

time: 1170 us -> 492 us (0.42)
  matrix products: 368 us -> 9.55 us
  waiting for transfers between devices: 308 us -> 131 us
  blocking collectives: 132 us -> 0 us
  Pallas kernels: 0 us -> 127 us
  starting transfers between devices: 12.7 us -> 124 us
  other arithmetic: 141 us -> 33.1 us
  local copies, waits for them, and re-layouts: 141 us -> 53 us
  loops' own time: 34 us -> 0 us
  between operations: 17.2 us -> 4.2 us
    dot_general x102 -> x3, matrix products: 368 us -> 9.55 us  [the longest x1 3.98 us: mm(): lax.dot_general(a, b, (((1,), (0,)), ((), ())), preferred_element_type=F32)]
    reduce_scatter x4 -> x0, waiting for transfers between devices: 286 us -> none  [the longest x1 142 us: local(): lax.psum_scatter(grad_w_down, 'dev', scatter_dimension=0, tiled=True)]
    unnamed x2 -> x0, blocking collectives: 132 us -> none
    ppermute x5 -> x52, waiting for transfers between devices: 0.01 us -> 131 us  [the longest x48 131 us: shifted(): return lax.ppermute(value, AXIS, moves)]
    pallas_call x0 -> x4, Pallas kernels: none -> 127 us  [the longest x1 54.6 us: attend(): pl.pallas_call(functools.partial(attend_body, prior), grid_spec=pltpu.Pre...]
    ppermute x5 -> x52, starting transfers between devices: 12.4 us -> 124 us  [the longest x48 116 us: shifted(): return lax.ppermute(value, AXIS, moves)]
    reduce_sum x18 -> x0, other arithmetic: 42.7 us -> none  [the longest x12 30.5 us: pair_forward(): normal = jnp.sum(exponent, axis=-1, keepdims=True)]
    another operation x2 -> x0, loops' own time: 34 us -> none  [the longest x1 29.2 us: local(): lax.map(pair_backward, jnp.arange(pair_count))]
  transfers between devices with their start and end apart: 13 -> 52, of which waited for: 4 -> 18; matrix products, arithmetic and copies ran while one was open for 55% -> 19% of each run, Pallas kernels for 0% -> 26%
where the time goes in v2:
time: 492 us; the launch traced here: 482 us
  waiting for transfers between devices  131 us (27%)
  Pallas kernels  127 us (26%)
  starting transfers between devices  124 us (25%)
  local copies, waits for them, and re-layouts  53 us (11%)
  other arithmetic  33.1 us (7%)
  matrix products  9.55 us (2%)
    ppermute x48, waiting for transfers between devices, shifted(): return lax.ppermute(value, AXIS, moves)  131 us
    ppermute x48, starting transfers between devices, shifted(): return lax.ppermute(value, AXIS, moves)  116 us
    pallas_call x1, Pallas kernels, attend(): pl.pallas_call(functools.partial(attend_body, prior), grid_spec=pltpu.Pre...  54.6 us
    pallas_call x1, Pallas kernels, mlp(): pl.pallas_call(mlp_body, grid=(ff // tile,), in_specs=[full, full, vector...  41.6 us
    pallas_call x1, Pallas kernels, back(): pl.pallas_call(functools.partial(back_body, per), grid=(total // tile,),...  21.5 us
  transfers between devices with their start and end apart: 52, of which 18 were waited for; matrix products, arithmetic and copies ran while one was open for 19% of the time, Pallas kernels for 26%

profile of v2, /device:TPU:0, one launch (start us, length us, event | category | flops | bytes accessed | tf_op | source)
XLA Modules:
  0.0 482.1 jit_solution(16996953582162631286)
XLA Ops:
  0.6 3.1 collective-permute-start.14
  3.7 2.6 collective-permute-start.15
  13.5 1.8 collective-permute-start.2
  16.6 2.0 convert_reduce_fusion.1
  23.9 4.6 collective-permute-start.3
  38.4 2.8 collective-permute-done.16
  41.4 1.5 collective-permute-start.17
  44.1 7.4 %collective-permute-done.4 = bf16[4,24,2432]{2,1,0:T(8,128)(2,1)S(1)} collective-permute-done((bf16[4,24,2432]{2,1,0:T(8,128)(2,1)S(1)}, bf16[4,24,2432]{2,1,0:T(8,128)(2,1)S(1)}, u32[]{:S(2)}, u32[]{:S(2)}) %collective-permute-start.4) | collective-permute-done | bytes 466976 | tf_op jit(solution)/shard_map/ppermute | solution.py:51
  53.0 4.9 %collective-permute-done.9 = bf16[2,24,3840]{2,1,0:T(8,128)(2,1)S(1)} collective-permute-done((bf16[2,24,3840]{2,1,0:T(8,128)(2,1)S(1)}, bf16[2,24,3840]{2,1,0:T(8,128)(2,1)S(1)}, u32[]{:S(2)}, u32[]{:S(2)}) %collective-permute-start.9) | collective-permute-done | bytes 368672 | tf_op jit(solution)/shard_map/ppermute | solution.py:51
  59.4 2.0 collective-permute-start.11
  62.9 1.6 collective-permute-start.18
  64.5 11.2 %collective-permute-done.5 = bf16[4,48,2432]{2,1,0:T(8,128)(2,1)S(1)} collective-permute-done((bf16[4,48,2432]{2,1,0:T(8,128)(2,1)S(1)}, bf16[4,48,2432]{2,1,0:T(8,128)(2,1)S(1)}, u32[]{:S(2)}, u32[]{:S(2)}) %collective-permute-start.5) | collective-permute-done | bytes 933920 | tf_op jit(solution)/shard_map/ppermute | solution.py:51
  76.4 3.1 collective-permute-done.10
  79.5 29.3 %collective-permute-done.11 = bf16[1,96,3840]{2,1,0:T(8,128)(2,1)S(1)} collective-permute-done((bf16[1,96,3840]{2,1,0:T(8,128)(2,1)S(1)}, bf16[1,96,3840]{2,1,0:T(8,128)(2,1)S(1)}, u32[]{:S(2)}, u32[]{:S(2)}) %collective-permute-start.11) | collective-permute-done | bytes 737312 | tf_op jit(solution)/shard_map/ppermute | solution.py:51
  112.6 1.6 copy.162
  115.3 1.8 copy-done.2
  118.0 1.9 reshape.509.b_ref
  122.3 9.2 %qkv_project.1 = (bf16[1024,2304]{1,0:T(8,128)(2,1)}, bf16[1024,768]{1,0:T(8,128)(2,1)}) custom-call(bf16[1024,768]{1,0:T(8,128)(2,1)} %x_ref.5, f32[1,768]{1,0:T(1,128)} %reshape.507.gain_ref, f32[1,768]{1,0:T(1,128)} %reshape.508.shift_ref, bf16[768,2432]{1,0:T(8,128)(2,1)} %bitcast.280, f32[1,2304]{1,0:T(1,128)} %reshape.509.b_ref, ...), custom_call_target="tpu_custom_call" | custom-call | flops 3623878656 | bytes 16777216 | tf_op jit(solution)/shard_map/qkv_project/pallas_call | solution.py:167
  132.4 1.9 reshape.517.bias_ref
  135.5 2.7 slice.79
  138.1 4.0 collective-permute-start.7
  142.2 2.2 select_bitcast_fusion.1
  145.8 2.6 fusion.5.dc_ref
  148.4 2.7 select_bitcast_fusion.3
  151.5 2.6 copy.163
  154.1 41.6 %mlp.1 = (f32[1024,768]{1,0:T(8,128)}, bf16[768,3072]{1,0:T(8,128)(2,1)}, bf16[3072,768]{1,0:T(8,128)(2,1)}, f32[1,3072]{1,0:T(1,128)}, f32[1024,768]{1,0:T(8,12...) custom-call(bf16[1024,768]{1,0:T(8,128)(2,1)} %x_ref.5, bf16[1024,768]{1,0:T(8,128)(2,1)} %cot_ref.1, ...), custom_call_target="tpu_custom_call" | custom-call | flops 28991029248 | bytes 31457280 | tf_op jit(solution)/shard_map/mlp/pallas_call | solution.py:411
  195.7 3.4 dynamic-slice_bitcast_fusion
  199.5 1.7 dynamic-slice_bitcast_fusion.1
  205.8 54.6 %attend.1 = (bf16[1024,768]{1,0:T(8,128)(2,1)}, bf16[1024,768]{1,0:T(8,128)(2,1)}, f32[1024,768]{1,0:T(8,128)}, f32[1024,768]{1,0:T(8,128)}, bf16[512,768]{1,0:T(8,128)(2,1)}, /*index=5*/bf16[512,768]{1,0:T(8,128)(2,1)}) custom-call(s32[4]{0:T(128)} %and_select_fusion.1.first_ref, bf16[1024,2304]{1,0:T(8,128)(2,1)} %get-tuple-element.35.q_ref.k_ref.v_ref, ...), custom_call_target="tpu_custom_call" | custom-call | flops 49999998976 | bytes 25165824 | tf_op jit(solution)/shard_map/attend/pallas_call | solution.py:295
  260.5 3.0 convolution_convert_fusion.1
  263.6 2.9 collective-permute-start.34
  269.0 4.0 add_convert_fusion
  273.9 3.4 collective-permute-start.35
  278.5 21.5 %qkv_back.1 = (bf16[768,2304]{1,0:T(8,128)(2,1)}, f32[1,2304]{1,0:T(1,128)}, f32[1024,768]{1,0:T(8,128)}, f32[1,768]{1,0:T(1,128)}, f32[1,768]{1,0:T(1,128)}) custom-call(bf16[1024,768]{1,0:T(8,128)(2,1)} %x_ref.5, bf16[1024,768]{1,0:T(8,128)(2,1)} %get-tuple-element.38.in_ref, f32[1,768]{1,0:T(1,128)} %reshape.507.gain_ref, bf16[768,2432]{1,0:T(8,128)(2,1)} %bitcast.281, ...), custom_call_target="tpu_custom_call" | custom-call | flops 7247757312 | bytes 31457280 | tf_op jit(solution)/shard_map/qkv_back/pallas_call | solution.py:534
  300.0 2.8 dynamic-slice_bitcast_fusion.2
  305.9 2.8 concatenate.15
  309.7 10.6 %collective-permute-start.22 = (f32[16,24,128]{2,1,0:T(8,128)S(1)}, f32[16,24,128]{2,1,0:T(8,128)S(1)}, u32[]{:S(2)}, u32[]{:S(2)}) collective-permute-start(f32[16,24,128]{2,1,0:T(8,128)S(1)} %dynamic-slice_bitcast_fusion.12), channel_id=1, source_target_pairs={{0,1},{1,0},{2,3},{3,2},{4,5},{5,4},{6,7},{7,6},{8,9},{9,8},{10,11... | collective-permute-start | bytes 589832 | tf_op jit(solution)/shard_map/ppermute | solution.py:51
  321.5 17.3 %collective-permute-start.36 = (bf16[1,48,768]{2,1,0:T(8,128)(2,1)S(1)}, bf16[1,48,768]{2,1,0:T(8,128)(2,1)S(1)}, u32[]{:S(2)}, u32[]{:S(2)}) collective-permute-start(bf16[1,48,768]{2,1,0:T(8,128)(2,1)S(1)} %get-tuple-element.107), channel_id=1, source_target_pairs={{0,8},{1,9},{2,10},{3,11},{4,12},{5,13},{6,14},{7,15},{8,16},{9,17... | collective-permute-start | bytes 221192 | tf_op jit(solution)/shard_map/ppermute | solution.py:51
  341.9 3.3 collective-permute-start.23
  345.6 2.2 collective-permute-done.23
  347.9 1.5 collective-permute-start.24
  349.4 2.0 collective-permute-start.39
  352.8 2.1 collective-permute-start.26
  354.9 2.4 collective-permute-start.27
  360.1 3.4 fusion.1
  363.7 1.5 collective-permute-start.41
  365.2 3.2 collective-permute-start.42
  370.2 2.1 collective-permute-start.47
  372.4 9.8 %collective-permute-done.41 = bf16[1,96,3072]{2,1,0:T(8,128)(2,1)S(1)} collective-permute-done((bf16[1,96,3072]{2,1,0:T(8,128)(2,1)S(1)}, bf16[1,96,3072]{2,1,0:T(8,128)(2,1)S(1)}, u32[]{:S(2)}, u32[]{:S(2)}) %collective-permute-start.41) | collective-permute-done | bytes 589856 | tf_op jit(solution)/shard_map/ppermute | solution.py:51
  382.2 23.8 %collective-permute-done.42 = bf16[1,96,3072]{2,1,0:T(8,128)(2,1)S(1)} collective-permute-done((bf16[1,96,3072]{2,1,0:T(8,128)(2,1)S(1)}, bf16[1,96,3072]{2,1,0:T(8,128)(2,1)S(1)}, u32[]{:S(2)}, u32[]{:S(2)}) %collective-permute-start.42) | collective-permute-done | bytes 589856 | tf_op jit(solution)/shard_map/ppermute | solution.py:51
  406.4 2.1 collective-permute-start.44
  408.5 1.9 fusion.2
  410.4 3.4 collective-permute-done.44
  414.0 2.1 collective-permute-start.45
  416.2 4.6 collective-permute-done.45
  421.9 2.1 collective-permute-start.48
  424.0 15.8 %collective-permute-done.29 = bf16[4,48,2304]{2,1,0:T(8,128)(2,1)S(1)} collective-permute-done((bf16[4,48,2304]{2,1,0:T(8,128)(2,1)S(1)}, bf16[4,48,2304]{2,1,0:T(8,128)(2,1)S(1)}, u32[]{:S(2)}, u32[]{:S(2)}) %collective-permute-start.29) | collective-permute-done | bytes 884768 | tf_op jit(solution)/shard_map/ppermute | solution.py:51
  440.1 13.1 %collective-permute-start.30 = (bf16[1,48,2304]{2,1,0:T(8,128)(2,1)S(1)}, bf16[1,48,2304]{2,1,0:T(8,128)(2,1)S(1)}, u32[]{:S(2)}, u32[]{:S(2)}) collective-permute-start(bf16[1,48,2304]{2,1,0:T(8,128)(2,1)S(1)} %get-tuple-element.88), channel_id=1, source_target_pairs={{0,8},{1,9},{2,10},{3,11},{4,12},{5,13},{6,14},{7,15},{8,16},{9,17... | collective-permute-start | bytes 663560 | tf_op jit(solution)/shard_map/ppermute | solution.py:51
  453.2 2.4 collective-permute-start.32
  455.8 7.8 %collective-permute-start.49 = (bf16[1,96,768]{2,1,0:T(8,128)(2,1)S(1)}, bf16[1,96,768]{2,1,0:T(8,128)(2,1)S(1)}, u32[]{:S(2)}, u32[]{:S(2)}) collective-permute-start(bf16[1,96,768]{2,1,0:T(8,128)(2,1)S(1)} %get-tuple-element.93), channel_id=1, source_target_pairs={{0,8},{1,9},{2,10},{3,11},{4,12},{5,13},{6,14},{7,15},{8,16},{9,17... | collective-permute-start | bytes 442376 | tf_op jit(solution)/shard_map/ppermute | solution.py:51
  463.6 2.4 collective-permute-start.51
  466.1 4.7 collective-permute-done.31
  470.9 2.8 collective-permute-start.33
  473.7 5.9 %collective-permute-done.50 = bf16[1,96,768]{2,1,0:T(8,128)(2,1)S(1)} collective-permute-done((bf16[1,96,768]{2,1,0:T(8,128)(2,1)S(1)}, bf16[1,96,768]{2,1,0:T(8,128)(2,1)S(1)}, u32[]{:S(2)}, u32[]{:S(2)}) %collective-permute-start.50) | collective-permute-done | bytes 147488 | tf_op jit(solution)/shard_map/ppermute | solution.py:51
  (234 shorter events, 68.7 us)
Async XLA Ops:
  0.6 37.8 %collective-permute-start.14 = (bf16[1,96,768]{2,1,0:T(8,128)(2,1)}, bf16[1,96,768]{2,1,0:T(8,128)(2,1)S(1)}, u32[]{:S(2)}, u32[]{:S(2)}) collective-permute-start(bf16[1,96,768]{2,1,0:T(8,128)(2,1)} %bitcast.305), channel_id=1, source_target_pairs={{0,8},{1,9},{2,10},{3,11},{4,12},{5,13},{6,14},{7,15},{8,16},{9,17... | collective-permute-start | bytes 442376 | tf_op jit(solution)/shard_map/ppermute | solution.py:51
  3.7 34.7 %collective-permute-start.15 = (bf16[1,96,768]{2,1,0:T(8,128)(2,1)}, bf16[1,96,768]{2,1,0:T(8,128)(2,1)S(1)}, u32[]{:S(2)}, u32[]{:S(2)}) collective-permute-start(bf16[1,96,768]{2,1,0:T(8,128)(2,1)} %bitcast.306), channel_id=1, source_target_pairs={{0,16},{1,17},{2,18},{3,19},{4,20},{5,21},{6,22},{7,23},{8,24},{9,... | collective-permute-start | bytes 442376 | tf_op jit(solution)/shard_map/ppermute | solution.py:51
  13.3 22.7 %collective-permute-start.1 = (bf16[1,24,2432]{2,1,0:T(8,128)(2,1)S(1)}, bf16[1,24,2432]{2,1,0:T(8,128)(2,1)S(1)}, u32[]{:S(2)}, u32[]{:S(2)}) collective-permute-start(bf16[1,24,2432]{2,1,0:T(8,128)(2,1)S(1)} %fusion.19), channel_id=1, source_target_pairs={{0,8},{1,9},{2,10},{3,11},{4,12},{5,13},{6,14},{7,15},{8,16},{9,17... | collective-permute-start | bytes 350216 | tf_op jit(solution)/shard_map/ppermute | solution.py:51
  13.5 23.2 %collective-permute-start.2 = (bf16[1,24,2432]{2,1,0:T(8,128)(2,1)S(1)}, bf16[1,24,2432]{2,1,0:T(8,128)(2,1)S(1)}, u32[]{:S(2)}, u32[]{:S(2)}) collective-permute-start(bf16[1,24,2432]{2,1,0:T(8,128)(2,1)S(1)} %fusion.19), channel_id=1, source_target_pairs={{0,16},{1,17},{2,18},{3,19},{4,20},{5,21},{6,22},{7,23},{8,24},{9,... | collective-permute-start | bytes 350216 | tf_op jit(solution)/shard_map/ppermute | solution.py:51
  20.0 3.9 collective-permute-start
  23.9 13.5 %collective-permute-start.3 = (bf16[1,24,2432]{2,1,0:T(8,128)(2,1)S(1)}, bf16[1,24,2432]{2,1,0:T(8,128)(2,1)S(1)}, u32[]{:S(2)}, u32[]{:S(2)}) collective-permute-start(bf16[1,24,2432]{2,1,0:T(8,128)(2,1)S(1)} %fusion.19), channel_id=1, source_target_pairs={{0,24},{1,25},{2,26},{3,27},{4,28},{5,29},{6,30},{7,31},{8,0},{9,1... | collective-permute-start | bytes 350216 | tf_op jit(solution)/shard_map/ppermute | solution.py:51
  36.0 6.9 %copy-start.7 = (bf16[24,3072]{1,0:T(8,128)(2,1)S(1)}, bf16[24,3072]{1,0:T(8,128)(2,1)}, u32[]{:S(2)}) copy-start(bf16[24,3072]{1,0:T(8,128)(2,1)} %param.26) | copy-start | bytes 442372
  36.0 6.9 %copy-start.9 = (bf16[24,768]{1,0:T(8,128)(2,1)S(1)}, bf16[24,768]{1,0:T(8,128)(2,1)}, u32[]{:S(2)}) copy-start(bf16[24,768]{1,0:T(8,128)(2,1)} %param.24) | copy-start | bytes 110596
  36.0 5.2 %collective-permute-start.16 = (bf16[1,96,768]{2,1,0:T(8,128)(2,1)S(1)}, bf16[1,96,768]{2,1,0:T(8,128)(2,1)S(1)}, u32[]{:S(2)}, u32[]{:S(2)}) collective-permute-start(bf16[1,96,768]{2,1,0:T(8,128)(2,1)S(1)} %bitcast.307), channel_id=1, source_target_pairs={{0,24},{1,25},{2,26},{3,27},{4,28},{5,29},{6,30},{7,31},{8,0},{9,1... | collective-permute-start | bytes 442376 | tf_op jit(solution)/shard_map/ppermute | solution.py:51
  36.7 6.2 %collective-permute-start.8 = (bf16[1,24,3840]{2,1,0:T(8,128)(2,1)S(1)}, bf16[1,24,3840]{2,1,0:T(8,128)(2,1)S(1)}, u32[]{:S(2)}, u32[]{:S(2)}) collective-permute-start(bf16[1,24,3840]{2,1,0:T(8,128)(2,1)S(1)} %maximum_bitcast_fusion.3), channel_id=1, source_target_pairs={{0,4},{1,5},{2,6},{3,7},{4,0},{5,1},{6,2},{7,3},{8,12},{9,13},{10,... | collective-permute-start | bytes 552968 | tf_op jit(solution)/shard_map/ppermute | solution.py:51
  37.8 13.7 %collective-permute-start.4 = (bf16[4,24,2432]{2,1,0:T(8,128)(2,1)S(1)}, bf16[4,24,2432]{2,1,0:T(8,128)(2,1)S(1)}, u32[]{:S(2)}, u32[]{:S(2)}) collective-permute-start(bf16[4,24,2432]{2,1,0:T(8,128)(2,1)S(1)} %maximum_bitcast_fusion.1), channel_id=1, source_target_pairs={{0,2},{1,3},{2,0},{3,1},{4,6},{5,7},{6,4},{7,5},{8,10},{9,11},{10,... | collective-permute-start | bytes 1400840 | tf_op jit(solution)/shard_map/ppermute | solution.py:51
  41.4 21.3 %collective-permute-start.17 = (bf16[4,96,768]{2,1,0:T(8,128)(2,1)S(1)}, bf16[4,96,768]{2,1,0:T(8,128)(2,1)S(1)}, u32[]{:S(2)}, u32[]{:S(2)}) collective-permute-start(bf16[4,96,768]{2,1,0:T(8,128)(2,1)S(1)} %maximum_bitcast_fusion), channel_id=1, source_target_pairs={{0,4},{1,5},{2,6},{3,7},{4,0},{5,1},{6,2},{7,3},{8,12},{9,13},{10,... | collective-permute-start | bytes 1769480 | tf_op jit(solution)/shard_map/ppermute | solution.py:51
  43.0 15.0 %collective-permute-start.9 = (bf16[2,24,3840]{2,1,0:T(8,128)(2,1)S(1)}, bf16[2,24,3840]{2,1,0:T(8,128)(2,1)S(1)}, u32[]{:S(2)}, u32[]{:S(2)}) collective-permute-start(bf16[2,24,3840]{2,1,0:T(8,128)(2,1)S(1)} %maximum_bitcast_fusion.2), channel_id=1, source_target_pairs={{0,2},{1,3},{2,0},{3,1},{4,6},{5,7},{6,4},{7,5},{8,10},{9,11},{10,... | collective-permute-start | bytes 1105928 | tf_op jit(solution)/shard_map/ppermute | solution.py:51
  51.7 24.0 %collective-permute-start.5 = (bf16[4,48,2432]{2,1,0:T(8,128)(2,1)S(1)}, bf16[4,48,2432]{2,1,0:T(8,128)(2,1)S(1)}, u32[]{:S(2)}, u32[]{:S(2)}) collective-permute-start(bf16[4,48,2432]{2,1,0:T(8,128)(2,1)S(1)} %bitcast.282), channel_id=1, source_target_pairs={{0,4},{1,5},{2,6},{3,7},{4,0},{5,1},{6,2},{7,3},{8,12},{9,13},{10,... | collective-permute-start | bytes 2801672 | tf_op jit(solution)/shard_map/ppermute | solution.py:51
  58.1 21.4 %collective-permute-start.10 = (bf16[1,96,3840]{2,1,0:T(8,128)(2,1)S(1)}, bf16[1,96,3840]{2,1,0:T(8,128)(2,1)S(1)}, u32[]{:S(2)}, u32[]{:S(2)}) collective-permute-start(bf16[1,96,3840]{2,1,0:T(8,128)(2,1)S(1)} %bitcast.285), channel_id=1, source_target_pairs={{0,8},{1,9},{2,10},{3,11},{4,12},{5,13},{6,14},{7,15},{8,16},{9,17... | collective-permute-start | bytes 2211848 | tf_op jit(solution)/shard_map/ppermute | solution.py:51
  59.4 49.4 %collective-permute-start.11 = (bf16[1,96,3840]{2,1,0:T(8,128)(2,1)S(1)}, bf16[1,96,3840]{2,1,0:T(8,128)(2,1)S(1)}, u32[]{:S(2)}, u32[]{:S(2)}) collective-permute-start(bf16[1,96,3840]{2,1,0:T(8,128)(2,1)S(1)} %bitcast.286), channel_id=1, source_target_pairs={{0,16},{1,17},{2,18},{3,19},{4,20},{5,21},{6,22},{7,23},{8,24},{9,... | collective-permute-start | bytes 2211848 | tf_op jit(solution)/shard_map/ppermute | solution.py:51
  61.4 47.4 %collective-permute-start.12 = (bf16[1,96,3840]{2,1,0:T(8,128)(2,1)S(1)}, bf16[1,96,3840]{2,1,0:T(8,128)(2,1)S(1)}, u32[]{:S(2)}, u32[]{:S(2)}) collective-permute-start(bf16[1,96,3840]{2,1,0:T(8,128)(2,1)S(1)} %bitcast.287), channel_id=1, source_target_pairs={{0,24},{1,25},{2,26},{3,27},{4,28},{5,29},{6,30},{7,31},{8,0},{9,1... | collective-permute-start | bytes 2211848 | tf_op jit(solution)/shard_map/ppermute | solution.py:51
  62.9 49.3 %collective-permute-start.18 = (bf16[8,96,768]{2,1,0:T(8,128)(2,1)S(1)}, bf16[8,96,768]{2,1,0:T(8,128)(2,1)S(1)}, u32[]{:S(2)}, u32[]{:S(2)}) collective-permute-start(bf16[8,96,768]{2,1,0:T(8,128)(2,1)S(1)} %bitcast.275), channel_id=1, source_target_pairs={{0,2},{1,3},{2,0},{3,1},{4,6},{5,7},{6,4},{7,5},{8,10},{9,11},{10,... | collective-permute-start | bytes 3538952 | tf_op jit(solution)/shard_map/ppermute | solution.py:51
  76.3 37.9 %collective-permute-start.6 = (bf16[16,24,2432]{2,1,0:T(8,128)(2,1)S(1)}, bf16[16,24,2432]{2,1,0:T(8,128)(2,1)S(1)}, u32[]{:S(2)}, u32[]{:S(2)}) collective-permute-start(bf16[16,24,2432]{2,1,0:T(8,128)(2,1)S(1)} %bitcast.262), channel_id=1, source_target_pairs={{0,1},{1,0},{2,3},{3,2},{4,5},{5,4},{6,7},{7,6},{8,9},{9,8},{10,11... | collective-permute-start | bytes 5603336 | tf_op jit(solution)/shard_map/ppermute | solution.py:51
  109.6 32.6 %collective-permute-start.13 = (bf16[16,24,3840]{2,1,0:T(8,128)(2,1)S(1)}, bf16[16,24,3840]{2,1,0:T(8,128)(2,1)}, u32[]{:S(2)}, u32[]{:S(2)}) collective-permute-start(bf16[16,24,3840]{2,1,0:T(8,128)(2,1)S(1)} %bitcast.256), channel_id=1, source_target_pairs={{0,1},{1,0},{2,3},{3,2},{4,5},{5,4},{6,7},{7,6},{8,9},{9,8},{10,11... | collective-permute-start | bytes 8847368 | tf_op jit(solution)/shard_map/ppermute | solution.py:51
  114.2 34.2 %collective-permute-start.19 = (bf16[16,96,768]{2,1,0:T(8,128)(2,1)}, bf16[16,96,768]{2,1,0:T(8,128)(2,1)}, u32[]{:S(2)}, u32[]{:S(2)}) collective-permute-start(bf16[16,96,768]{2,1,0:T(8,128)(2,1)} %bitcast.60), channel_id=1, source_target_pairs={{0,1},{1,0},{2,3},{3,2},{4,5},{5,4},{6,7},{7,6},{8,9},{9,8},{10,11... | collective-permute-start | bytes 7077896 | tf_op jit(solution)/shard_map/ppermute | solution.py:51
  138.1 67.7 %collective-permute-start.7 = (bf16[512,1536]{1,0:T(8,128)(2,1)}, bf16[512,1536]{1,0:T(8,128)(2,1)}, u32[]{:S(2)}, u32[]{:S(2)}) collective-permute-start(bf16[512,1536]{1,0:T(8,128)(2,1)} %slice.79), channel_id=1, source_target_pairs={{0,1},{1,2},{2,3},{3,4},{4,5},{5,6},{6,7},{7,8},{8,9},{9,10},{10,1... | collective-permute-start | bytes 4718600 | tf_op jit(solution)/shard_map/ppermute | solution.py:122
  199.1 170.3 %collective-permute-start.46 = (bf16[16,96,768]{2,1,0:T(8,128)(2,1)}, bf16[16,96,768]{2,1,0:T(8,128)(2,1)S(1)}, u32[]{:S(2)}, u32[]{:S(2)}) collective-permute-start(bf16[16,96,768]{2,1,0:T(8,128)(2,1)} %dynamic-slice_bitcast_fusion), channel_id=1, source_target_pairs={{0,1},{1,0},{2,3},{3,2},{4,5},{5,4},{6,7},{7,6},{8,9},{9,8},{10,11... | collective-permute-start | bytes 7077896 | tf_op jit(solution)/shard_map/ppermute | solution.py:51
  201.2 159.0 %collective-permute-start.40 = (bf16[16,24,3072]{2,1,0:T(8,128)(2,1)}, bf16[16,24,3072]{2,1,0:T(8,128)(2,1)}, u32[]{:S(2)}, u32[]{:S(2)}) collective-permute-start(bf16[16,24,3072]{2,1,0:T(8,128)(2,1)} %dynamic-slice_bitcast_fusion.1), channel_id=1, source_target_pairs={{0,1},{1,0},{2,3},{3,2},{4,5},{5,4},{6,7},{7,6},{8,9},{9,8},{10,11... | collective-permute-start | bytes 7077896 | tf_op jit(solution)/shard_map/ppermute | solution.py:51
  205.8 54.7 %copy-start.19 = (bf16[1024,768]{1,0:T(8,128)(2,1)S(1)}, bf16[1024,768]{1,0:T(8,128)(2,1)}, u32[]{:S(2)}) copy-start(bf16[1024,768]{1,0:T(8,128)(2,1)} %cot_ref.1) | copy-start | bytes 4718596
  260.4 6.0 %copy-start.24 = (bf16[512,768]{1,0:T(8,128)(2,1)S(1)}, bf16[512,768]{1,0:T(8,128)(2,1)}, u32[]{:S(2)}) copy-start(bf16[512,768]{1,0:T(8,128)(2,1)} %get-tuple-element.42) | copy-start | bytes 2359300
  260.4 7.3 %copy-start.22 = (bf16[512,768]{1,0:T(8,128)(2,1)S(1)}, bf16[512,768]{1,0:T(8,128)(2,1)}, u32[]{:S(2)}) copy-start(bf16[512,768]{1,0:T(8,128)(2,1)} %get-tuple-element.43) | copy-start | bytes 2359300
  260.5 8.6 %copy-start.20 = (bf16[1024,768]{1,0:T(8,128)(2,1)S(1)}, bf16[1024,768]{1,0:T(8,128)(2,1)}, u32[]{:S(2)}) copy-start(bf16[1024,768]{1,0:T(8,128)(2,1)} %x_ref.5) | copy-start | bytes 4718596
  260.5 8.6 %copy-start.25 = (f32[1024,768]{1,0:T(8,128)S(1)}, f32[1024,768]{1,0:T(8,128)}, u32[]{:S(2)}) copy-start(f32[1024,768]{1,0:T(8,128)} %get-tuple-element.37) | copy-start | bytes 9437188
  260.5 8.6 %copy-start.26 = (bf16[1024,768]{1,0:T(8,128)(2,1)S(1)}, bf16[1024,768]{1,0:T(8,128)(2,1)}, u32[]{:S(2)}) copy-start(bf16[1024,768]{1,0:T(8,128)(2,1)} %get-tuple-element.36) | copy-start | bytes 4718596
  263.6 9.5 %collective-permute-start.34 = (bf16[16,24,768]{2,1,0:T(8,128)(2,1)S(1)}, bf16[16,24,768]{2,1,0:T(8,128)(2,1)S(1)}, u32[]{:S(2)}, u32[]{:S(2)}) collective-permute-start(bf16[16,24,768]{2,1,0:T(8,128)(2,1)S(1)} %dynamic-slice_bitcast_fusion.9), channel_id=1, source_target_pairs={{0,1},{1,0},{2,3},{3,2},{4,5},{5,4},{6,7},{7,6},{8,9},{9,8},{10,11... | collective-permute-start | bytes 1769480 | tf_op jit(solution)/shard_map/ppermute | solution.py:51
  266.4 10.9 %collective-permute-start.20 = (bf16[512,768]{1,0:T(8,128)(2,1)S(1)}, bf16[512,768]{1,0:T(8,128)(2,1)S(1)}, u32[]{:S(2)}, u32[]{:S(2)}) collective-permute-start(bf16[512,768]{1,0:T(8,128)(2,1)S(1)} %copy-done.24), channel_id=1, source_target_pairs={{1,0},{2,1},{3,2},{4,3},{5,4},{6,5},{7,6},{8,7},{9,8},{10,9},{11,1... | collective-permute-start | bytes 2359304 | tf_op jit(solution)/shard_map/ppermute | solution.py:122
  267.7 9.6 %collective-permute-start.21 = (bf16[512,768]{1,0:T(8,128)(2,1)S(1)}, bf16[512,768]{1,0:T(8,128)(2,1)S(1)}, u32[]{:S(2)}, u32[]{:S(2)}) collective-permute-start(bf16[512,768]{1,0:T(8,128)(2,1)S(1)} %copy-done.22), channel_id=1, source_target_pairs={{1,0},{2,1},{3,2},{4,3},{5,4},{6,5},{7,6},{8,7},{9,8},{10,9},{11,1... | collective-permute-start | bytes 2359304 | tf_op jit(solution)/shard_map/ppermute | solution.py:122
  273.9 46.4 %collective-permute-start.35 = (bf16[4,48,768]{2,1,0:T(8,128)(2,1)}, bf16[4,48,768]{2,1,0:T(8,128)(2,1)}, u32[]{:S(2)}, u32[]{:S(2)}) collective-permute-start(bf16[4,48,768]{2,1,0:T(8,128)(2,1)} %dynamic-slice_bitcast_fusion.11), channel_id=1, source_target_pairs={{0,4},{1,5},{2,6},{3,7},{4,0},{5,1},{6,2},{7,3},{8,12},{9,13},{10,... | collective-permute-start | bytes 884744 | tf_op jit(solution)/shard_map/ppermute | solution.py:51
  309.7 30.3 %collective-permute-start.22 = (f32[16,24,128]{2,1,0:T(8,128)S(1)}, f32[16,24,128]{2,1,0:T(8,128)S(1)}, u32[]{:S(2)}, u32[]{:S(2)}) collective-permute-start(f32[16,24,128]{2,1,0:T(8,128)S(1)} %dynamic-slice_bitcast_fusion.12), channel_id=1, source_target_pairs={{0,1},{1,0},{2,3},{3,2},{4,5},{5,4},{6,7},{7,6},{8,9},{9,8},{10,11... | collective-permute-start | bytes 589832 | tf_op jit(solution)/shard_map/ppermute | solution.py:51
  320.3 49.1 %slice-start = ((s8[4718592]{0:T(1024)(128)(4,1)}), s8[524288]{0:T(1024)(128)(4,1)S(1)}, s32[]{:S(2)}) async-start(s8[4718592]{0:T(1024)(128)(4,1)} %bitcast.270), calls=%async_computation | async-start | bytes 1048576
  321.5 20.4 %collective-permute-start.36 = (bf16[1,48,768]{2,1,0:T(8,128)(2,1)S(1)}, bf16[1,48,768]{2,1,0:T(8,128)(2,1)S(1)}, u32[]{:S(2)}, u32[]{:S(2)}) collective-permute-start(bf16[1,48,768]{2,1,0:T(8,128)(2,1)S(1)} %get-tuple-element.107), channel_id=1, source_target_pairs={{0,8},{1,9},{2,10},{3,11},{4,12},{5,13},{6,14},{7,15},{8,16},{9,17... | collective-permute-start | bytes 221192 | tf_op jit(solution)/shard_map/ppermute | solution.py:51
  338.8 6.4 %collective-permute-start.37 = (bf16[1,48,768]{2,1,0:T(8,128)(2,1)S(1)}, bf16[1,48,768]{2,1,0:T(8,128)(2,1)S(1)}, u32[]{:S(2)}, u32[]{:S(2)}) collective-permute-start(bf16[1,48,768]{2,1,0:T(8,128)(2,1)S(1)} %get-tuple-element.109), channel_id=1, source_target_pairs={{0,16},{1,17},{2,18},{3,19},{4,20},{5,21},{6,22},{7,23},{8,24},{9,... | collective-permute-start | bytes 221192 | tf_op jit(solution)/shard_map/ppermute | solution.py:51
  340.0 5.6 %collective-permute-start.38 = (bf16[1,48,768]{2,1,0:T(8,128)(2,1)S(1)}, bf16[1,48,768]{2,1,0:T(8,128)(2,1)S(1)}, u32[]{:S(2)}, u32[]{:S(2)}) collective-permute-start(bf16[1,48,768]{2,1,0:T(8,128)(2,1)S(1)} %get-tuple-element.108), channel_id=1, source_target_pairs={{0,24},{1,25},{2,26},{3,27},{4,28},{5,29},{6,30},{7,31},{8,0},{9,1... | collective-permute-start | bytes 221192 | tf_op jit(solution)/shard_map/ppermute | solution.py:51
  341.9 5.9 %collective-permute-start.23 = (f32[8,24,128]{2,1,0:T(8,128)S(1)}, f32[8,24,128]{2,1,0:T(8,128)S(1)}, u32[]{:S(2)}, u32[]{:S(2)}) collective-permute-start(f32[8,24,128]{2,1,0:T(8,128)S(1)} %dynamic-slice_bitcast_fusion.14), channel_id=1, source_target_pairs={{0,2},{1,3},{2,0},{3,1},{4,6},{5,7},{6,4},{7,5},{8,10},{9,11},{10,... | collective-permute-start | bytes 294920 | tf_op jit(solution)/shard_map/ppermute | solution.py:51
  347.9 4.2 collective-permute-start.24
  349.4 5.5 %collective-permute-start.39 = (bf16[1,24,768]{2,1,0:T(8,128)(2,1)S(1)}, bf16[1,24,768]{2,1,0:T(8,128)(2,1)S(1)}, u32[]{:S(2)}, u32[]{:S(2)}) collective-permute-start(bf16[1,24,768]{2,1,0:T(8,128)(2,1)S(1)} %dynamic-slice_bitcast_fusion.16), channel_id=1, source_target_pairs={{0,2},{1,3},{2,0},{3,1},{4,6},{5,7},{6,4},{7,5},{8,10},{9,11},{10,... | collective-permute-start | bytes 110600 | tf_op jit(solution)/shard_map/ppermute | solution.py:51
  352.0 5.9 %collective-permute-start.25 = (f32[1,24,128]{2,1,0:T(8,128)S(1)}, f32[1,24,128]{2,1,0:T(8,128)S(1)}, u32[]{:S(2)}, u32[]{:S(2)}) collective-permute-start(f32[1,24,128]{2,1,0:T(8,128)S(1)} %get-tuple-element.110), channel_id=1, source_target_pairs={{0,8},{1,9},{2,10},{3,11},{4,12},{5,13},{6,14},{7,15},{8,16},{9,17... | collective-permute-start | bytes 36872 | tf_op jit(solution)/shard_map/ppermute | solution.py:51
  352.8 5.2 %collective-permute-start.26 = (f32[1,24,128]{2,1,0:T(8,128)S(1)}, f32[1,24,128]{2,1,0:T(8,128)S(1)}, u32[]{:S(2)}, u32[]{:S(2)}) collective-permute-start(f32[1,24,128]{2,1,0:T(8,128)S(1)} %get-tuple-element.112), channel_id=1, source_target_pairs={{0,16},{1,17},{2,18},{3,19},{4,20},{5,21},{6,22},{7,23},{8,24},{9,... | collective-permute-start | bytes 36872 | tf_op jit(solution)/shard_map/ppermute | solution.py:51
  354.9 3.8 collective-permute-start.27
  358.0 50.6 %collective-permute-start.28 = (bf16[16,24,2304]{2,1,0:T(8,128)(2,1)}, bf16[16,24,2304]{2,1,0:T(8,128)(2,1)}, u32[]{:S(2)}, u32[]{:S(2)}) collective-permute-start(bf16[16,24,2304]{2,1,0:T(8,128)(2,1)} %dynamic-slice_bitcast_fusion.2), channel_id=1, source_target_pairs={{0,1},{1,0},{2,3},{3,2},{4,5},{5,4},{6,7},{7,6},{8,9},{9,8},{10,11... | collective-permute-start | bytes 5308424 | tf_op jit(solution)/shard_map/ppermute | solution.py:51
  360.1 9.3 %slice-start.1 = ((s8[4718592]{0:T(1024)(128)(4,1)}), s8[4194304]{0:T(1024)(128)(4,1)S(1)}, s32[]{:S(2)}) async-start(s8[4718592]{0:T(1024)(128)(4,1)} %bitcast.270), calls=%async_computation.1 | async-start | bytes 8388608
  363.7 18.5 %collective-permute-start.41 = (bf16[1,96,3072]{2,1,0:T(8,128)(2,1)S(1)}, bf16[1,96,3072]{2,1,0:T(8,128)(2,1)S(1)}, u32[]{:S(2)}, u32[]{:S(2)}) collective-permute-start(bf16[1,96,3072]{2,1,0:T(8,128)(2,1)S(1)} %get-tuple-element.77), channel_id=1, source_target_pairs={{0,8},{1,9},{2,10},{3,11},{4,12},{5,13},{6,14},{7,15},{8,16},{9,17... | collective-permute-start | bytes 1769480 | tf_op jit(solution)/shard_map/ppermute | solution.py:51
  365.2 40.8 %collective-permute-start.42 = (bf16[1,96,3072]{2,1,0:T(8,128)(2,1)S(1)}, bf16[1,96,3072]{2,1,0:T(8,128)(2,1)S(1)}, u32[]{:S(2)}, u32[]{:S(2)}) collective-permute-start(bf16[1,96,3072]{2,1,0:T(8,128)(2,1)S(1)} %get-tuple-element.79), channel_id=1, source_target_pairs={{0,16},{1,17},{2,18},{3,19},{4,20},{5,21},{6,22},{7,23},{8,24},{9,... | collective-permute-start | bytes 1769480 | tf_op jit(solution)/shard_map/ppermute | solution.py:51
  368.4 37.6 %collective-permute-start.43 = (bf16[1,96,3072]{2,1,0:T(8,128)(2,1)S(1)}, bf16[1,96,3072]{2,1,0:T(8,128)(2,1)S(1)}, u32[]{:S(2)}, u32[]{:S(2)}) collective-permute-start(bf16[1,96,3072]{2,1,0:T(8,128)(2,1)S(1)} %get-tuple-element.78), channel_id=1, source_target_pairs={{0,24},{1,25},{2,26},{3,27},{4,28},{5,29},{6,30},{7,31},{8,0},{9,1... | collective-permute-start | bytes 1769480 | tf_op jit(solution)/shard_map/ppermute | solution.py:51
  369.4 111.7 %copy-start.17 = (f32[24]{0:T(128)}, f32[24]{0:T(128)S(1)}, u32[]{:S(2)}) copy-start(f32[24]{0:T(128)S(1)} %get-tuple-element.152) | copy-start | bytes 292
  370.2 38.3 %copy-start.3 = (bf16[768,2304]{1,0:T(8,128)(2,1)S(1)}, bf16[768,2304]{1,0:T(8,128)(2,1)}, u32[]{:S(2)}) copy-start(bf16[768,2304]{1,0:T(8,128)(2,1)} %get-tuple-element.53) | copy-start | bytes 10616836
  370.2 51.3 %collective-permute-start.47 = (bf16[8,96,768]{2,1,0:T(8,128)(2,1)S(1)}, bf16[8,96,768]{2,1,0:T(8,128)(2,1)S(1)}, u32[]{:S(2)}, u32[]{:S(2)}) collective-permute-start(bf16[8,96,768]{2,1,0:T(8,128)(2,1)S(1)} %dynamic-slice_bitcast_fusion.3), channel_id=1, source_target_pairs={{0,2},{1,3},{2,0},{3,1},{4,6},{5,7},{6,4},{7,5},{8,10},{9,11},{10,... | collective-permute-start | bytes 3538952 | tf_op jit(solution)/shard_map/ppermute | solution.py:51
  406.4 7.4 %collective-permute-start.44 = (bf16[2,24,3072]{2,1,0:T(8,128)(2,1)S(1)}, bf16[2,24,3072]{2,1,0:T(8,128)(2,1)S(1)}, u32[]{:S(2)}, u32[]{:S(2)}) collective-permute-start(bf16[2,24,3072]{2,1,0:T(8,128)(2,1)S(1)} %dynamic-slice_bitcast_fusion.10), channel_id=1, source_target_pairs={{0,2},{1,3},{2,0},{3,1},{4,6},{5,7},{6,4},{7,5},{8,10},{9,11},{10,... | collective-permute-start | bytes 884744 | tf_op jit(solution)/shard_map/ppermute | solution.py:51
  414.0 6.9 %collective-permute-start.45 = (bf16[1,24,3072]{2,1,0:T(8,128)(2,1)S(1)}, bf16[1,24,3072]{2,1,0:T(8,128)(2,1)S(1)}, u32[]{:S(2)}, u32[]{:S(2)}) collective-permute-start(bf16[1,24,3072]{2,1,0:T(8,128)(2,1)S(1)} %constant_dynamic-slice_fusion.3), channel_id=1, source_target_pairs={{0,4},{1,5},{2,6},{3,7},{4,0},{5,1},{6,2},{7,3},{8,12},{9,13},{10,... | collective-permute-start | bytes 442376 | tf_op jit(solution)/shard_map/ppermute | solution.py:51
  416.1 23.7 %collective-permute-start.29 = (bf16[4,48,2304]{2,1,0:T(8,128)(2,1)S(1)}, bf16[4,48,2304]{2,1,0:T(8,128)(2,1)S(1)}, u32[]{:S(2)}, u32[]{:S(2)}) collective-permute-start(bf16[4,48,2304]{2,1,0:T(8,128)(2,1)S(1)} %dynamic-slice_bitcast_fusion.4), channel_id=1, source_target_pairs={{0,4},{1,5},{2,6},{3,7},{4,0},{5,1},{6,2},{7,3},{8,12},{9,13},{10,... | collective-permute-start | bytes 2654216 | tf_op jit(solution)/shard_map/ppermute | solution.py:51
  421.9 33.7 %collective-permute-start.48 = (bf16[4,96,768]{2,1,0:T(8,128)(2,1)S(1)}, bf16[4,96,768]{2,1,0:T(8,128)(2,1)S(1)}, u32[]{:S(2)}, u32[]{:S(2)}) collective-permute-start(bf16[4,96,768]{2,1,0:T(8,128)(2,1)S(1)} %dynamic-slice_bitcast_fusion.5), channel_id=1, source_target_pairs={{0,4},{1,5},{2,6},{3,7},{4,0},{5,1},{6,2},{7,3},{8,12},{9,13},{10,... | collective-permute-start | bytes 1769480 | tf_op jit(solution)/shard_map/ppermute | solution.py:51
  440.1 23.6 %collective-permute-start.30 = (bf16[1,48,2304]{2,1,0:T(8,128)(2,1)S(1)}, bf16[1,48,2304]{2,1,0:T(8,128)(2,1)S(1)}, u32[]{:S(2)}, u32[]{:S(2)}) collective-permute-start(bf16[1,48,2304]{2,1,0:T(8,128)(2,1)S(1)} %get-tuple-element.88), channel_id=1, source_target_pairs={{0,8},{1,9},{2,10},{3,11},{4,12},{5,13},{6,14},{7,15},{8,16},{9,17... | collective-permute-start | bytes 663560 | tf_op jit(solution)/shard_map/ppermute | solution.py:51
  453.2 17.5 %collective-permute-start.31 = (bf16[1,48,2304]{2,1,0:T(8,128)(2,1)S(1)}, bf16[1,48,2304]{2,1,0:T(8,128)(2,1)S(1)}, u32[]{:S(2)}, u32[]{:S(2)}) collective-permute-start(bf16[1,48,2304]{2,1,0:T(8,128)(2,1)S(1)} %get-tuple-element.90), channel_id=1, source_target_pairs={{0,16},{1,17},{2,18},{3,19},{4,20},{5,21},{6,22},{7,23},{8,24},{9,... | collective-permute-start | bytes 663560 | tf_op jit(solution)/shard_map/ppermute | solution.py:51
  453.2 17.5 %collective-permute-start.32 = (bf16[1,48,2304]{2,1,0:T(8,128)(2,1)S(1)}, bf16[1,48,2304]{2,1,0:T(8,128)(2,1)S(1)}, u32[]{:S(2)}, u32[]{:S(2)}) collective-permute-start(bf16[1,48,2304]{2,1,0:T(8,128)(2,1)S(1)} %get-tuple-element.89), channel_id=1, source_target_pairs={{0,24},{1,25},{2,26},{3,27},{4,28},{5,29},{6,30},{7,31},{8,0},{9,1... | collective-permute-start | bytes 663560 | tf_op jit(solution)/shard_map/ppermute | solution.py:51
  455.8 17.8 %collective-permute-start.49 = (bf16[1,96,768]{2,1,0:T(8,128)(2,1)S(1)}, bf16[1,96,768]{2,1,0:T(8,128)(2,1)S(1)}, u32[]{:S(2)}, u32[]{:S(2)}) collective-permute-start(bf16[1,96,768]{2,1,0:T(8,128)(2,1)S(1)} %get-tuple-element.93), channel_id=1, source_target_pairs={{0,8},{1,9},{2,10},{3,11},{4,12},{5,13},{6,14},{7,15},{8,16},{9,17... | collective-permute-start | bytes 442376 | tf_op jit(solution)/shard_map/ppermute | solution.py:51
  463.6 16.0 %collective-permute-start.50 = (bf16[1,96,768]{2,1,0:T(8,128)(2,1)S(1)}, bf16[1,96,768]{2,1,0:T(8,128)(2,1)S(1)}, u32[]{:S(2)}, u32[]{:S(2)}) collective-permute-start(bf16[1,96,768]{2,1,0:T(8,128)(2,1)S(1)} %get-tuple-element.95), channel_id=1, source_target_pairs={{0,16},{1,17},{2,18},{3,19},{4,20},{5,21},{6,22},{7,23},{8,24},{9,... | collective-permute-start | bytes 442376 | tf_op jit(solution)/shard_map/ppermute | solution.py:51
  463.6 16.0 %collective-permute-start.51 = (bf16[1,96,768]{2,1,0:T(8,128)(2,1)S(1)}, bf16[1,96,768]{2,1,0:T(8,128)(2,1)S(1)}, u32[]{:S(2)}, u32[]{:S(2)}) collective-permute-start(bf16[1,96,768]{2,1,0:T(8,128)(2,1)S(1)} %get-tuple-element.94), channel_id=1, source_target_pairs={{0,24},{1,25},{2,26},{3,27},{4,28},{5,29},{6,30},{7,31},{8,0},{9,1... | collective-permute-start | bytes 442376 | tf_op jit(solution)/shard_map/ppermute | solution.py:51
  470.9 9.5 %collective-permute-start.33 = (bf16[1,24,2304]{2,1,0:T(8,128)(2,1)S(1)}, bf16[1,24,2304]{2,1,0:T(8,128)(2,1)S(1)}, u32[]{:S(2)}, u32[]{:S(2)}) collective-permute-start(bf16[1,24,2304]{2,1,0:T(8,128)(2,1)S(1)} %dynamic-slice_bitcast_fusion.13), channel_id=1, source_target_pairs={{0,2},{1,3},{2,0},{3,1},{4,6},{5,7},{6,4},{7,5},{8,10},{9,11},{10,... | collective-permute-start | bytes 331784 | tf_op jit(solution)/shard_map/ppermute | solution.py:51
  (17 other events, 49.6 us)

commit v3 on v2

--- a/solution.py
+++ b/solution.py
@@ -64,56 +64,77 @@
     return jnp.stack(slots, axis=1)
 
 
-def gather(value, order):
-    sizes, strides = split_axis(lax.axis_size(AXIS))
-    rows, width = value.shape
-    held = [1, 1, 1, 1]
-    me = lax.axis_index(AXIS)
-    for dim in order:
-        size = sizes[dim]
-        digit = me // strides[dim] % size
-        outer = 1
-        inner = rows
+class Gather:
+    def __init__(self, value, order):
+        self.sizes, self.strides = split_axis(lax.axis_size(AXIS))
+        self.value, self.order = value, list(order)
+        self.rows, self.width = value.shape
+        self.held = [1, 1, 1, 1]
+
+    def step(self):
+        dim = self.order.pop(0)
+        size, stride = self.sizes[dim], self.strides[dim]
+        digit = lax.axis_index(AXIS) // stride % size
+        outer, inner = 1, self.rows
         for d in range(4):
             if d < dim:
-                outer *= held[d]
+                outer *= self.held[d]
             if d > dim:
-                inner *= held[d]
-        piece = value.reshape(outer, inner, width)
-        pieces = [piece] + [shifted(piece, size, strides[dim], s) for s in range(1, size)]
-        value = place(pieces, digit)
-        held[dim] = size
-    return value.reshape(lax.axis_size(AXIS) * rows, width)
-
-
-def scatter(value, order):
-    sizes, strides = split_axis(lax.axis_size(AXIS))
-    width = value.shape[1]
-    rows = value.shape[0] // lax.axis_size(AXIS)
-    held = list(sizes)
-    me = lax.axis_index(AXIS)
-    kind = value.dtype
-    for dim in order:
-        size = sizes[dim]
-        digit = me // strides[dim] % size
-        outer = 1
-        inner = rows
+                inner *= self.held[d]
+        piece = self.value.reshape(outer, inner, self.width)
+        pieces = [piece] + [shifted(piece, size, stride, s) for s in range(1, size)]
+        self.value = place(pieces, digit)
+        self.held[dim] = size
+
+    def whole(self):
+        return self.value.reshape(lax.axis_size(AXIS) * self.rows, self.width)
+
+
+class Scatter:
+    def __init__(self, value, order):
+        self.sizes, self.strides = split_axis(lax.axis_size(AXIS))
+        self.value, self.order, self.kind = value, list(order), value.dtype
+        self.rows = value.shape[0] // lax.axis_size(AXIS)
+        self.held = list(self.sizes)
+
+    def step(self):
+        dim = self.order.pop(0)
+        size, stride = self.sizes[dim], self.strides[dim]
+        digit = lax.axis_index(AXIS) // stride % size
+        outer, inner = 1, self.rows
         for d in range(4):
             if d < dim:
-                outer *= held[d]
+                outer *= self.held[d]
             if d > dim:
-                inner *= held[d]
-        parts = value.reshape(outer, size, inner, width)
+                inner *= self.held[d]
+        parts = self.value.reshape(outer, size, inner, self.value.shape[-1])
 
         def part(at):
             return lax.dynamic_index_in_dim(parts, at, 1, keepdims=False)
 
         total = part(digit).astype(F32)
         for s in range(1, size):
-            total = total + shifted(part((digit + s) % size), size, strides[dim], s).astype(F32)
-        held[dim] = 1
-        value = total if dim == order[-1] else total.astype(kind)
-    return value.reshape(rows, width)
+            total = total + shifted(part((digit + s) % size), size, stride, s).astype(F32)
+        self.held[dim] = 1
+        self.value = total.astype(self.kind) if self.order else total
+        return self.value
+
+    def rest(self):
+        while self.order:
+            self.step()
+        return self.value.reshape(self.rows, -1)
+
+
+def together(*chains):
+    values = lax.optimization_barrier(tuple(c.value for c in chains))
+    for chain, value in zip(chains, values):
+        chain.value = value
+
+
+def behind(value, *chains):
+    values = lax.optimization_barrier((value, *[c.value for c in chains]))
+    for chain, held in zip(chains, values[1:]):
+        chain.value = held
 
 
 def from_behind(value, steps):
@@ -144,13 +165,14 @@
     return values * cosine + sign * (back + ahead)
 
 
-def qkv_body(x_ref, gain_ref, shift_ref, w_ref, b_ref, table_ref, out_ref, in_ref):
+def qkv_body(cut, x_ref, gain_ref, shift_ref, w_ref, v_ref, b_ref, table_ref, out_ref, in_ref):
     width = x_ref.shape[1]
     normal, _ = normalize(x_ref[...].astype(F32))
     rows_in = (normal * gain_ref[...] + shift_ref[...]).astype(BF16)
     in_ref[...] = rows_in
     for j in range(0, out_ref.shape[1], 256):
-        mixed = mm(rows_in, w_ref[:, j : j + 256]) + b_ref[:, j : j + 256]
+        tile = w_ref[:, j : j + 256] if j < cut else v_ref[:, j - cut : j - cut + 256]
+        mixed = mm(rows_in, tile) + b_ref[:, j : j + 256]
         if j < 2 * width:
             for c in (0, 128):
                 out_ref[:, j + c : j + c + 128] = turn(
@@ -160,18 +182,19 @@
             out_ref[:, j : j + 256] = mixed.astype(BF16)
 
 
-def project(tokens, gain, shift, weight, bias, table):
+def project(tokens, gain, shift, weight, weight_more, bias, table):
     rows, width = tokens.shape
     total = 3 * width
     whole = lambda i: (0, 0)
     return pl.pallas_call(
-        qkv_body,
+        functools.partial(qkv_body, weight.shape[1]),
         grid=(rows // BLOCK,),
         in_specs=[
             pl.BlockSpec((BLOCK, width), lambda i: (i, 0)),
             pl.BlockSpec((1, width), whole),
             pl.BlockSpec((1, width), whole),
             pl.BlockSpec(weight.shape, whole),
+            pl.BlockSpec(weight_more.shape, whole),
             pl.BlockSpec((1, total), whole),
             pl.BlockSpec((3, BLOCK, 128), lambda i: (0, i, 0)),
         ],
@@ -188,11 +211,12 @@
             flops=2 * rows * width * total, transcendentals=0, bytes_accessed=16 << 20
         ),
         name="qkv_project",
-    )(tokens, gain, shift, weight, bias, table)
+    )(tokens, gain, shift, weight, weight_more, bias, table)
 
 
 def attend_body(
     prior,
+    extra,
     first_ref,
     q_ref,
     k_ref,
@@ -202,17 +226,9 @@
     dc_ref,
     low_ref,
     table_ref,
-    ctx_ref,
-    dq_ref,
-    dk_ref,
-    dv_ref,
-    pdk_ref,
-    pdv_ref,
-    keys,
-    vals,
-    dk_sum,
-    dv_sum,
+    *refs,
 ):
+    ctx_ref, dq_ref, dk_ref, dv_ref, pdk_ref, pdv_ref, keys, vals, dk_sum, dv_sum = refs[extra:]
     block = pl.program_id(1)
     lead = prior // BLOCK
 
@@ -286,17 +302,18 @@
         dv_ref[...] = dv_sum[prior:]
 
 
-def attend(first, qkv, before, d_context, low, table):
+def attend(first, qkv, before, d_context, low, table, begin, count, made=(), after=()):
     rows, width = d_context.shape
     prior = before.shape[0]
     pairs = width // 128
-    wide = lambda off: (lambda p, i, f: (0, off + p))
-    tile = lambda p, i, f: (i, p)
+    wide = lambda off: (lambda p, i, f: (0, off + begin + p))
+    tile = lambda p, i, f: (i, begin + p)
+    extra = (*made, *after)
     return pl.pallas_call(
-        functools.partial(attend_body, prior),
+        functools.partial(attend_body, prior, len(extra)),
         grid_spec=pltpu.PrefetchScalarGridSpec(
             num_scalar_prefetch=1,
-            grid=(pairs, rows // BLOCK),
+            grid=(count, rows // BLOCK),
             in_specs=[
                 pl.BlockSpec((BLOCK, 128), tile),
                 pl.BlockSpec((rows, 128), wide(pairs)),
@@ -306,14 +323,15 @@
                 pl.BlockSpec((BLOCK, 128), tile),
                 pl.BlockSpec((BLOCK, 1), lambda p, i, f: (i, 0)),
                 pl.BlockSpec((3, BLOCK, 128), lambda p, i, f: (0, i, 0)),
+                *[pl.BlockSpec(memory_space=pl.ANY) for _ in extra],
             ],
             out_specs=[
                 pl.BlockSpec((BLOCK, 128), tile),
                 pl.BlockSpec((BLOCK, 128), tile),
                 pl.BlockSpec((rows, 128), wide(0)),
                 pl.BlockSpec((rows, 128), wide(0)),
-                pl.BlockSpec((prior, 128), wide(0)),
-                pl.BlockSpec((prior, 128), wide(0)),
+                pl.BlockSpec((prior, 128), lambda p, i, f: (0, p)),
+                pl.BlockSpec((prior, 128), lambda p, i, f: (0, p)),
             ],
             scratch_shapes=[
                 pltpu.VMEM((prior + rows, 128), BF16),
@@ -327,15 +345,16 @@
             jax.ShapeDtypeStruct((rows, width), BF16),
             jax.ShapeDtypeStruct((rows, width), F32),
             jax.ShapeDtypeStruct((rows, width), F32),
-            jax.ShapeDtypeStruct((prior, width), BF16),
-            jax.ShapeDtypeStruct((prior, width), BF16),
+            jax.ShapeDtypeStruct((prior, 128 * count), BF16),
+            jax.ShapeDtypeStruct((prior, 128 * count), BF16),
         ],
         compiler_params=params_of("arbitrary", "arbitrary"),
         cost_estimate=pl.CostEstimate(
-            flops=50 * 10**9, transcendentals=10**7, bytes_accessed=24 << 20
+            flops=8 * 10**9 * count, transcendentals=10**6 * count, bytes_accessed=4 * count << 20
         ),
+        input_output_aliases={9 + i: i for i in range(len(made))},
         name="attend",
-    )(first, qkv, qkv, qkv, before, before, d_context, low, table)
+    )(first, qkv, qkv, qkv, before, before, d_context, low, table, *extra)
 
 
 def mlp_body(
@@ -458,7 +477,9 @@
     x_ref,
     in_ref,
     gain_ref,
-    w_ref,
+    wq_ref,
+    wk_ref,
+    wv_ref,
     dq_ref,
     dk_ref,
     dv_ref,
@@ -466,13 +487,9 @@
     hv_ref,
     table_ref,
     rest_ref,
-    d_w_ref,
-    d_bias_ref,
-    grad_ref,
-    d_gain_ref,
-    d_shift_ref,
-    moved,
+    *refs,
 ):
+    d_wk_ref, d_wv_ref, d_bias_ref, grad_ref, d_gain_ref, d_shift_ref, moved = refs[-7:]
     step = pl.program_id(0)
     rows = x_ref.shape[0]
     own = rows - hk_ref.shape[0]
@@ -480,13 +497,10 @@
 
     @pl.when(step == 0)
     def _():
-        grad_ref[...] = jnp.zeros_like(grad_ref)
+        for s in spans:
+            grad_ref[s] = mm_bt(dq_ref[s], wq_ref[...])
 
     @pl.when(step < per_part)
-    def _():
-        moved[...] = dq_ref[...]
-
-    @pl.when((step >= per_part) & (step < 2 * per_part))
     def _():
         for s in spans:
             for c in range(0, moved.shape[1], 128):
@@ -494,19 +508,22 @@
                 if s.start >= own:
                     part = part + hk_ref[s.start - own : s.stop - own, c : c + 128].astype(F32)
                 moved[s, c : c + 128] = turn(part, table_ref[:, s], -1.0).astype(BF16)
-
-    @pl.when(step >= 2 * per_part)
+        d_wk_ref[...] = mm_at(in_ref[...], moved[...]).astype(BF16)
+        for s in spans:
+            grad_ref[s] += mm_bt(moved[s], wk_ref[...])
+
+    @pl.when(step >= per_part)
     def _():
         for s in spans:
             part = dv_ref[s]
             if s.start >= own:
                 part = part + hv_ref[s.start - own : s.stop - own].astype(F32)
             moved[s] = part.astype(BF16)
+        d_wv_ref[...] = mm_at(in_ref[...], moved[...]).astype(BF16)
+        for s in spans:
+            grad_ref[s] += mm_bt(moved[s], wv_ref[...])
 
     d_bias_ref[...] = jnp.sum(moved[...].astype(F32), axis=0, keepdims=True)
-    d_w_ref[...] = mm_at(in_ref[...], moved[...]).astype(BF16)
-    for s in spans:
-        grad_ref[s] += mm_bt(moved[s], w_ref[...])
 
     @pl.when(step == pl.num_programs(0) - 1)
     def _():
@@ -521,11 +538,10 @@
         d_shift_ref[...] = d_shift
 
 
-def back(tokens, attn_in, gain, weight, dq, dk, dv, halo_k, halo_v, table, rest):
+def back(tokens, attn_in, gain, weight, weight_more, dq, dk, dv, halo_k, halo_v, table, rest, after):
     rows, width = tokens.shape
     tile = 256
     per = width // tile
-    total = 3 * width
     prior = halo_k.shape[0]
     whole = lambda j: (0, 0)
     vector = pl.BlockSpec((1, width), whole)
@@ -533,30 +549,35 @@
     near = lambda off: (lambda j: (0, jnp.clip(j - off, 0, per - 1)))
     return pl.pallas_call(
         functools.partial(back_body, per),
-        grid=(total // tile,),
+        grid=(2 * per,),
         in_specs=[
             full,
             full,
             vector,
-            pl.BlockSpec((width, tile), lambda j: (0, j)),
+            pl.BlockSpec((width, width), whole),
+            pl.BlockSpec((width, tile), lambda j: (0, per + jnp.clip(j, 0, per - 1))),
+            pl.BlockSpec((width, tile), near(per)),
+            full,
             pl.BlockSpec((rows, tile), near(0)),
             pl.BlockSpec((rows, tile), near(per)),
-            pl.BlockSpec((rows, tile), near(2 * per)),
+            pl.BlockSpec((prior, tile), near(0)),
             pl.BlockSpec((prior, tile), near(per)),
-            pl.BlockSpec((prior, tile), near(2 * per)),
             pl.BlockSpec((3, rows, 128), lambda j: (0, 0, 0)),
             full,
+            *[pl.BlockSpec(memory_space=pl.ANY) for _ in after],
         ],
         out_specs=[
-            pl.BlockSpec((width, tile), lambda j: (0, j)),
+            pl.BlockSpec((width, tile), near(0)),
+            pl.BlockSpec((width, tile), near(per)),
             pl.BlockSpec((1, tile), lambda j: (0, j)),
             full,
             vector,
             vector,
         ],
         out_shape=[
-            jax.ShapeDtypeStruct((width, total), BF16),
-            jax.ShapeDtypeStruct((1, total), F32),
+            jax.ShapeDtypeStruct((width, width), BF16),
+            jax.ShapeDtypeStruct((width, width), BF16),
+            jax.ShapeDtypeStruct((1, 2 * width), F32),
             jax.ShapeDtypeStruct((rows, width), F32),
             jax.ShapeDtypeStruct((1, width), F32),
             jax.ShapeDtypeStruct((1, width), F32),
@@ -564,10 +585,10 @@
         scratch_shapes=[pltpu.VMEM((rows, tile), BF16)],
         compiler_params=params_of("arbitrary"),
         cost_estimate=pl.CostEstimate(
-            flops=4 * rows * width * total, transcendentals=0, bytes_accessed=30 << 20
+            flops=10 * rows * width * width, transcendentals=0, bytes_accessed=30 << 20
         ),
         name="qkv_back",
-    )(tokens, attn_in, gain, weight, dq, dk, dv, halo_k, halo_v, table, rest)
+    )(tokens, attn_in, gain, weight, weight, weight_more, dq, dk, dv, halo_k, halo_v, table, rest, *after)
 
 
 def local(
@@ -600,20 +621,31 @@
         up_bias,
         down_bias,
     )
-    counts = [v.shape[0] // own for v in vectors]
-    packed = jnp.concatenate([v.reshape(own, -1) for v in vectors], axis=1)
-    packed = jnp.pad(packed, ((0, 0), (0, 128 - packed.shape[1])))
-
-    first_half = gather(jnp.concatenate([qkv_weight, packed], axis=1), (0, 2, 1, 3))
-    w_down = gather(down_weight, (0, 1, 2, 3))
-    second = gather(jnp.concatenate([up_weight, out_weight], axis=1), (1, 2, 0, 3))
-    w_out = second[:, up_weight.shape[1] :]
-    flat, at = [], qkv_weight.shape[1]
-    small = first_half[:, at : at + 128].astype(F32)
-    at = 0
-    for count in counts:
-        flat.append(small[:, at : at + count].reshape(1, -1))
-        at += count
+    count = lax.axis_size(AXIS)
+    packed = jnp.concatenate(vectors)
+    packed = jnp.pad(packed, (0, own * 128 - packed.shape[0])).reshape(own, 128)
+
+    w_first = Gather(qkv_weight[:, : 2 * width], (0, 1, 2, 3))
+    w_then = Gather(
+        jnp.concatenate([qkv_weight[:, 2 * width :], out_weight, packed], axis=1), (0, 2, 1, 3)
+    )
+    w_up, w_down = Gather(up_weight, (0, 2, 1, 3)), Gather(down_weight, (0, 1, 2, 3))
+    w_first.step(), w_then.step()
+    behind(w_first.value, w_up, w_down, w_then)
+    for _ in range(3):
+        together(w_first, w_then)
+        w_first.step(), w_then.step()
+    w_up.step(), w_down.step()
+    for _ in range(3):
+        together(w_up, w_down)
+        w_up.step(), w_down.step()
+    w_first, w_then, w_up, w_down = [w.whole() for w in (w_first, w_then, w_up, w_down)]
+    w_out = w_then[:, width : 2 * width]
+    small = w_then[:, 2 * width :].reshape(count, own * 128).astype(F32)
+    flat, at = [], 0
+    for v in vectors:
+        flat.append(small[:, at : at + v.shape[0]].reshape(1, -1))
+        at += v.shape[0]
     gain_a, shift_a, gain_m, shift_m, b_qkv, b_out, b_up, b_down = flat
 
     row_index = jnp.arange(rows, dtype=jnp.int32)
@@ -638,45 +670,68 @@
         ]
     )
 
-    qkv, attn_in = project(tokens, gain_a, shift_a, first_half, b_qkv, table)
+    qkv, attn_in = project(tokens, gain_a, shift_a, w_first, w_then, b_qkv, table)
     halo = from_behind(qkv[rows - prior :, width:], 1)
     ffn, d_up, d_down, d_up_bias, rest, d_gain_m, d_shift_m, d_out_bias = mlp(
-        tokens, cotangent, gain_m, shift_m, second, b_up, w_down
-    )
+        tokens, cotangent, gain_m, shift_m, w_up, b_up, w_down
+    )
+    d_up, d_down = Scatter(d_up, (3, 1, 2, 0)), Scatter(d_down, (3, 2, 1, 0))
     d_context = mm_bt(cotangent, w_out).astype(BF16)
-    context, dq, dk, dv, back_k, back_v = attend(
-        first_block, qkv, halo, d_context, low[:, None], table
-    )
-    halo_k = from_behind(back_k, -1)
-    halo_v = from_behind(back_v, -1)
+    pairs = width // 128
+    shared = (first_block, qkv, halo, d_context, low[:, None], table)
+    *made, back_k, back_v = attend(*shared, 0, pairs // 2)
+    halo_k, halo_v = [from_behind(back_k, -1)], [from_behind(back_v, -1)]
+    summed = (d_up.step(), d_down.step())
+    *made, back_k, back_v = attend(*shared, pairs // 2, pairs - pairs // 2, made, summed)
+    context, dq, dk, dv = made
+    halo_k = jnp.concatenate([*halo_k, from_behind(back_k, -1)], axis=1)
+    halo_v = jnp.concatenate([*halo_v, from_behind(back_v, -1)], axis=1)
+    summed = (d_up.step(), d_down.step())
+    (context, dq), _ = lax.optimization_barrier(((context, dq), summed))
+    d_out = Scatter(mm_at(context, cotangent).astype(BF16), (3, 1, 2, 0))
+    d_wq = Scatter(mm_at(attn_in, dq).astype(BF16), (3, 2, 1, 0))
+    d_bias_q = jnp.sum(dq.astype(F32), axis=0, keepdims=True)
     block_out = (tokens.astype(F32) + (mm(context, w_out) + b_out) + (ffn + b_down)).astype(BF16)
-    d_out = mm_at(context, cotangent).astype(BF16)
-    d_qkv, d_qkv_bias, grad_tokens, d_gain_a, d_shift_a = back(
-        tokens, attn_in, gain_a, first_half, dq, dk, dv, halo_k, halo_v, table, rest
-    )
-
-    d_down = scatter(d_down, (3, 2, 1, 0))
-    d_up = scatter(d_up, (3, 0, 2, 1))
-    d_out = scatter(d_out, (3, 1, 0, 2))
-    d_qkv = scatter(d_qkv, (3, 1, 0, 2))
+    summed = (d_out.step(), d_wq.step())
+    d_wk, d_wv, d_bias_kv, grad_tokens, d_gain_a, d_shift_a = back(
+        tokens, attn_in, gain_a, w_first, w_then, dq, dk, dv, halo_k, halo_v, table, rest, summed
+    )
+
+    d_wk, d_wv = Scatter(d_wk, (3, 1, 2, 0)), Scatter(d_wv, (3, 2, 1, 0))
+    d_up.step(), d_down.step()
+    together(d_up, d_down, d_out, d_wq, d_wk, d_wv)
     sums = (
         d_gain_a,
         d_shift_a,
         d_gain_m,
         d_shift_m,
-        d_qkv_bias,
+        d_bias_q,
+        d_bias_kv,
         d_out_bias,
         d_up_bias,
     )
-    wide = jnp.concatenate([s.reshape(width, -1) for s in sums], axis=1)
-    wide = jnp.pad(wide, ((0, 0), (0, 128 - wide.shape[1])))
-    wide = scatter(wide, (3, 2, 1, 0))
+    wide = jnp.concatenate([s[:, :width].reshape(count, -1) for s in sums[:4]], axis=1)
+    d_bias = jnp.concatenate([d_bias_q, d_bias_kv], axis=1).reshape(count, -1)
+    wide = jnp.concatenate(
+        [wide, d_bias, d_out_bias.reshape(count, -1), d_up_bias.reshape(count, -1)], axis=1
+    )
+    wide = Scatter(wide, (3, 2, 1, 0))
+    for at in range(3):
+        chains = (d_wk, d_wv, wide, d_out, d_wq)
+        for chain in chains:
+            chain.step()
+        if at < 2:
+            together(*chains)
+        else:
+            together(d_wk, d_wv, wide)
+    wide = wide.rest().reshape(-1)
     out, at = [], 0
-    for s in sums:
-        count = s.shape[1] // width
-        out.append(wide[:, at : at + count].reshape(-1))
-        at += count
+    for many in (1, 1, 1, 1, 3, 1, 4):
+        out.append(wide[at : at + many * own])
+        at += many * own
     g_gain_a, g_shift_a, g_gain_m, g_shift_m, g_qkv_b, g_out_b, g_up_b = out
+    d_qkv = jnp.concatenate([d_wq.rest(), d_wk.rest(), d_wv.rest()], axis=1)
+    d_out, d_up, d_down = d_out.rest(), d_up.rest(), d_down.rest()
     return (
         block_out,
         grad_tokens,

time: 492 us -> 482 us (0.980)
  starting transfers between devices: 124 us -> 93.5 us
  waiting for transfers between devices: 131 us -> 145 us
  other arithmetic: 33.1 us -> 43.8 us
    ppermute x48 -> x66, starting transfers between devices: 116 us -> 82.8 us  [shifted(): return lax.ppermute(value, AXIS, moves)]
    reshape x23 -> x9, local copies, waits for them, and re-layouts: 19.4 us -> 5.32 us  [the longest x6 4.41 us: local(): flat.append(small[:, at:at + v.shape[0]].reshape(1, -1))]
    ppermute x48 -> x66, waiting for transfers between devices: 131 us -> 145 us  [shifted(): return lax.ppermute(value, AXIS, moves)]
    concatenate x2 -> x9, local copies, waits for them, and re-layouts: 2.9 us -> 13.4 us  [the longest x8 7.97 us: local(): jnp.concatenate([wide, d_bias, d_out_bias.reshape(count, -1), d_up_bias.r...]
    convert_element_type x13 -> x19, other arithmetic: 8.52 us -> 14 us  [the longest x18 14 us: step(): self.value = total.astype(self.kind) if self.order else total]
    concatenate x0 -> x4, other arithmetic: none -> 5.07 us  [the longest x1 2.1 us: local(): halo_v = jnp.concatenate([*halo_v, from_behind(back_v, -1)], axis=1)]
    squeeze x20 -> x27, local copies, waits for them, and re-layouts: 9.3 us -> 13.7 us  [part(): return lax.dynamic_index_in_dim(parts, at, 1, keepdims=False)]
    pallas_call x3 -> x4, Pallas kernels: 85.3 us -> 82.5 us  [the longest x2 52.5 us: attend(): pl.pallas_call(functools.partial(attend_body, prior, len(extra)), grid_sp...]
  transfers between devices with their start and end apart: 52 -> 72, of which waited for: 18 -> 22; matrix products, arithmetic and copies ran while one was open for 19% -> 20% of each run, Pallas kernels for 26% -> 26%
where the time goes in v3:
time: 482 us; the launch traced here: 473 us
  waiting for transfers between devices  145 us (30%)
  Pallas kernels  124 us (26%)
  starting transfers between devices  93.5 us (19%)
  local copies, waits for them, and re-layouts  54.6 us (11%)
  other arithmetic  43.8 us (9%)
  matrix products  8.19 us (2%)
    ppermute x66, waiting for transfers between devices, shifted(): return lax.ppermute(value, AXIS, moves)  145 us
    ppermute x66, starting transfers between devices, shifted(): return lax.ppermute(value, AXIS, moves)  82.8 us
    pallas_call x2, Pallas kernels, attend(): pl.pallas_call(functools.partial(attend_body, prior, len(extra)), grid_sp...  52.5 us
    pallas_call x1, Pallas kernels, mlp(): pl.pallas_call(mlp_body, grid=(ff // tile,), in_specs=[full, full, vector...  41.7 us
    pallas_call x1, Pallas kernels, back(): pl.pallas_call(functools.partial(back_body, per), grid=(2 * per,), in_spe...  20.2 us
    convert_element_type x18, other arithmetic, step(): self.value = total.astype(self.kind) if self.order else total  14 us
    squeeze x27, local copies, waits for them, and re-layouts, part(): return lax.dynamic_index_in_dim(parts, at, 1, keepdims=False)  13.7 us
    ppermute x6, starting transfers between devices, from_behind(): lax.ppermute(value, AXIS, [(source, source + steps) for source in range(l...  10.6 us
  transfers between devices with their start and end apart: 72, of which 22 were waited for; matrix products, arithmetic and copies ran while one was open for 20% of the time, Pallas kernels for 26%

profile of v3, /device:TPU:0, one launch (start us, length us, event | category | flops | bytes accessed | tf_op | source)
XLA Modules:
  0.0 473.0 jit_solution(5639095171465954260)
XLA Ops:
  1.5 4.0 collective-permute-start.2
  8.4 5.4 %concatenate.36 = bf16[312]{0:T(512)(128)(2,1)S(1)} concatenate(bf16[24]{0:T(256)(128)(2,1)} %param.18, bf16[24]{0:T(256)(128)(2,1)} %param.19, bf16[24]{0:T(256)(128)(2,1)} %param.20, bf16[24]{0:T(256)(128)(2,1)} %param.21, bf16[72]{0:T(256)(128)(2,1)} %param.23, bf16[24]{0:T(256)(128)(2,1)} %param.25, bf16[96]{0:T(256)(128)(2,1)} %param.27, bf16[24]{0:T(256)(128)(2,1)} %param.29), dimensions={0} | concatenate | bytes 1248 | tf_op jit(solution)/shard_map/concatenate | solution.py:625
  16.9 2.0 convert_reduce_fusion.2
  23.2 6.7 %collective-permute-start.6 = (bf16[1,24,1664]{2,1,0:T(8,128)(2,1)S(1)}, bf16[1,24,1664]{2,1,0:T(8,128)(2,1)S(1)}, u32[]{:S(2)}, u32[]{:S(2)}) collective-permute-start(bf16[1,24,1664]{2,1,0:T(8,128)(2,1)S(1)} %maximum_bitcast_fusion), channel_id=1, source_target_pairs={{0,24},{1,25},{2,26},{3,27},{4,28},{5,29},{6,30},{7,31},{8,0},{9,1... | collective-permute-start | bytes 239624 | tf_op jit(solution)/shard_map/ppermute | solution.py:51
  36.4 6.8 %collective-permute-done.4 = bf16[1,24,1664]{2,1,0:T(8,128)(2,1)S(1)} collective-permute-done((bf16[1,24,1664]{2,1,0:T(8,128)(2,1)S(1)}, bf16[1,24,1664]{2,1,0:T(8,128)(2,1)S(1)}, u32[]{:S(2)}, u32[]{:S(2)}) %collective-permute-start.4) | collective-permute-done | bytes 79904 | tf_op jit(solution)/shard_map/ppermute | solution.py:51
  43.6 2.0 collective-permute-start.17
  46.8 2.9 collective-permute-start.15
  50.6 8.2 %collective-permute-done.18 = bf16[1,96,768]{2,1,0:T(8,128)(2,1)S(1)} collective-permute-done((bf16[1,96,768]{2,1,0:T(8,128)(2,1)S(1)}, bf16[1,96,768]{2,1,0:T(8,128)(2,1)S(1)}, u32[]{:S(2)}, u32[]{:S(2)}) %collective-permute-start.18) | collective-permute-done | bytes 147488 | tf_op jit(solution)/shard_map/ppermute | solution.py:51
  59.1 5.1 %collective-permute-done.15 = bf16[1,24,3072]{2,1,0:T(8,128)(2,1)S(1)} collective-permute-done((bf16[1,24,3072]{2,1,0:T(8,128)(2,1)S(1)}, bf16[1,24,3072]{2,1,0:T(8,128)(2,1)S(1)}, u32[]{:S(2)}, u32[]{:S(2)}) %collective-permute-start.15) | collective-permute-done | bytes 147488 | tf_op jit(solution)/shard_map/ppermute | solution.py:51
  66.2 2.0 collective-permute-start.21
  70.5 11.9 %collective-permute-done.20 = bf16[4,24,3072]{2,1,0:T(8,128)(2,1)S(1)} collective-permute-done((bf16[4,24,3072]{2,1,0:T(8,128)(2,1)S(1)}, bf16[4,24,3072]{2,1,0:T(8,128)(2,1)S(1)}, u32[]{:S(2)}, u32[]{:S(2)}) %collective-permute-start.20) | collective-permute-done | bytes 589856 | tf_op jit(solution)/shard_map/ppermute | solution.py:51
  82.8 2.1 collective-permute-start.22
  85.9 9.1 %collective-permute-done.9 = bf16[8,24,1536]{2,1,0:T(8,128)(2,1)S(1)} collective-permute-done((bf16[8,24,1536]{2,1,0:T(8,128)(2,1)S(1)}, bf16[8,24,1536]{2,1,0:T(8,128)(2,1)S(1)}, u32[]{:S(2)}, u32[]{:S(2)}) %collective-permute-start.9) | collective-permute-done | bytes 589856 | tf_op jit(solution)/shard_map/ppermute | solution.py:51
  97.3 19.3 %collective-permute-done.23 = bf16[8,96,768]{2,1,0:T(8,128)(2,1)S(1)} collective-permute-done((bf16[8,96,768]{2,1,0:T(8,128)(2,1)S(1)}, bf16[8,96,768]{2,1,0:T(8,128)(2,1)S(1)}, u32[]{:S(2)}, u32[]{:S(2)}) %collective-permute-start.23) | collective-permute-done | bytes 1179680 | tf_op jit(solution)/shard_map/ppermute | solution.py:51
  117.1 2.1 collective-permute-done.22
  123.8 1.7 copy.101
  131.0 9.8 %qkv_project.1 = (bf16[1024,2304]{1,0:T(8,128)(2,1)}, bf16[1024,768]{1,0:T(8,128)(2,1)}) custom-call(bf16[1024,768]{1,0:T(8,128)(2,1)} %x_ref.5, f32[1,768]{1,0:T(1,128)} %reshape.507.gain_ref, f32[1,768]{1,0:T(1,128)} %reshape.508.shift_ref, bf16[768,1536]{1,0:T(8,128)(2,1)} %bitcast.350, bf16[768,1664]{1,0:T(8,128)(2,1)} %bitcast.354, ...), custom_call_target="tpu_custom_call" | custom-call | flops 3623878656 | bytes 16777216 | tf_op jit(solution)/shard_map/qkv_project/pallas_call | solution.py:189
  140.8 2.8 slice.108
  143.6 3.5 collective-permute-start.13
  147.1 2.6 fusion.4.dc_ref
  149.7 2.7 select_bitcast_fusion.3
  152.8 2.5 copy.110
  155.4 2.7 select_bitcast_fusion.1
  158.5 2.5 copy.112
  161.0 41.7 %mlp.1 = (f32[1024,768]{1,0:T(8,128)}, bf16[768,3072]{1,0:T(8,128)(2,1)}, bf16[3072,768]{1,0:T(8,128)(2,1)}, f32[1,3072]{1,0:T(1,128)}, f32[1024,768]{1,0:T(8,12...) custom-call(bf16[1024,768]{1,0:T(8,128)(2,1)} %x_ref.5, bf16[1024,768]{1,0:T(8,128)(2,1)} %cot_ref.1, ...), custom_call_target="tpu_custom_call" | custom-call | flops 28991029248 | bytes 31457280 | tf_op jit(solution)/shard_map/mlp/pallas_call | solution.py:430
  202.7 3.4 dynamic-slice_bitcast_fusion.1
  208.3 26.1 %attend.2 = (bf16[1024,768]{1,0:T(8,128)(2,1)}, bf16[1024,768]{1,0:T(8,128)(2,1)}, f32[1024,768]{1,0:T(8,128)}, f32[1024,768]{1,0:T(8,128)}, bf16[512,384]{1,0:T(8,128)(2,1)}, /*index=5*/bf16[512,384]{1,0:T(8,128)(2,1)}) custom-call(s32[4]{0:T(128)} %and_select_fusion.1.first_ref, bf16[1024,2304]{1,0:T(8,128)(2,1)} %get-tuple-element.85.q_ref.k_ref.v_ref, ...), custom_call_target="tpu_custom_call" | custom-call | flops 24000000000 | bytes 12582912 | tf_op jit(solution)/shard_map/attend/pallas_call | solution.py:312
  236.0 3.3 fusion.1.refs_4_
  240.5 6.7 %collective-permute-start.28 = (bf16[4,48,3072]{2,1,0:T(8,128)(2,1)}, bf16[4,48,3072]{2,1,0:T(8,128)(2,1)}, u32[]{:S(2)}, u32[]{:S(2)}) collective-permute-start(bf16[4,48,3072]{2,1,0:T(8,128)(2,1)} %dynamic-slice_bitcast_fusion.3), channel_id=1, source_target_pairs={{0,4},{1,5},{2,6},{3,7},{4,0},{5,1},{6,2},{7,3},{8,12},{9,13},{10,... | collective-permute-start | bytes 3538952 | tf_op jit(solution)/shard_map/ppermute | solution.py:51
  247.2 2.1 fusion.refs_5_
  249.3 26.3 %attend.3 = (bf16[1024,768]{1,0:T(8,128)(2,1)}, bf16[1024,768]{1,0:T(8,128)(2,1)}, f32[1024,768]{1,0:T(8,128)}, f32[1024,768]{1,0:T(8,128)}, bf16[512,384]{1,0:T(8,128)(2,1)}, /*index=5*/bf16[512,384]{1,0:T(8,128)(2,1)}) custom-call(s32[4]{0:T(128)} %and_select_fusion.1.first_ref, ...), custom_call_target="tpu_custom_call", output_to_operand_aliasing={{0}: (9, {}), {1}: (10, {}), {2}: (11, {}), {3}: (12, {})} | custom-call | flops 24000000000 | bytes 12582912 | tf_op jit(solution)/shard_map/attend/pallas_call | solution.py:312
  278.2 1.7 collective-permute-start.33
  279.9 2.4 dynamic-slice_bitcast_fusion.2
  282.4 6.8 %collective-permute-start.29 = (bf16[8,96,768]{2,1,0:T(8,128)(2,1)}, bf16[8,96,768]{2,1,0:T(8,128)(2,1)}, u32[]{:S(2)}, u32[]{:S(2)}) collective-permute-start(bf16[8,96,768]{2,1,0:T(8,128)(2,1)} %dynamic-slice_bitcast_fusion.2), channel_id=1, source_target_pairs={{0,2},{1,3},{2,0},{3,1},{4,6},{5,7},{6,4},{7,5},{8,10},{9,11},{10,... | collective-permute-start | bytes 3538952 | tf_op jit(solution)/shard_map/ppermute | solution.py:51
  293.8 2.1 pad_maximum_fusion.12.hv_ref
  295.9 1.8 fusion.3
  297.8 26.9 %collective-permute-done.29 = bf16[8,96,768]{2,1,0:T(8,128)(2,1)} collective-permute-done((bf16[8,96,768]{2,1,0:T(8,128)(2,1)}, bf16[8,96,768]{2,1,0:T(8,128)(2,1)}, u32[]{:S(2)}, u32[]{:S(2)}) %collective-permute-start.29) | collective-permute-done | bytes 1179680 | tf_op jit(solution)/shard_map/ppermute | solution.py:51
  331.1 2.4 collective-permute-start.36
  335.1 2.7 add_convert_fusion
  338.7 8.7 %collective-permute-done.36 = bf16[4,24,3072]{2,1,0:T(8,128)(2,1)S(1)} collective-permute-done((bf16[4,24,3072]{2,1,0:T(8,128)(2,1)S(1)}, bf16[4,24,3072]{2,1,0:T(8,128)(2,1)S(1)}, u32[]{:S(2)}, u32[]{:S(2)}) %collective-permute-start.36) | collective-permute-done | bytes 589856 | tf_op jit(solution)/shard_map/ppermute | solution.py:51
  348.6 20.2 %qkv_back.1 = (bf16[768,768]{1,0:T(8,128)(2,1)}, bf16[768,768]{1,0:T(8,128)(2,1)}, f32[1,1536]{1,0:T(1,128)}, f32[1024,768]{1,0:T(8,128)}, f32[1,768]{1,0:T(1,128)}, /*index=5*/f32[1,768]{1,0:T(1,128)}) custom-call(bf16[1024,768]{1,0:T(8,128)(2,1)} %x_ref.5, bf16[1024,768]{1,0:T(8,128)(2,1)} %get-tuple-element.104.in_ref, f32[1,768]{1,0:T(1,128)} %reshape.507.gain_ref, ...), custom_call_target="tpu_custom_call" | custom-call | flops 6039797760 | bytes 31457280 | tf_op jit(solution)/shard_map/qkv_back/pallas_call | solution.py:550
  370.1 2.0 dynamic-slice_bitcast_fusion.5
  384.5 2.5 collective-permute-start.67
  387.5 2.7 collective-permute-done.68
  390.2 2.9 collective-permute-start.71
  393.1 9.7 %collective-permute-done.67 = bf16[1,24,3072]{2,1,0:T(8,128)(2,1)S(1)} collective-permute-done((bf16[1,24,3072]{2,1,0:T(8,128)(2,1)S(1)}, bf16[1,24,3072]{2,1,0:T(8,128)(2,1)S(1)}, u32[]{:S(2)}, u32[]{:S(2)}) %collective-permute-start.67) | collective-permute-done | bytes 147488 | tf_op jit(solution)/shard_map/ppermute | solution.py:51
  404.6 8.4 %collective-permute-done.70 = bf16[1,96,768]{2,1,0:T(8,128)(2,1)S(1)} collective-permute-done((bf16[1,96,768]{2,1,0:T(8,128)(2,1)S(1)}, bf16[1,96,768]{2,1,0:T(8,128)(2,1)S(1)}, u32[]{:S(2)}, u32[]{:S(2)}) %collective-permute-start.70) | collective-permute-done | bytes 147488 | tf_op jit(solution)/shard_map/ppermute | solution.py:51
  412.9 1.8 collective-permute-start.42
  415.6 5.5 %collective-permute-done.42 = bf16[8,24,768]{2,1,0:T(8,128)(2,1)S(1)} collective-permute-done((bf16[8,24,768]{2,1,0:T(8,128)(2,1)S(1)}, bf16[8,24,768]{2,1,0:T(8,128)(2,1)S(1)}, u32[]{:S(2)}, u32[]{:S(2)}) %collective-permute-start.42) | collective-permute-done | bytes 294944 | tf_op jit(solution)/shard_map/ppermute | solution.py:51
  424.0 1.8 collective-permute-start.44
  426.2 1.8 collective-permute-start.46
  428.8 3.7 collective-permute-done.45
  432.5 1.8 collective-permute-done.46
  434.6 1.8 collective-permute-start.48
  438.7 3.3 collective-permute-start.55
  443.6 2.4 collective-permute-start.65
  448.0 2.8 collective-permute-done.64
  450.8 2.9 collective-permute-done.63
  454.6 1.9 collective-permute-start.51
  456.6 2.4 collective-permute-start.62
  459.6 2.0 collective-permute-start.60
  461.6 1.9 collective-permute-start.59
  466.0 2.4 collective-permute-done.58
  468.4 3.2 collective-permute-done.57
  (312 shorter events, 91.4 us)
Async XLA Ops:
  1.5 34.7 %collective-permute-start.2 = (bf16[1,24,1536]{2,1,0:T(8,128)(2,1)S(1)}, bf16[1,24,1536]{2,1,0:T(8,128)(2,1)S(1)}, u32[]{:S(2)}, u32[]{:S(2)}) collective-permute-start(bf16[1,24,1536]{2,1,0:T(8,128)(2,1)S(1)} %slice_bitcast_fusion), channel_id=1, source_target_pairs={{0,16},{1,17},{2,18},{3,19},{4,20},{5,21},{6,22},{7,23},{8,24},{9,... | collective-permute-start | bytes 221192 | tf_op jit(solution)/shard_map/ppermute | solution.py:51
  5.6 30.7 %collective-permute-start.3 = (bf16[1,24,1536]{2,1,0:T(8,128)(2,1)S(1)}, bf16[1,24,1536]{2,1,0:T(8,128)(2,1)S(1)}, u32[]{:S(2)}, u32[]{:S(2)}) collective-permute-start(bf16[1,24,1536]{2,1,0:T(8,128)(2,1)S(1)} %slice_bitcast_fusion), channel_id=1, source_target_pairs={{0,24},{1,25},{2,26},{3,27},{4,28},{5,29},{6,30},{7,31},{8,0},{9,1... | collective-permute-start | bytes 221192 | tf_op jit(solution)/shard_map/ppermute | solution.py:51
  6.9 29.3 %collective-permute-start.1 = (bf16[1,24,1536]{2,1,0:T(8,128)(2,1)S(1)}, bf16[1,24,1536]{2,1,0:T(8,128)(2,1)S(1)}, u32[]{:S(2)}, u32[]{:S(2)}) collective-permute-start(bf16[1,24,1536]{2,1,0:T(8,128)(2,1)S(1)} %slice_bitcast_fusion), channel_id=1, source_target_pairs={{0,8},{1,9},{2,10},{3,11},{4,12},{5,13},{6,14},{7,15},{8,16},{9,17... | collective-permute-start | bytes 221192 | tf_op jit(solution)/shard_map/ppermute | solution.py:51
  14.6 21.8 %collective-permute-start.5 = (bf16[1,24,1664]{2,1,0:T(8,128)(2,1)S(1)}, bf16[1,24,1664]{2,1,0:T(8,128)(2,1)S(1)}, u32[]{:S(2)}, u32[]{:S(2)}) collective-permute-start(bf16[1,24,1664]{2,1,0:T(8,128)(2,1)S(1)} %maximum_bitcast_fusion), channel_id=1, source_target_pairs={{0,16},{1,17},{2,18},{3,19},{4,20},{5,21},{6,22},{7,23},{8,24},{9,... | collective-permute-start | bytes 239624 | tf_op jit(solution)/shard_map/ppermute | solution.py:51
  23.2 13.2 %collective-permute-start.6 = (bf16[1,24,1664]{2,1,0:T(8,128)(2,1)S(1)}, bf16[1,24,1664]{2,1,0:T(8,128)(2,1)S(1)}, u32[]{:S(2)}, u32[]{:S(2)}) collective-permute-start(bf16[1,24,1664]{2,1,0:T(8,128)(2,1)S(1)} %maximum_bitcast_fusion), channel_id=1, source_target_pairs={{0,24},{1,25},{2,26},{3,27},{4,28},{5,29},{6,30},{7,31},{8,0},{9,1... | collective-permute-start | bytes 239624 | tf_op jit(solution)/shard_map/ppermute | solution.py:51
  36.2 7.0 %collective-permute-start.4 = (bf16[1,24,1664]{2,1,0:T(8,128)(2,1)S(1)}, bf16[1,24,1664]{2,1,0:T(8,128)(2,1)S(1)}, u32[]{:S(2)}, u32[]{:S(2)}) collective-permute-start(bf16[1,24,1664]{2,1,0:T(8,128)(2,1)S(1)} %maximum_bitcast_fusion), channel_id=1, source_target_pairs={{0,8},{1,9},{2,10},{3,11},{4,12},{5,13},{6,14},{7,15},{8,16},{9,17... | collective-permute-start | bytes 239624 | tf_op jit(solution)/shard_map/ppermute | solution.py:51
  43.4 15.4 %collective-permute-start.18 = (bf16[1,96,768]{2,1,0:T(8,128)(2,1)S(1)}, bf16[1,96,768]{2,1,0:T(8,128)(2,1)S(1)}, u32[]{:S(2)}, u32[]{:S(2)}) collective-permute-start(bf16[1,96,768]{2,1,0:T(8,128)(2,1)S(1)} %bitcast.409), channel_id=1, source_target_pairs={{0,16},{1,17},{2,18},{3,19},{4,20},{5,21},{6,22},{7,23},{8,24},{9,... | collective-permute-start | bytes 442376 | tf_op jit(solution)/shard_map/ppermute | solution.py:51
  43.5 15.3 %collective-permute-start.19 = (bf16[1,96,768]{2,1,0:T(8,128)(2,1)S(1)}, bf16[1,96,768]{2,1,0:T(8,128)(2,1)S(1)}, u32[]{:S(2)}, u32[]{:S(2)}) collective-permute-start(bf16[1,96,768]{2,1,0:T(8,128)(2,1)S(1)} %bitcast.410), channel_id=1, source_target_pairs={{0,24},{1,25},{2,26},{3,27},{4,28},{5,29},{6,30},{7,31},{8,0},{9,1... | collective-permute-start | bytes 442376 | tf_op jit(solution)/shard_map/ppermute | solution.py:51
  43.6 15.3 %collective-permute-start.17 = (bf16[1,96,768]{2,1,0:T(8,128)(2,1)S(1)}, bf16[1,96,768]{2,1,0:T(8,128)(2,1)S(1)}, u32[]{:S(2)}, u32[]{:S(2)}) collective-permute-start(bf16[1,96,768]{2,1,0:T(8,128)(2,1)S(1)} %bitcast.411), channel_id=1, source_target_pairs={{0,8},{1,9},{2,10},{3,11},{4,12},{5,13},{6,14},{7,15},{8,16},{9,17... | collective-permute-start | bytes 442376 | tf_op jit(solution)/shard_map/ppermute | solution.py:51
  46.8 17.4 %collective-permute-start.15 = (bf16[1,24,3072]{2,1,0:T(8,128)(2,1)S(1)}, bf16[1,24,3072]{2,1,0:T(8,128)(2,1)S(1)}, u32[]{:S(2)}, u32[]{:S(2)}) collective-permute-start(bf16[1,24,3072]{2,1,0:T(8,128)(2,1)S(1)} %bitcast.412), channel_id=1, source_target_pairs={{0,16},{1,17},{2,18},{3,19},{4,20},{5,21},{6,22},{7,23},{8,24},{9,... | collective-permute-start | bytes 442376 | tf_op jit(solution)/shard_map/ppermute | solution.py:51
  49.7 14.6 %collective-permute-start.16 = (bf16[1,24,3072]{2,1,0:T(8,128)(2,1)S(1)}, bf16[1,24,3072]{2,1,0:T(8,128)(2,1)S(1)}, u32[]{:S(2)}, u32[]{:S(2)}) collective-permute-start(bf16[1,24,3072]{2,1,0:T(8,128)(2,1)S(1)} %bitcast.413), channel_id=1, source_target_pairs={{0,24},{1,25},{2,26},{3,27},{4,28},{5,29},{6,30},{7,31},{8,0},{9,1... | collective-permute-start | bytes 442376 | tf_op jit(solution)/shard_map/ppermute | solution.py:51
  58.8 7.0 %collective-permute-start.14 = (bf16[1,24,3072]{2,1,0:T(8,128)(2,1)S(1)}, bf16[1,24,3072]{2,1,0:T(8,128)(2,1)S(1)}, u32[]{:S(2)}, u32[]{:S(2)}) collective-permute-start(bf16[1,24,3072]{2,1,0:T(8,128)(2,1)S(1)} %bitcast.414), channel_id=1, source_target_pairs={{0,8},{1,9},{2,10},{3,11},{4,12},{5,13},{6,14},{7,15},{8,16},{9,17... | collective-permute-start | bytes 442376 | tf_op jit(solution)/shard_map/ppermute | solution.py:51
  58.8 9.4 %collective-permute-start.7 = (bf16[4,24,1536]{2,1,0:T(8,128)(2,1)S(1)}, bf16[4,24,1536]{2,1,0:T(8,128)(2,1)S(1)}, u32[]{:S(2)}, u32[]{:S(2)}) collective-permute-start(bf16[4,24,1536]{2,1,0:T(8,128)(2,1)S(1)} %bitcast.408), channel_id=1, source_target_pairs={{0,4},{1,5},{2,6},{3,7},{4,0},{5,1},{6,2},{7,3},{8,12},{9,13},{10,... | collective-permute-start | bytes 884744 | tf_op jit(solution)/shard_map/ppermute | solution.py:51
  58.9 9.5 %collective-permute-start.8 = (bf16[4,24,1664]{2,1,0:T(8,128)(2,1)S(1)}, bf16[4,24,1664]{2,1,0:T(8,128)(2,1)S(1)}, u32[]{:S(2)}, u32[]{:S(2)}) collective-permute-start(bf16[4,24,1664]{2,1,0:T(8,128)(2,1)S(1)} %bitcast.391), channel_id=1, source_target_pairs={{0,2},{1,3},{2,0},{3,1},{4,6},{5,7},{6,4},{7,5},{8,10},{9,11},{10,... | collective-permute-start | bytes 958472 | tf_op jit(solution)/shard_map/ppermute | solution.py:51
  66.1 16.3 %collective-permute-start.20 = (bf16[4,24,3072]{2,1,0:T(8,128)(2,1)S(1)}, bf16[4,24,3072]{2,1,0:T(8,128)(2,1)S(1)}, u32[]{:S(2)}, u32[]{:S(2)}) collective-permute-start(bf16[4,24,3072]{2,1,0:T(8,128)(2,1)S(1)} %bitcast.386), channel_id=1, source_target_pairs={{0,2},{1,3},{2,0},{3,1},{4,6},{5,7},{6,4},{7,5},{8,10},{9,11},{10,... | collective-permute-start | bytes 1769480 | tf_op jit(solution)/shard_map/ppermute | solution.py:51
  66.2 16.3 %collective-permute-start.21 = (bf16[4,96,768]{2,1,0:T(8,128)(2,1)S(1)}, bf16[4,96,768]{2,1,0:T(8,128)(2,1)S(1)}, u32[]{:S(2)}, u32[]{:S(2)}) collective-permute-start(bf16[4,96,768]{2,1,0:T(8,128)(2,1)S(1)} %bitcast.384), channel_id=1, source_target_pairs={{0,4},{1,5},{2,6},{3,7},{4,0},{5,1},{6,2},{7,3},{8,12},{9,13},{10,... | collective-permute-start | bytes 1769480 | tf_op jit(solution)/shard_map/ppermute | solution.py:51
  68.5 26.5 %collective-permute-start.9 = (bf16[8,24,1536]{2,1,0:T(8,128)(2,1)S(1)}, bf16[8,24,1536]{2,1,0:T(8,128)(2,1)S(1)}, u32[]{:S(2)}, u32[]{:S(2)}) collective-permute-start(bf16[8,24,1536]{2,1,0:T(8,128)(2,1)S(1)} %bitcast.385), channel_id=1, source_target_pairs={{0,2},{1,3},{2,0},{3,1},{4,6},{5,7},{6,4},{7,5},{8,10},{9,11},{10,... | collective-permute-start | bytes 1769480 | tf_op jit(solution)/shard_map/ppermute | solution.py:51
  69.6 26.6 %collective-permute-start.10 = (bf16[4,48,1664]{2,1,0:T(8,128)(2,1)S(1)}, bf16[4,48,1664]{2,1,0:T(8,128)(2,1)S(1)}, u32[]{:S(2)}, u32[]{:S(2)}) collective-permute-start(bf16[4,48,1664]{2,1,0:T(8,128)(2,1)S(1)} %bitcast.383), channel_id=1, source_target_pairs={{0,4},{1,5},{2,6},{3,7},{4,0},{5,1},{6,2},{7,3},{8,12},{9,13},{10,... | collective-permute-start | bytes 1916936 | tf_op jit(solution)/shard_map/ppermute | solution.py:51
  82.8 36.4 %collective-permute-start.22 = (bf16[4,48,3072]{2,1,0:T(8,128)(2,1)S(1)}, bf16[4,48,3072]{2,1,0:T(8,128)(2,1)S(1)}, u32[]{:S(2)}, u32[]{:S(2)}) collective-permute-start(bf16[4,48,3072]{2,1,0:T(8,128)(2,1)S(1)} %bitcast.374), channel_id=1, source_target_pairs={{0,4},{1,5},{2,6},{3,7},{4,0},{5,1},{6,2},{7,3},{8,12},{9,13},{10,... | collective-permute-start | bytes 3538952 | tf_op jit(solution)/shard_map/ppermute | solution.py:51
  84.9 31.8 %collective-permute-start.23 = (bf16[8,96,768]{2,1,0:T(8,128)(2,1)S(1)}, bf16[8,96,768]{2,1,0:T(8,128)(2,1)S(1)}, u32[]{:S(2)}, u32[]{:S(2)}) collective-permute-start(bf16[8,96,768]{2,1,0:T(8,128)(2,1)S(1)} %bitcast.375), channel_id=1, source_target_pairs={{0,2},{1,3},{2,0},{3,1},{4,6},{5,7},{6,4},{7,5},{8,10},{9,11},{10,... | collective-permute-start | bytes 3538952 | tf_op jit(solution)/shard_map/ppermute | solution.py:51
  96.6 28.9 %collective-permute-start.11 = (bf16[16,24,1664]{2,1,0:T(8,128)(2,1)S(1)}, bf16[16,24,1664]{2,1,0:T(8,128)(2,1)S(1)}, u32[]{:S(2)}, u32[]{:S(2)}) collective-permute-start(bf16[16,24,1664]{2,1,0:T(8,128)(2,1)S(1)} %bitcast.366), channel_id=1, source_target_pairs={{0,1},{1,0},{2,3},{3,2},{4,5},{5,4},{6,7},{7,6},{8,9},{9,8},{10,11... | collective-permute-start | bytes 3833864 | tf_op jit(solution)/shard_map/ppermute | solution.py:51
  96.8 26.6 %collective-permute-start.12 = (bf16[16,24,1536]{2,1,0:T(8,128)(2,1)S(1)}, bf16[16,24,1536]{2,1,0:T(8,128)(2,1)S(1)}, u32[]{:S(2)}, u32[]{:S(2)}) collective-permute-start(bf16[16,24,1536]{2,1,0:T(8,128)(2,1)S(1)} %bitcast.376), channel_id=1, source_target_pairs={{0,1},{1,0},{2,3},{3,2},{4,5},{5,4},{6,7},{7,6},{8,9},{9,8},{10,11... | collective-permute-start | bytes 3538952 | tf_op jit(solution)/shard_map/ppermute | solution.py:51
  121.3 28.4 %collective-permute-start.24 = (bf16[16,24,3072]{2,1,0:T(8,128)(2,1)}, bf16[16,24,3072]{2,1,0:T(8,128)(2,1)}, u32[]{:S(2)}, u32[]{:S(2)}) collective-permute-start(bf16[16,24,3072]{2,1,0:T(8,128)(2,1)} %bitcast.66), channel_id=1, source_target_pairs={{0,1},{1,0},{2,3},{3,2},{4,5},{5,4},{6,7},{7,6},{8,9},{9,8},{10,11... | collective-permute-start | bytes 7077896 | tf_op jit(solution)/shard_map/ppermute | solution.py:51
  122.8 32.5 %collective-permute-start.25 = (bf16[16,96,768]{2,1,0:T(8,128)(2,1)}, bf16[16,96,768]{2,1,0:T(8,128)(2,1)}, u32[]{:S(2)}, u32[]{:S(2)}) collective-permute-start(bf16[16,96,768]{2,1,0:T(8,128)(2,1)} %bitcast.70), channel_id=1, source_target_pairs={{0,1},{1,0},{2,3},{3,2},{4,5},{5,4},{6,7},{7,6},{8,9},{9,8},{10,11... | collective-permute-start | bytes 7077896 | tf_op jit(solution)/shard_map/ppermute | solution.py:51
  143.6 64.7 %collective-permute-start.13 = (bf16[512,1536]{1,0:T(8,128)(2,1)}, bf16[512,1536]{1,0:T(8,128)(2,1)}, u32[]{:S(2)}, u32[]{:S(2)}) collective-permute-start(bf16[512,1536]{1,0:T(8,128)(2,1)} %slice.108), channel_id=1, source_target_pairs={{0,1},{1,2},{2,3},{3,4},{4,5},{5,6},{6,7},{7,8},{8,9},{9,10},{10,1... | collective-permute-start | bytes 4718600 | tf_op jit(solution)/shard_map/ppermute | solution.py:143
  206.1 29.9 %collective-permute-start.26 = (bf16[16,24,3072]{2,1,0:T(8,128)(2,1)}, bf16[16,24,3072]{2,1,0:T(8,128)(2,1)}, u32[]{:S(2)}, u32[]{:S(2)}) collective-permute-start(bf16[16,24,3072]{2,1,0:T(8,128)(2,1)} %dynamic-slice_bitcast_fusion.1), channel_id=1, source_target_pairs={{0,1},{1,0},{2,3},{3,2},{4,5},{5,4},{6,7},{7,6},{8,9},{9,8},{10,11... | collective-permute-start | bytes 7077896 | tf_op jit(solution)/shard_map/ppermute | solution.py:51
  207.8 39.4 %collective-permute-start.27 = (bf16[16,96,768]{2,1,0:T(8,128)(2,1)}, bf16[16,96,768]{2,1,0:T(8,128)(2,1)S(1)}, u32[]{:S(2)}, u32[]{:S(2)}) collective-permute-start(bf16[16,96,768]{2,1,0:T(8,128)(2,1)} %dynamic-slice_bitcast_fusion), channel_id=1, source_target_pairs={{0,1},{1,0},{2,3},{3,2},{4,5},{5,4},{6,7},{7,6},{8,9},{9,8},{10,11... | collective-permute-start | bytes 7077896 | tf_op jit(solution)/shard_map/ppermute | solution.py:51
  234.5 47.9 %collective-permute-start.30 = (bf16[512,384]{1,0:T(8,128)(2,1)}, bf16[512,384]{1,0:T(8,128)(2,1)S(1)}, u32[]{:S(2)}, u32[]{:S(2)}) collective-permute-start(bf16[512,384]{1,0:T(8,128)(2,1)} %get-tuple-element.108), channel_id=1, source_target_pairs={{1,0},{2,1},{3,2},{4,3},{5,4},{6,5},{7,6},{8,7},{9,8},{10,9},{11,1... | collective-permute-start | bytes 1179656 | tf_op jit(solution)/shard_map/ppermute | solution.py:143
  240.5 55.4 %collective-permute-start.28 = (bf16[4,48,3072]{2,1,0:T(8,128)(2,1)}, bf16[4,48,3072]{2,1,0:T(8,128)(2,1)}, u32[]{:S(2)}, u32[]{:S(2)}) collective-permute-start(bf16[4,48,3072]{2,1,0:T(8,128)(2,1)} %dynamic-slice_bitcast_fusion.3), channel_id=1, source_target_pairs={{0,4},{1,5},{2,6},{3,7},{4,0},{5,1},{6,2},{7,3},{8,12},{9,13},{10,... | collective-permute-start | bytes 3538952 | tf_op jit(solution)/shard_map/ppermute | solution.py:51
  275.6 17.2 %collective-permute-start.31 = (bf16[512,384]{1,0:T(8,128)(2,1)}, bf16[512,384]{1,0:T(8,128)(2,1)S(1)}, u32[]{:S(2)}, u32[]{:S(2)}) collective-permute-start(bf16[512,384]{1,0:T(8,128)(2,1)} %get-tuple-element.109), channel_id=1, source_target_pairs={{1,0},{2,1},{3,2},{4,3},{5,4},{6,5},{7,6},{8,7},{9,8},{10,9},{11,1... | collective-permute-start | bytes 1179656 | tf_op jit(solution)/shard_map/ppermute | solution.py:143
  276.9 16.9 %collective-permute-start.32 = (bf16[512,384]{1,0:T(8,128)(2,1)}, bf16[512,384]{1,0:T(8,128)(2,1)}, u32[]{:S(2)}, u32[]{:S(2)}) collective-permute-start(bf16[512,384]{1,0:T(8,128)(2,1)} %get-tuple-element.110), channel_id=1, source_target_pairs={{1,0},{2,1},{3,2},{4,3},{5,4},{6,5},{7,6},{8,7},{9,8},{10,9},{11,1... | collective-permute-start | bytes 1179656 | tf_op jit(solution)/shard_map/ppermute | solution.py:143
  278.2 15.6 %collective-permute-start.33 = (bf16[512,384]{1,0:T(8,128)(2,1)}, bf16[512,384]{1,0:T(8,128)(2,1)}, u32[]{:S(2)}, u32[]{:S(2)}) collective-permute-start(bf16[512,384]{1,0:T(8,128)(2,1)} %get-tuple-element.111), channel_id=1, source_target_pairs={{1,0},{2,1},{3,2},{4,3},{5,4},{6,5},{7,6},{8,7},{9,8},{10,9},{11,1... | collective-permute-start | bytes 1179656 | tf_op jit(solution)/shard_map/ppermute | solution.py:143
  282.4 42.3 %collective-permute-start.29 = (bf16[8,96,768]{2,1,0:T(8,128)(2,1)}, bf16[8,96,768]{2,1,0:T(8,128)(2,1)}, u32[]{:S(2)}, u32[]{:S(2)}) collective-permute-start(bf16[8,96,768]{2,1,0:T(8,128)(2,1)} %dynamic-slice_bitcast_fusion.2), channel_id=1, source_target_pairs={{0,2},{1,3},{2,0},{3,1},{4,6},{5,7},{6,4},{7,5},{8,10},{9,11},{10,... | collective-permute-start | bytes 3538952 | tf_op jit(solution)/shard_map/ppermute | solution.py:51
  327.9 9.9 %collective-permute-start.34 = (bf16[16,24,768]{2,1,0:T(8,128)(2,1)S(1)}, bf16[16,24,768]{2,1,0:T(8,128)(2,1)S(1)}, u32[]{:S(2)}, u32[]{:S(2)}) collective-permute-start(bf16[16,24,768]{2,1,0:T(8,128)(2,1)S(1)} %dynamic-slice_bitcast_fusion.9), channel_id=1, source_target_pairs={{0,1},{1,0},{2,3},{3,2},{4,5},{5,4},{6,7},{7,6},{8,9},{9,8},{10,11... | collective-permute-start | bytes 1769480 | tf_op jit(solution)/shard_map/ppermute | solution.py:51
  330.8 16.8 %collective-permute-start.35 = (bf16[16,24,768]{2,1,0:T(8,128)(2,1)S(1)}, bf16[16,24,768]{2,1,0:T(8,128)(2,1)S(1)}, u32[]{:S(2)}, u32[]{:S(2)}) collective-permute-start(bf16[16,24,768]{2,1,0:T(8,128)(2,1)S(1)} %dynamic-slice_bitcast_fusion.8), channel_id=1, source_target_pairs={{0,1},{1,0},{2,3},{3,2},{4,5},{5,4},{6,7},{7,6},{8,9},{9,8},{10,11... | collective-permute-start | bytes 1769480 | tf_op jit(solution)/shard_map/ppermute | solution.py:51
  331.1 16.3 %collective-permute-start.36 = (bf16[4,24,3072]{2,1,0:T(8,128)(2,1)S(1)}, bf16[4,24,3072]{2,1,0:T(8,128)(2,1)S(1)}, u32[]{:S(2)}, u32[]{:S(2)}) collective-permute-start(bf16[4,24,3072]{2,1,0:T(8,128)(2,1)S(1)} %dynamic-slice_bitcast_fusion.7), channel_id=1, source_target_pairs={{0,2},{1,3},{2,0},{3,1},{4,6},{5,7},{6,4},{7,5},{8,10},{9,11},{10,... | collective-permute-start | bytes 1769480 | tf_op jit(solution)/shard_map/ppermute | solution.py:51
  334.4 34.3 %collective-permute-start.37 = (bf16[4,96,768]{2,1,0:T(8,128)(2,1)}, bf16[4,96,768]{2,1,0:T(8,128)(2,1)}, u32[]{:S(2)}, u32[]{:S(2)}) collective-permute-start(bf16[4,96,768]{2,1,0:T(8,128)(2,1)} %dynamic-slice_bitcast_fusion.6), channel_id=1, source_target_pairs={{0,4},{1,5},{2,6},{3,7},{4,0},{5,1},{6,2},{7,3},{8,12},{9,13},{10,... | collective-permute-start | bytes 1769480 | tf_op jit(solution)/shard_map/ppermute | solution.py:51
  372.1 49.1 %collective-permute-start.38 = (bf16[16,24,768]{2,1,0:T(8,128)(2,1)}, bf16[16,24,768]{2,1,0:T(8,128)(2,1)}, u32[]{:S(2)}, u32[]{:S(2)}) collective-permute-start(bf16[16,24,768]{2,1,0:T(8,128)(2,1)} %dynamic-slice_bitcast_fusion.5), channel_id=1, source_target_pairs={{0,1},{1,0},{2,3},{3,2},{4,5},{5,4},{6,7},{7,6},{8,9},{9,8},{10,11... | collective-permute-start | bytes 1769480 | tf_op jit(solution)/shard_map/ppermute | solution.py:51
  384.2 31.3 %collective-permute-start.41 = (bf16[4,48,768]{2,1,0:T(8,128)(2,1)S(1)}, bf16[4,48,768]{2,1,0:T(8,128)(2,1)S(1)}, u32[]{:S(2)}, u32[]{:S(2)}) collective-permute-start(bf16[4,48,768]{2,1,0:T(8,128)(2,1)S(1)} %dynamic-slice_bitcast_fusion.13), channel_id=1, source_target_pairs={{0,4},{1,5},{2,6},{3,7},{4,0},{5,1},{6,2},{7,3},{8,12},{9,13},{10,... | collective-permute-start | bytes 884744 | tf_op jit(solution)/shard_map/ppermute | solution.py:51
  384.4 5.8 %collective-permute-start.68 = (bf16[1,24,3072]{2,1,0:T(8,128)(2,1)S(1)}, bf16[1,24,3072]{2,1,0:T(8,128)(2,1)S(1)}, u32[]{:S(2)}, u32[]{:S(2)}) collective-permute-start(bf16[1,24,3072]{2,1,0:T(8,128)(2,1)S(1)} %get-tuple-element.168), channel_id=1, source_target_pairs={{0,24},{1,25},{2,26},{3,27},{4,28},{5,29},{6,30},{7,31},{8,0},{9,1... | collective-permute-start | bytes 442376 | tf_op jit(solution)/shard_map/ppermute | solution.py:51
  384.5 18.3 %collective-permute-start.67 = (bf16[1,24,3072]{2,1,0:T(8,128)(2,1)S(1)}, bf16[1,24,3072]{2,1,0:T(8,128)(2,1)S(1)}, u32[]{:S(2)}, u32[]{:S(2)}) collective-permute-start(bf16[1,24,3072]{2,1,0:T(8,128)(2,1)S(1)} %get-tuple-element.169), channel_id=1, source_target_pairs={{0,16},{1,17},{2,18},{3,19},{4,20},{5,21},{6,22},{7,23},{8,24},{9,... | collective-permute-start | bytes 442376 | tf_op jit(solution)/shard_map/ppermute | solution.py:51
  387.1 15.7 %collective-permute-start.66 = (bf16[1,24,3072]{2,1,0:T(8,128)(2,1)S(1)}, bf16[1,24,3072]{2,1,0:T(8,128)(2,1)S(1)}, u32[]{:S(2)}, u32[]{:S(2)}) collective-permute-start(bf16[1,24,3072]{2,1,0:T(8,128)(2,1)S(1)} %get-tuple-element.167), channel_id=1, source_target_pairs={{0,8},{1,9},{2,10},{3,11},{4,12},{5,13},{6,14},{7,15},{8,16},{9,17... | collective-permute-start | bytes 442376 | tf_op jit(solution)/shard_map/ppermute | solution.py:51
  390.2 14.4 %collective-permute-start.71 = (bf16[1,96,768]{2,1,0:T(8,128)(2,1)S(1)}, bf16[1,96,768]{2,1,0:T(8,128)(2,1)S(1)}, u32[]{:S(2)}, u32[]{:S(2)}) collective-permute-start(bf16[1,96,768]{2,1,0:T(8,128)(2,1)S(1)} %get-tuple-element.165), channel_id=1, source_target_pairs={{0,24},{1,25},{2,26},{3,27},{4,28},{5,29},{6,30},{7,31},{8,0},{9,1... | collective-permute-start | bytes 442376 | tf_op jit(solution)/shard_map/ppermute | solution.py:51
  402.8 10.2 %collective-permute-start.70 = (bf16[1,96,768]{2,1,0:T(8,128)(2,1)S(1)}, bf16[1,96,768]{2,1,0:T(8,128)(2,1)S(1)}, u32[]{:S(2)}, u32[]{:S(2)}) collective-permute-start(bf16[1,96,768]{2,1,0:T(8,128)(2,1)S(1)} %get-tuple-element.166), channel_id=1, source_target_pairs={{0,16},{1,17},{2,18},{3,19},{4,20},{5,21},{6,22},{7,23},{8,24},{9,... | collective-permute-start | bytes 442376 | tf_op jit(solution)/shard_map/ppermute | solution.py:51
  402.8 11.9 %collective-permute-start.69 = (bf16[1,96,768]{2,1,0:T(8,128)(2,1)S(1)}, bf16[1,96,768]{2,1,0:T(8,128)(2,1)S(1)}, u32[]{:S(2)}, u32[]{:S(2)}) collective-permute-start(bf16[1,96,768]{2,1,0:T(8,128)(2,1)S(1)} %get-tuple-element.164), channel_id=1, source_target_pairs={{0,8},{1,9},{2,10},{3,11},{4,12},{5,13},{6,14},{7,15},{8,16},{9,17... | collective-permute-start | bytes 442376 | tf_op jit(solution)/shard_map/ppermute | solution.py:51
  404.6 17.8 %collective-permute-start.39 = (bf16[16,24,768]{2,1,0:T(8,128)(2,1)S(1)}, bf16[16,24,768]{2,1,0:T(8,128)(2,1)S(1)}, u32[]{:S(2)}, u32[]{:S(2)}) collective-permute-start(bf16[16,24,768]{2,1,0:T(8,128)(2,1)S(1)} %copy-done.13), channel_id=1, source_target_pairs={{0,1},{1,0},{2,3},{3,2},{4,5},{5,4},{6,7},{7,6},{8,9},{9,8},{10,11... | collective-permute-start | bytes 1769480 | tf_op jit(solution)/shard_map/ppermute | solution.py:51
  412.9 8.1 %collective-permute-start.42 = (bf16[8,24,768]{2,1,0:T(8,128)(2,1)S(1)}, bf16[8,24,768]{2,1,0:T(8,128)(2,1)S(1)}, u32[]{:S(2)}, u32[]{:S(2)}) collective-permute-start(bf16[8,24,768]{2,1,0:T(8,128)(2,1)S(1)} %dynamic-slice_bitcast_fusion.12), channel_id=1, source_target_pairs={{0,2},{1,3},{2,0},{3,1},{4,6},{5,7},{6,4},{7,5},{8,10},{9,11},{10,... | collective-permute-start | bytes 884744 | tf_op jit(solution)/shard_map/ppermute | solution.py:51
  422.6 11.8 %collective-permute-start.43 = (bf16[4,48,768]{2,1,0:T(8,128)(2,1)S(1)}, bf16[4,48,768]{2,1,0:T(8,128)(2,1)S(1)}, u32[]{:S(2)}, u32[]{:S(2)}) collective-permute-start(bf16[4,48,768]{2,1,0:T(8,128)(2,1)S(1)} %dynamic-slice_bitcast_fusion.11), channel_id=1, source_target_pairs={{0,4},{1,5},{2,6},{3,7},{4,0},{5,1},{6,2},{7,3},{8,12},{9,13},{10,... | collective-permute-start | bytes 884744 | tf_op jit(solution)/shard_map/ppermute | solution.py:51
  424.0 10.5 %collective-permute-start.44 = (bf16[8,24,768]{2,1,0:T(8,128)(2,1)S(1)}, bf16[8,24,768]{2,1,0:T(8,128)(2,1)S(1)}, u32[]{:S(2)}, u32[]{:S(2)}) collective-permute-start(bf16[8,24,768]{2,1,0:T(8,128)(2,1)S(1)} %dynamic-slice_bitcast_fusion.10), channel_id=1, source_target_pairs={{0,2},{1,3},{2,0},{3,1},{4,6},{5,7},{6,4},{7,5},{8,10},{9,11},{10,... | collective-permute-start | bytes 884744 | tf_op jit(solution)/shard_map/ppermute | solution.py:51
  425.9 6.7 %collective-permute-start.45 = (f32[8,1,288]{2,0,1:T(8,128)S(1)}, f32[8,1,288]{2,0,1:T(8,128)S(1)}, u32[]{:S(2)}, u32[]{:S(2)}) collective-permute-start(f32[8,1,288]{2,0,1:T(8,128)S(1)} %bitcast.417), channel_id=1, source_target_pairs={{0,2},{1,3},{2,0},{3,1},{4,6},{5,7},{6,4},{7,5},{8,10},{9,11},{10,... | collective-permute-start | bytes 27656 | tf_op jit(solution)/shard_map/ppermute | solution.py:51
  426.2 8.1 %collective-permute-start.46 = (bf16[4,24,768]{2,1,0:T(8,128)(2,1)S(1)}, bf16[4,24,768]{2,1,0:T(8,128)(2,1)S(1)}, u32[]{:S(2)}, u32[]{:S(2)}) collective-permute-start(bf16[4,24,768]{2,1,0:T(8,128)(2,1)S(1)} %dynamic-slice_bitcast_fusion.17), channel_id=1, source_target_pairs={{0,2},{1,3},{2,0},{3,1},{4,6},{5,7},{6,4},{7,5},{8,10},{9,11},{10,... | collective-permute-start | bytes 442376 | tf_op jit(solution)/shard_map/ppermute | solution.py:51
  428.0 6.3 %collective-permute-start.47 = (bf16[4,24,768]{2,1,0:T(8,128)(2,1)S(1)}, bf16[4,24,768]{2,1,0:T(8,128)(2,1)S(1)}, u32[]{:S(2)}, u32[]{:S(2)}) collective-permute-start(bf16[4,24,768]{2,1,0:T(8,128)(2,1)S(1)} %dynamic-slice_bitcast_fusion.16), channel_id=1, source_target_pairs={{0,4},{1,5},{2,6},{3,7},{4,0},{5,1},{6,2},{7,3},{8,12},{9,13},{10,... | collective-permute-start | bytes 442376 | tf_op jit(solution)/shard_map/ppermute | solution.py:51
  434.6 19.7 %collective-permute-start.48 = (bf16[4,24,768]{2,1,0:T(8,128)(2,1)S(1)}, bf16[4,24,768]{2,1,0:T(8,128)(2,1)S(1)}, u32[]{:S(2)}, u32[]{:S(2)}) collective-permute-start(bf16[4,24,768]{2,1,0:T(8,128)(2,1)S(1)} %dynamic-slice_bitcast_fusion.15), channel_id=1, source_target_pairs={{0,2},{1,3},{2,0},{3,1},{4,6},{5,7},{6,4},{7,5},{8,10},{9,11},{10,... | collective-permute-start | bytes 442376 | tf_op jit(solution)/shard_map/ppermute | solution.py:51
  436.4 17.9 %collective-permute-start.49 = (bf16[4,24,768]{2,1,0:T(8,128)(2,1)S(1)}, bf16[4,24,768]{2,1,0:T(8,128)(2,1)S(1)}, u32[]{:S(2)}, u32[]{:S(2)}) collective-permute-start(bf16[4,24,768]{2,1,0:T(8,128)(2,1)S(1)} %dynamic-slice_bitcast_fusion.14), channel_id=1, source_target_pairs={{0,4},{1,5},{2,6},{3,7},{4,0},{5,1},{6,2},{7,3},{8,12},{9,13},{10,... | collective-permute-start | bytes 442376 | tf_op jit(solution)/shard_map/ppermute | solution.py:51
  438.7 7.2 %collective-permute-start.55 = (bf16[1,24,768]{2,1,0:T(8,128)(2,1)S(1)}, bf16[1,24,768]{2,1,0:T(8,128)(2,1)S(1)}, u32[]{:S(2)}, u32[]{:S(2)}) collective-permute-start(bf16[1,24,768]{2,1,0:T(8,128)(2,1)S(1)} %get-tuple-element.201), channel_id=1, source_target_pairs={{0,16},{1,17},{2,18},{3,19},{4,20},{5,21},{6,22},{7,23},{8,24},{9,... | collective-permute-start | bytes 110600 | tf_op jit(solution)/shard_map/ppermute | solution.py:51
  442.0 5.9 %collective-permute-start.54 = (bf16[1,24,768]{2,1,0:T(8,128)(2,1)S(1)}, bf16[1,24,768]{2,1,0:T(8,128)(2,1)S(1)}, u32[]{:S(2)}, u32[]{:S(2)}) collective-permute-start(bf16[1,24,768]{2,1,0:T(8,128)(2,1)S(1)} %get-tuple-element.199), channel_id=1, source_target_pairs={{0,8},{1,9},{2,10},{3,11},{4,12},{5,13},{6,14},{7,15},{8,16},{9,17... | collective-permute-start | bytes 110600 | tf_op jit(solution)/shard_map/ppermute | solution.py:51
  447.9 5.8 %collective-permute-start.63 = (bf16[1,24,768]{2,1,0:T(8,128)(2,1)S(1)}, bf16[1,24,768]{2,1,0:T(8,128)(2,1)S(1)}, u32[]{:S(2)}, u32[]{:S(2)}) collective-permute-start(bf16[1,24,768]{2,1,0:T(8,128)(2,1)S(1)} %get-tuple-element.196), channel_id=1, source_target_pairs={{0,8},{1,9},{2,10},{3,11},{4,12},{5,13},{6,14},{7,15},{8,16},{9,17... | collective-permute-start | bytes 110600 | tf_op jit(solution)/shard_map/ppermute | solution.py:51
  454.5 5.2 %collective-permute-start.53 = (f32[1,1,288]{2,1,0:T(1,128)S(1)}, f32[1,1,288]{2,1,0:T(1,128)S(1)}, u32[]{:S(2)}, u32[]{:S(2)}) collective-permute-start(f32[1,1,288]{2,1,0:T(1,128)S(1)} %get-tuple-element.213), channel_id=1, source_target_pairs={{0,24},{1,25},{2,26},{3,27},{4,28},{5,29},{6,30},{7,31},{8,0},{9,1... | collective-permute-start | bytes 3464 | tf_op jit(solution)/shard_map/ppermute | solution.py:51
  454.5 7.1 %collective-permute-start.52 = (f32[1,1,288]{2,1,0:T(1,128)S(1)}, f32[1,1,288]{2,1,0:T(1,128)S(1)}, u32[]{:S(2)}, u32[]{:S(2)}) collective-permute-start(f32[1,1,288]{2,1,0:T(1,128)S(1)} %get-tuple-element.214), channel_id=1, source_target_pairs={{0,16},{1,17},{2,18},{3,19},{4,20},{5,21},{6,22},{7,23},{8,24},{9,... | collective-permute-start | bytes 3464 | tf_op jit(solution)/shard_map/ppermute | solution.py:51
  454.6 8.9 %collective-permute-start.51 = (f32[1,1,288]{2,1,0:T(1,128)S(1)}, f32[1,1,288]{2,1,0:T(1,128)S(1)}, u32[]{:S(2)}, u32[]{:S(2)}) collective-permute-start(f32[1,1,288]{2,1,0:T(1,128)S(1)} %get-tuple-element.212), channel_id=1, source_target_pairs={{0,8},{1,9},{2,10},{3,11},{4,12},{5,13},{6,14},{7,15},{8,16},{9,17... | collective-permute-start | bytes 3464 | tf_op jit(solution)/shard_map/ppermute | solution.py:51
  456.6 9.2 %collective-permute-start.62 = (bf16[1,24,768]{2,1,0:T(8,128)(2,1)S(1)}, bf16[1,24,768]{2,1,0:T(8,128)(2,1)S(1)}, u32[]{:S(2)}, u32[]{:S(2)}) collective-permute-start(bf16[1,24,768]{2,1,0:T(8,128)(2,1)S(1)} %get-tuple-element.206), channel_id=1, source_target_pairs={{0,24},{1,25},{2,26},{3,27},{4,28},{5,29},{6,30},{7,31},{8,0},{9,1... | collective-permute-start | bytes 110600 | tf_op jit(solution)/shard_map/ppermute | solution.py:51
  459.0 7.0 %collective-permute-start.61 = (bf16[1,24,768]{2,1,0:T(8,128)(2,1)S(1)}, bf16[1,24,768]{2,1,0:T(8,128)(2,1)S(1)}, u32[]{:S(2)}, u32[]{:S(2)}) collective-permute-start(bf16[1,24,768]{2,1,0:T(8,128)(2,1)S(1)} %get-tuple-element.207), channel_id=1, source_target_pairs={{0,16},{1,17},{2,18},{3,19},{4,20},{5,21},{6,22},{7,23},{8,24},{9,... | collective-permute-start | bytes 110600 | tf_op jit(solution)/shard_map/ppermute | solution.py:51
  459.6 6.3 %collective-permute-start.60 = (bf16[1,24,768]{2,1,0:T(8,128)(2,1)S(1)}, bf16[1,24,768]{2,1,0:T(8,128)(2,1)S(1)}, u32[]{:S(2)}, u32[]{:S(2)}) collective-permute-start(bf16[1,24,768]{2,1,0:T(8,128)(2,1)S(1)} %get-tuple-element.205), channel_id=1, source_target_pairs={{0,8},{1,9},{2,10},{3,11},{4,12},{5,13},{6,14},{7,15},{8,16},{9,17... | collective-permute-start | bytes 110600 | tf_op jit(solution)/shard_map/ppermute | solution.py:51
  465.8 5.8 %collective-permute-start.57 = (bf16[1,24,768]{2,1,0:T(8,128)(2,1)S(1)}, bf16[1,24,768]{2,1,0:T(8,128)(2,1)S(1)}, u32[]{:S(2)}, u32[]{:S(2)}) collective-permute-start(bf16[1,24,768]{2,1,0:T(8,128)(2,1)S(1)} %get-tuple-element.202), channel_id=1, source_target_pairs={{0,8},{1,9},{2,10},{3,11},{4,12},{5,13},{6,14},{7,15},{8,16},{9,17... | collective-permute-start | bytes 110600 | tf_op jit(solution)/shard_map/ppermute | solution.py:51
  (38 other events, 364.1 us)
